TPU v7x, 32 devices: a whole 2x2x4 slice. The times are simulated.
32 devices in a mesh: fsdp: 4 (over z), context: 2 (over y), tensor: 4 (over x, core).
Axes of the slice: x: 2, y: 2, z: 4, core: 2. Of those that a mesh axis runs over, the one named last changes fastest.
Arguments:
- hidden_in: bfloat16 [4, 1024, 2048], P('fsdp', 'context'), may hold values from -6 to 6
- attn_gain: bfloat16 [2048], P(('fsdp', 'context')), may hold values from 0.5 to 1.5
- w_query: bfloat16 [2048, 4096], P(('fsdp', 'context'), 'tensor'), may hold values from -0.125 to 0.125
- key_weight: bfloat16 [2048, 512], P(('fsdp', 'context'), 'tensor'), may hold values from -0.125 to 0.125
- value_weight: bfloat16 [2048, 512], P(('fsdp', 'context'), 'tensor'), may hold values from -0.125 to 0.125
- w_output: bfloat16 [2048, 4096], P(('fsdp', 'context'), 'tensor'), may hold values from -0.5 to 0.5
- query_gain: bfloat16 [128], P(('fsdp', 'context')), may hold values from 0.796875 to 2
- key_gain: bfloat16 [128], P(('fsdp', 'context')), may hold values from 0.796875 to 2
- ffn_gain: bfloat16 [2048], P(('fsdp', 'context')), may hold values from 0.5 to 1.5
- router: bfloat16 [2048, 32], P(('fsdp', 'context')), may hold values from -0.0625 to 0.0625
- gate_weight: bfloat16 [32, 2048, 768], P(('fsdp', 'context'), None, 'tensor'), may hold values from -0.125 to 0.125
- up_weight: bfloat16 [32, 2048, 768], P(('fsdp', 'context'), None, 'tensor'), may hold values from -0.125 to 0.125
- down_weight: bfloat16 [32, 768, 2048], P(('fsdp', 'context'), 'tensor'), may hold values from -1.25 to 1.25
- routes: int32 [4, 1024, 8], P('fsdp', 'context'), may hold values from 0 to 31, all different within a row
- segments: int32 [4, 1024], P('fsdp', 'context'), may hold values from 0 to 3, never falling along the last dimension, each value on 1 to 512 neighbouring positions
- cotangent: bfloat16 [4, 1024, 2048], P('fsdp', 'context'), may hold values from -6 to 6
Outputs:
- output: bfloat16 [4, 1024, 2048], P('fsdp', 'context')
- input_grad: float32 [4, 1024, 2048], P('fsdp', 'context')
- grad_attn_gain: float32 [2048], P(('fsdp', 'context'))
- grad_w_query: float32 [2048, 4096], P(('fsdp', 'context'), 'tensor')
- grad_w_key: float32 [2048, 512], P(('fsdp', 'context'), 'tensor')
- grad_w_value: float32 [2048, 512], P(('fsdp', 'context'), 'tensor')
- grad_w_output: float32 [2048, 4096], P(('fsdp', 'context'), 'tensor')
- grad_query_gain: float32 [128], P(('fsdp', 'context'))
- grad_key_gain: float32 [128], P(('fsdp', 'context'))
- grad_ffn_gain: float32 [2048], P(('fsdp', 'context'))
- grad_router: float32 [2048, 32], P(('fsdp', 'context'))
- grad_w_gate: float32 [32, 2048, 768], P(('fsdp', 'context'), None, 'tensor')
- grad_w_up: float32 [32, 2048, 768], P(('fsdp', 'context'), None, 'tensor')
- grad_w_down: float32 [32, 768, 2048], P(('fsdp', 'context'), 'tensor')
Inputs may be any that keep to these rules, and one draw needn't show every extreme that they name: `routes`: the 8 experts of a token are different. `segments`: segment numbers never fall along a sequence.
All inputs are finite; a program needn't handle non-finite values.
Results may differ from a plain program's by a relative error of at most 0.03.
Values may be sent and summed in bfloat16 or wider, within the bound.
A program may use at most 320 MiB of HBM per device.

v0:
```python
import math

import jax
import jax.numpy as jnp
from jax import lax
from jax.sharding import PartitionSpec as P

HEAD_SIZE = 128
TOPK = 8


EPSILON = 1e-06
ROPE_BASE = 1000000.0
NEGATIVE = -1e30


def rms_scale(values, gain_vec):
    return (
        values * lax.rsqrt(jnp.mean(values * values, axis=-1, keepdims=True) + EPSILON) * gain_vec
    )


def rotate(values):
    half_width = values.shape[-1] // 2
    return jnp.concatenate([-values[..., half_width:], values[..., :half_width]], axis=-1)


def rope_tables(positions, head_width):
    step_index = jnp.arange(head_width // 2, dtype=jnp.float32)
    inverse = jnp.exp(step_index * (-2.0 * math.log(ROPE_BASE) / head_width))
    angles = positions.astype(jnp.float32)[:, None] * inverse[None, :]
    cosine_table = jnp.cos(angles)
    sine_table = jnp.sin(angles)
    return (
        jnp.concatenate([cosine_table, cosine_table], -1),
        jnp.concatenate([sine_table, sine_table], -1),
    )


def doc_positions(segment):
    length = segment.shape[0]
    token_index = jnp.arange(length, dtype=jnp.int32)
    starts = jnp.concatenate([jnp.ones((1,), bool), segment[1:] != segment[:-1]])
    first_index = lax.cummax(jnp.where(starts, token_index, 0), axis=0)
    return token_index - first_index


def qk_finish(raw_values, gain_vec, cosine_table, sine_table):
    normed = rms_scale(raw_values, gain_vec)
    return normed * cosine_table + rotate(normed) * sine_table


def matmul(left_side, right_side):
    return jnp.dot(left_side, right_side, preferred_element_type=jnp.float32)


def matmul_nt(left_side, right_side):
    return lax.dot_general(
        left_side, right_side, (((1,), (1,)), ((), ())), preferred_element_type=jnp.float32
    )


def matmul_tn(left_side, right_side):
    return lax.dot_general(
        left_side, right_side, (((0,), (0,)), ((), ())), preferred_element_type=jnp.float32
    )


def block_scores(query_vectors, keys_all, seg_all, query_seg, query_index, block_id, key_block):
    leading_row = block_id * key_block
    keys_part = lax.dynamic_slice_in_dim(keys_all, leading_row, key_block, 0)
    seg_part = lax.dynamic_slice_in_dim(seg_all, leading_row, key_block, 0)
    key_index = leading_row + jnp.arange(key_block, dtype=jnp.int32)
    score_scale = query_vectors.shape[2] ** (-0.5)
    scores = (
        jnp.einsum("qhd,kd->hqk", query_vectors, keys_part, preferred_element_type=jnp.float32)
        * score_scale
    )
    allowed = (query_seg[:, None] == seg_part[None, :]) & (
        key_index[None, :] <= query_index[:, None]
    )
    return (scores, allowed[None, :, :], keys_part)


def attention_forward(
    query_vectors, keys_all, values_all, seg_all, query_seg, query_index, key_block
):
    row_count, head_count, head_width = query_vectors.shape
    block_count = keys_all.shape[0] // key_block

    def stats_step(running, block_id):
        run_max, run_sum = running
        scores, allowed, unused = block_scores(
            query_vectors, keys_all, seg_all, query_seg, query_index, block_id, key_block
        )
        masked = jnp.where(allowed, scores, NEGATIVE)
        new_max = jnp.maximum(run_max, jnp.max(masked, axis=2))
        weights = jnp.where(allowed, jnp.exp(masked - new_max[:, :, None]), 0.0)
        run_sum = run_sum * jnp.exp(run_max - new_max) + jnp.sum(weights, axis=2)
        return ((new_max, run_sum), None)

    start_state = (
        jnp.full((head_count, row_count), NEGATIVE, jnp.float32),
        jnp.zeros((head_count, row_count), jnp.float32),
    )
    (run_max, run_sum), ignored = lax.scan(
        stats_step, start_state, jnp.arange(block_count, dtype=jnp.int32)
    )
    log_total = run_max + jnp.log(run_sum)

    def value_step(accumulated, block_id):
        scores, allowed, unused = block_scores(
            query_vectors, keys_all, seg_all, query_seg, query_index, block_id, key_block
        )
        prob_block = jnp.where(allowed, jnp.exp(scores - log_total[:, :, None]), 0.0).astype(
            jnp.bfloat16
        )
        values_part = lax.dynamic_slice_in_dim(values_all, block_id * key_block, key_block, 0)
        accumulated = accumulated + jnp.einsum(
            "hqk,kd->qhd", prob_block, values_part, preferred_element_type=jnp.float32
        )
        return (accumulated, None)

    heads_full, ignored = lax.scan(
        value_step,
        jnp.zeros((row_count, head_count, head_width), jnp.float32),
        jnp.arange(block_count, dtype=jnp.int32),
    )
    return (heads_full, log_total)


def attention_backward(
    query_vectors,
    keys_all,
    values_all,
    seg_all,
    query_seg,
    query_index,
    key_block,
    log_total,
    grad_heads,
    row_delta,
):
    row_count, head_count, head_width = query_vectors.shape
    block_count = keys_all.shape[0] // key_block
    score_scale = head_width ** (-0.5)

    def grad_step(grad_query, block_id):
        scores, allowed, keys_part = block_scores(
            query_vectors, keys_all, seg_all, query_seg, query_index, block_id, key_block
        )
        values_part = lax.dynamic_slice_in_dim(values_all, block_id * key_block, key_block, 0)
        prob_block = jnp.where(allowed, jnp.exp(scores - log_total[:, :, None]), 0.0)
        grad_prob = jnp.einsum(
            "qhd,kd->hqk", grad_heads, values_part, preferred_element_type=jnp.float32
        )
        grad_score = (prob_block * (grad_prob - row_delta[:, :, None])).astype(jnp.bfloat16)
        grad_query = (
            grad_query
            + jnp.einsum("hqk,kd->qhd", grad_score, keys_part, preferred_element_type=jnp.float32)
            * score_scale
        )
        grad_key = (
            jnp.einsum("hqk,qhd->kd", grad_score, query_vectors, preferred_element_type=jnp.float32)
            * score_scale
        )
        grad_value = jnp.einsum(
            "hqk,qhd->kd",
            prob_block.astype(jnp.bfloat16),
            grad_heads,
            preferred_element_type=jnp.float32,
        )
        return (grad_query, (grad_key, grad_value))

    grad_query, (grad_key, grad_value) = lax.scan(
        grad_step,
        jnp.zeros((row_count, head_count, head_width), jnp.float32),
        jnp.arange(block_count, dtype=jnp.int32),
    )
    return (grad_query, grad_key.reshape(-1, head_width), grad_value.reshape(-1, head_width))


def to_experts(buffer):
    return lax.all_to_all(buffer, ("fsdp", "context"), split_axis=0, concat_axis=1, tiled=True)


def from_experts(result_rows):
    return lax.all_to_all(result_rows, ("fsdp", "context"), split_axis=1, concat_axis=0, tiled=True)


def pick_pairs(buffer, target, row_count):
    model_width = buffer.shape[2]
    flat_rows = jnp.concatenate(
        [buffer.reshape(-1, model_width), jnp.zeros((1, model_width), buffer.dtype)], axis=0
    )
    return flat_rows[target].reshape(row_count, TOPK, model_width)


def local(
    hidden_in,
    attn_gain,
    w_query,
    key_weight,
    value_weight,
    w_output,
    query_gain,
    key_gain,
    ffn_gain,
    router,
    gate_weight,
    up_weight,
    down_weight,
    routes,
    segments,
    cotangent,
):
    context_rank = lax.axis_index("context")
    input_rows = hidden_in[0].astype(jnp.float32)
    row_count, model_width = input_rows.shape
    gathered = (
        lax.all_gather(w_query, ("fsdp", "context"), axis=0, tiled=True),
        lax.all_gather(key_weight, ("fsdp", "context"), axis=0, tiled=True),
        lax.all_gather(value_weight, ("fsdp", "context"), axis=0, tiled=True),
        lax.all_gather(w_output, ("fsdp", "context"), axis=0, tiled=True),
        lax.all_gather(router, ("fsdp", "context"), axis=0, tiled=True),
        lax.all_gather(attn_gain, ("fsdp", "context"), axis=0, tiled=True),
        lax.all_gather(ffn_gain, ("fsdp", "context"), axis=0, tiled=True),
        lax.all_gather(query_gain, ("fsdp", "context"), axis=0, tiled=True),
        lax.all_gather(key_gain, ("fsdp", "context"), axis=0, tiled=True),
    )
    full_query, full_key, full_value, full_output, full_router = (
        gathered[0],
        gathered[1],
        gathered[2],
        gathered[3],
        gathered[4],
    )
    gain_attn = gathered[5].astype(jnp.float32)
    gain_ffn = gathered[6].astype(jnp.float32)
    gain_query = gathered[7].astype(jnp.float32)
    gain_key = gathered[8].astype(jnp.float32)
    local_heads = full_query.shape[1] // HEAD_SIZE
    seg_all = lax.all_gather(segments, "context", axis=1, tiled=True)[0]
    length = seg_all.shape[0]
    start_row = context_rank * row_count
    positions = lax.dynamic_slice_in_dim(doc_positions(seg_all), start_row, row_count)
    cosine_table, sine_table = rope_tables(positions, HEAD_SIZE)
    query_seg = segments[0]
    query_index = start_row + jnp.arange(row_count, dtype=jnp.int32)
    key_block = min(512, length)

    def query_finish(raw_values, gain_vec):
        return qk_finish(raw_values, gain_vec, cosine_table[:, None, :], sine_table[:, None, :])

    def key_finish(raw_values, gain_vec):
        return qk_finish(raw_values, gain_vec, cosine_table, sine_table)

    normed_f, first_pull = jax.vjp(rms_scale, input_rows, gain_attn)
    attention_normalized = normed_f.astype(jnp.bfloat16)
    query_unrotated = matmul(attention_normalized, full_query).reshape(
        row_count, local_heads, HEAD_SIZE
    )
    key_unrotated = matmul(attention_normalized, full_key)
    value_raw = matmul(attention_normalized, full_value)
    query_f, query_pull = jax.vjp(query_finish, query_unrotated, gain_query)
    key_f, key_pull = jax.vjp(key_finish, key_unrotated, gain_key)
    query_vectors = query_f.astype(jnp.bfloat16)
    keys_all, values_all = (
        lax.all_gather(key_f.astype(jnp.bfloat16), "context", axis=0, tiled=True),
        lax.all_gather(value_raw.astype(jnp.bfloat16), "context", axis=0, tiled=True),
    )
    heads_full, log_total = attention_forward(
        query_vectors, keys_all, values_all, seg_all, query_seg, query_index, key_block
    )
    heads_low = heads_full.reshape(row_count, local_heads * HEAD_SIZE).astype(jnp.bfloat16)
    attn_out = lax.psum(matmul_nt(heads_low, full_output).astype(jnp.bfloat16), "tensor").astype(
        jnp.float32
    )
    residual_stream = input_rows + attn_out
    second_f, second_pull = jax.vjp(rms_scale, residual_stream, gain_ffn)
    feedforward_normalized = second_f.astype(jnp.bfloat16)
    router_scores = matmul(feedforward_normalized, full_router)
    experts_total = full_router.shape[1]
    route_ids = routes[0]
    chosen = route_ids[:, :, None] == jnp.arange(experts_total, dtype=jnp.int32)
    selected = jnp.sum(jnp.where(chosen, router_scores[:, None, :], 0.0), axis=2)
    gate_probs = jax.nn.softmax(selected, axis=-1)
    capacity = 9 * row_count * TOPK // (8 * experts_total)
    counts = jnp.sum(chosen.astype(jnp.int32), axis=1)
    before = jnp.cumsum(counts, axis=0) - counts
    slot_index = jnp.sum(jnp.where(chosen, before[:, None, :], 0), axis=2)
    target = jnp.where(
        slot_index < capacity, route_ids * capacity + slot_index, experts_total * capacity
    ).reshape(-1)
    source = jnp.repeat(jnp.arange(row_count, dtype=jnp.int32), TOPK)
    send_rows = (
        jnp.zeros((experts_total * capacity, model_width), jnp.bfloat16)
        .at[target]
        .set(feedforward_normalized[source], mode="drop")
    )
    expert_input_rows = to_experts(send_rows.reshape(experts_total, capacity, model_width))
    gate_activation_input = jnp.einsum(
        "phu,puo->pho", expert_input_rows, gate_weight, preferred_element_type=jnp.float32
    )
    up_activation_input = jnp.einsum(
        "phu,puo->pho", expert_input_rows, up_weight, preferred_element_type=jnp.float32
    )
    sigmoid_gate = jax.nn.sigmoid(gate_activation_input)
    silu_gate = gate_activation_input * sigmoid_gate
    hidden_middle = (silu_gate * up_activation_input).astype(jnp.bfloat16)
    expert_part = jnp.einsum(
        "pic,pcw->piw", hidden_middle, down_weight, preferred_element_type=jnp.float32
    ).astype(jnp.bfloat16)
    grad_out = cotangent[0].astype(jnp.float32)
    returned = pick_pairs(from_experts(expert_part), target, row_count)
    moe_part = jnp.sum(returned.astype(jnp.float32) * gate_probs[:, :, None], axis=1)
    moe_out = lax.psum(moe_part.astype(jnp.bfloat16), "tensor").astype(jnp.float32)
    grad_gate_part = jnp.sum(returned.astype(jnp.float32) * grad_out[:, None, :], axis=2)
    output = (residual_stream + moe_out).astype(jnp.bfloat16)
    pair_grad = (
        (gate_probs[:, :, None] * grad_out[:, None, :])
        .astype(jnp.bfloat16)
        .reshape(row_count * TOPK, model_width)
    )
    send_grad = (
        jnp.zeros((experts_total * capacity, model_width), jnp.bfloat16)
        .at[target]
        .set(pair_grad, mode="drop")
    )
    expert_output_gradient = to_experts(send_grad.reshape(experts_total, capacity, model_width))
    grad_mid = jnp.einsum(
        "jtk,jvk->jtv", expert_output_gradient, down_weight, preferred_element_type=jnp.float32
    )
    grad_w_down = jnp.einsum(
        "tce,tci->tei", hidden_middle, expert_output_gradient, preferred_element_type=jnp.float32
    )
    gate_activation_gradient = (
        grad_mid
        * up_activation_input
        * sigmoid_gate
        * (1.0 + gate_activation_input * (1.0 - sigmoid_gate))
    ).astype(jnp.bfloat16)
    up_activation_gradient = (grad_mid * silu_gate).astype(jnp.bfloat16)
    grad_w_gate = jnp.einsum(
        "ahw,ahp->awp",
        expert_input_rows,
        gate_activation_gradient,
        preferred_element_type=jnp.float32,
    )
    grad_w_up = jnp.einsum(
        "ahw,ahp->awp",
        expert_input_rows,
        up_activation_gradient,
        preferred_element_type=jnp.float32,
    )
    grad_expert_in = (
        jnp.einsum(
            "ous,ops->oup",
            gate_activation_gradient,
            gate_weight,
            preferred_element_type=jnp.float32,
        )
        + jnp.einsum(
            "ous,ops->oup", up_activation_gradient, up_weight, preferred_element_type=jnp.float32
        )
    ).astype(jnp.bfloat16)
    grad_pairs = pick_pairs(from_experts(grad_expert_in), target, row_count)
    grad_normed_part = jnp.sum(grad_pairs.astype(jnp.float32), axis=1)
    grad_normed_moe, grad_gates = (
        lax.psum(grad_normed_part.astype(jnp.bfloat16), "tensor").astype(jnp.float32),
        lax.psum(grad_gate_part.astype(jnp.bfloat16), "tensor").astype(jnp.float32),
    )
    grad_selected = gate_probs * (
        grad_gates - jnp.sum(gate_probs * grad_gates, axis=1, keepdims=True)
    )
    grad_logits = jnp.sum(jnp.where(chosen, grad_selected[:, :, None], 0.0), axis=1).astype(
        jnp.bfloat16
    )
    grad_router = matmul_tn(feedforward_normalized, grad_logits)
    grad_normed_two = grad_normed_moe + matmul_nt(grad_logits, full_router)
    grad_resid_norm, grad_gain_ffn = second_pull(grad_normed_two)
    grad_resid = grad_out + grad_resid_norm
    grad_attn = grad_resid.astype(jnp.bfloat16)
    grad_w_output = matmul_tn(grad_attn, heads_low)
    grad_heads = (
        matmul(grad_attn, full_output)
        .astype(jnp.bfloat16)
        .reshape(row_count, local_heads, HEAD_SIZE)
    )
    row_delta = jnp.sum(grad_heads.astype(jnp.float32) * heads_full, axis=2).T
    grad_query, grad_key_terms, grad_value_terms = attention_backward(
        query_vectors,
        keys_all,
        values_all,
        seg_all,
        query_seg,
        query_index,
        key_block,
        log_total,
        grad_heads,
        row_delta,
    )
    grad_key_local, grad_value_local = (
        lax.psum_scatter(
            grad_key_terms.astype(jnp.bfloat16), "context", scatter_dimension=0, tiled=True
        ).astype(jnp.float32),
        lax.psum_scatter(
            grad_value_terms.astype(jnp.bfloat16), "context", scatter_dimension=0, tiled=True
        ).astype(jnp.float32),
    )
    grad_query_raw, grad_gain_query = query_pull(grad_query)
    grad_key_raw, grad_gain_key = key_pull(grad_key_local)
    grad_query_low = grad_query_raw.reshape(row_count, local_heads * HEAD_SIZE).astype(jnp.bfloat16)
    grad_key_low = grad_key_raw.astype(jnp.bfloat16)
    grad_value_low = grad_value_local.astype(jnp.bfloat16)
    grad_w_query = matmul_tn(attention_normalized, grad_query_low)
    grad_w_key = matmul_tn(attention_normalized, grad_key_low)
    grad_w_value = matmul_tn(attention_normalized, grad_value_low)
    grad_normed_one = (
        matmul_nt(grad_query_low, full_query)
        + matmul_nt(grad_key_low, full_key)
        + matmul_nt(grad_value_low, full_value)
    )
    grad_normed_one, grad_gain_query, grad_gain_key = (
        lax.psum(grad_normed_one.astype(jnp.bfloat16), "tensor").astype(jnp.float32),
        lax.psum(grad_gain_query.astype(jnp.bfloat16), "tensor").astype(jnp.float32),
        lax.psum(grad_gain_key.astype(jnp.bfloat16), "tensor").astype(jnp.float32),
    )
    grad_inputs_norm, grad_gain_attn = first_pull(grad_normed_one)
    input_grad = grad_resid + grad_inputs_norm
    owned = (
        lax.psum_scatter(
            grad_w_query.astype(jnp.bfloat16), ("fsdp", "context"), scatter_dimension=0, tiled=True
        ).astype(jnp.float32),
        lax.psum_scatter(
            grad_w_key.astype(jnp.bfloat16), ("fsdp", "context"), scatter_dimension=0, tiled=True
        ).astype(jnp.float32),
        lax.psum_scatter(
            grad_w_value.astype(jnp.bfloat16), ("fsdp", "context"), scatter_dimension=0, tiled=True
        ).astype(jnp.float32),
        lax.psum_scatter(
            grad_w_output.astype(jnp.bfloat16), ("fsdp", "context"), scatter_dimension=0, tiled=True
        ).astype(jnp.float32),
        lax.psum_scatter(
            grad_router.astype(jnp.bfloat16), ("fsdp", "context"), scatter_dimension=0, tiled=True
        ).astype(jnp.float32),
        lax.psum_scatter(
            grad_gain_attn.astype(jnp.bfloat16),
            ("fsdp", "context"),
            scatter_dimension=0,
            tiled=True,
        ).astype(jnp.float32),
        lax.psum_scatter(
            grad_gain_ffn.astype(jnp.bfloat16), ("fsdp", "context"), scatter_dimension=0, tiled=True
        ).astype(jnp.float32),
        lax.psum_scatter(
            grad_gain_query.astype(jnp.bfloat16),
            ("fsdp", "context"),
            scatter_dimension=0,
            tiled=True,
        ).astype(jnp.float32),
        lax.psum_scatter(
            grad_gain_key.astype(jnp.bfloat16), ("fsdp", "context"), scatter_dimension=0, tiled=True
        ).astype(jnp.float32),
    )
    return (
        output[None],
        input_grad[None],
        owned[5],
        owned[0],
        owned[1],
        owned[2],
        owned[3],
        owned[7],
        owned[8],
        owned[6],
        owned[4],
        grad_w_gate,
        grad_w_up,
        grad_w_down,
    )


def solution(mesh):
    in_specs = (
        P("fsdp", "context", None),
        P(("fsdp", "context")),
        P(("fsdp", "context"), "tensor"),
        P(("fsdp", "context"), "tensor"),
        P(("fsdp", "context"), "tensor"),
        P(("fsdp", "context"), "tensor"),
        P(("fsdp", "context")),
        P(("fsdp", "context")),
        P(("fsdp", "context")),
        P(("fsdp", "context"), None),
        P(("fsdp", "context"), None, "tensor"),
        P(("fsdp", "context"), None, "tensor"),
        P(("fsdp", "context"), "tensor", None),
        P("fsdp", "context", None),
        P("fsdp", "context"),
        P("fsdp", "context", None),
    )
    out_specs = (
        P("fsdp", "context", None),
        P("fsdp", "context", None),
        P(("fsdp", "context")),
        P(("fsdp", "context"), "tensor"),
        P(("fsdp", "context"), "tensor"),
        P(("fsdp", "context"), "tensor"),
        P(("fsdp", "context"), "tensor"),
        P(("fsdp", "context")),
        P(("fsdp", "context")),
        P(("fsdp", "context")),
        P(("fsdp", "context"), None),
        P(("fsdp", "context"), None, "tensor"),
        P(("fsdp", "context"), None, "tensor"),
        P(("fsdp", "context"), "tensor", None),
    )
    return jax.shard_map(local, mesh=mesh, in_specs=in_specs, out_specs=out_specs, check_vma=False)
```

profile of v0, /device:TPU:0, one launch (start us, length us, event | category | flops | bytes accessed | tf_op | source)
XLA Modules:
  0.0 2767.4 jit_solution(2307226080023366675)
XLA Ops:
  12.1 22.5 all-gather
  34.6 33.1 %all_gather.40 = bf16[2048,128]{1,0:T(8,128)(2,1)S(1)} all-gather(bf16[256,128]{1,0:T(8,128)(2,1)} %param.25), channel_id=1, replica_groups=mesh['fsdp'=4,'context'=2,'tensor'=4] {'fsdp','context'}, dimensions={0}, use_global_device_ids=true | all-gather | bytes 589824 | tf_op jit(solution)/shard_map/all_gather | solution.py:222
  114.4 32.7 %all_gather.37 = bf16[2048,128]{1,0:T(8,128)(2,1)S(1)} all-gather(bf16[256,128]{1,0:T(8,128)(2,1)S(1)} %copy-done.62), channel_id=1, replica_groups=mesh['fsdp'=4,'context'=2,'tensor'=4] {'fsdp','context'}, dimensions={0}, use_global_device_ids=true | all-gather | bytes 589824 | tf_op jit(solution)/shard_map/all_gather | solution.py:223
  178.2 24.4 while.39
  248.5 30.6 %all_gather.47 = bf16[2048,32]{0,1:T(8,128)(2,1)S(1)} all-gather(bf16[256,32]{0,1:T(8,128)(2,1)S(1)} %copy-done.80), channel_id=1, replica_groups=mesh['fsdp'=4,'context'=2,'tensor'=4] {'fsdp','context'}, dimensions={0}, use_global_device_ids=true | all-gather | bytes 147456 | tf_op jit(solution)/shard_map/all_gather | solution.py:225
  310.6 39.6 %scatter_custom_fusion.1 = bf16[4608,2048]{1,0:T(8,128)(2,1)} fusion(s32[4096]{0:T(1024)S(1)} %bitcast.382, f32[4096,2048]{1,0:T(8,128)} %mul.470, f32[512,8,2048]{2,1,0:T(8,128)} %mul.471, bf16[]{:T(256)} %constant.84.clone.1), kind=kCustom, calls=%fused_computation.79 | custom fusion | flops 16777216 | bytes 85983232 | tf_op jit(solution)/shard_map/scatter | solution.py:328
  356.4 33.2 %gather_fusion = bf16[4096,2048]{1,0:T(8,128)(2,1)} fusion(bf16[512,2048]{1,0:T(8,128)(2,1)} %copy-done.2, s32[4096]{0:T(1024)S(1)} %broadcast_clamp_fusion.1), kind=kCustom, calls=%fused_computation | custom fusion | bytes 33570816 | tf_op jit(solution)/shard_map/gather | solution.py:299
  389.6 34.8 %scatter_custom_fusion = bf16[4608,2048]{1,0:T(8,128)(2,1)} fusion(s32[4096]{0:T(1024)S(1)} %bitcast.383, bf16[4096,2048]{1,0:T(8,128)(2,1)} %gather_fusion, bf16[]{:T(256)} %constant.84.clone.1), kind=kCustom, calls=%fused_computation.82 | custom fusion | bytes 18874880 | tf_op jit(solution)/shard_map/scatter | solution.py:299
  424.4 336.8 %all-to-all-done.2 = bf16[32,144,2048]{2,1,0:T(8,128)(2,1)} async-done(((bf16[32,144,2048]{2,1,0:T(8,128)(2,1)}), bf16[32,144,2048]{2,1,0:T(8,128)(2,1)}, u32[]{:S(2)}, u32[]{:S(2)}) %all-to-all-start.2) | async-done | bytes 18874400 | tf_op jit(solution)/shard_map/all_to_all | solution.py:184
  784.0 388.8 %all-to-all-done = bf16[32,144,2048]{2,1,0:T(8,128)(2,1)} async-done(((bf16[32,144,2048]{2,1,0:T(8,128)(2,1)}), bf16[32,144,2048]{2,1,0:T(8,128)(2,1)}, u32[]{:S(2)}, u32[]{:S(2)}) %all-to-all-start) | async-done | bytes 18874400 | tf_op jit(solution)/shard_map/all_to_all | solution.py:184
  1244.2 22.8 fusion.64
  1267.0 24.6 copy.141
  1308.2 24.6 copy.136
  1332.9 371.6 %all-to-all-done.3 = bf16[4,1152,2048]{2,0,1:T(4,128)(2,1)} async-done(((bf16[4,1152,2048]{2,0,1:T(4,128)(2,1)}), bf16[4,1152,2048]{2,0,1:T(4,128)(2,1)}, u32[]{:S(2)}, u32[]{:S(2)}) %all-to-all-start.3) | async-done | bytes 18874400 | tf_op jit(solution)/shard_map/all_to_all | solution.py:188
  1735.7 40.1 %gather_fusion.2 = bf16[4096,2048]{1,0:T(8,128)(2,1)} fusion(bf16[4609,2048]{1,0:T(8,128)(2,1)} %concatenate.30, s32[4096]{0:T(1024)S(1)} %broadcast_clamp_fusion), kind=kCustom, calls=%fused_computation.2 | custom fusion | bytes 33570816 | tf_op jit(solution)/shard_map/gather | solution.py:196
  1790.8 326.5 %all-to-all-done.1 = bf16[4,1152,2048]{2,0,1:T(4,128)(2,1)} async-done(((bf16[4,1152,2048]{2,0,1:T(4,128)(2,1)}), bf16[4,1152,2048]{2,0,1:T(4,128)(2,1)}, u32[]{:S(2)}, u32[]{:S(2)}) %all-to-all-start.1) | async-done | bytes 18874400 | tf_op jit(solution)/shard_map/all_to_all | solution.py:188
  2142.4 40.2 %gather_fusion.1 = bf16[4096,2048]{1,0:T(8,128)(2,1)} fusion(bf16[4609,2048]{1,0:T(8,128)(2,1)} %concatenate.29, s32[4096]{0:T(1024)S(1)} %broadcast_clamp_fusion), kind=kCustom, calls=%fused_computation.1 | custom fusion | bytes 33570816 | tf_op jit(solution)/shard_map/gather | solution.py:196
  2222.2 43.1 %while.41 = (s32[]{:T(128)}, f32[512,8,128]{0,2,1:T(8,128)}, bf16[2,512,128]{2,1,0:T(8,128)(2,1)}, bf16[2,512,128]{2,1,0:T(8,128)(2,1)}, s32[2]{0:T(128)S(1)}, /...) while((s32[]{:T(128)}, f32[512,8,128]{0,2,1:T(8,128)}, ...), condition=%wide.region_33.34_spmd.clone, body=%wide.region_32.33_spmd.clone.sunk | while | flops 2707751936 | bytes 126551504 | solution.py:175
  2359.8 63.0 %reduce-scatter.14.cloned.1.call-done = bf16[256,128]{1,0:T(8,128)(2,1)} async-done(((bf16[2048,128]{1,0:T(8,128)(2,1)}), bf16[256,128]{1,0:T(8,128)(2,1)}) %reduce-scatter.14.cloned.1.call-update) | async-done | bytes 65552 | tf_op jit(solution)/shard_map/reduce_scatter | solution.py:435
  2424.3 86.4 %all-reduce.24.cloned.1.call-done = (bf16[512,2048]{1,0:T(8,128)(2,1)}, bf16[512,2048]{1,0:T(8,128)(2,1)}) async-done(((bf16[512,2048]{1,0:T(8,128)(2,1)}, bf16[512,2048]{1,0:T(8,128)(2,1)}), (bf16[512,2048]{1,0:T(8,128)(2,1)}, bf16[512,2048]{1,0:T(8,128)(2,1)})) %all-reduce.24.cloned.1.call-update) | async-done | bytes 4194320 | tf_op jit(solution)/shard_map/psum | solution.py:317
  2514.0 22.0 all-reduce.12
  2536.2 39.7 %reduce-scatter.16.cloned.1.call-done = bf16[256,128]{1,0:T(8,128)(2,1)} async-done(((bf16[2048,128]{1,0:T(8,128)(2,1)}), bf16[256,128]{1,0:T(8,128)(2,1)}) %reduce-scatter.16.cloned.1.call-update) | async-done | bytes 65552 | tf_op jit(solution)/shard_map/reduce_scatter | solution.py:438
  2592.7 74.2 %reduce-scatter.18.cloned.1.call-done = bf16[256,1024]{1,0:T(8,128)(2,1)} async-done(((bf16[2048,1024]{1,0:T(8,128)(2,1)}), bf16[256,1024]{1,0:T(8,128)(2,1)}) %reduce-scatter.18.cloned.1.call-update) | async-done | bytes 524304 | tf_op jit(solution)/shard_map/reduce_scatter | solution.py:441
  2669.0 89.2 %reduce-scatter.12.cloned.1.call-done = bf16[256,1024]{1,0:T(8,128)(2,1)} async-done(((bf16[2048,1024]{1,0:T(8,128)(2,1)}), bf16[256,1024]{1,0:T(8,128)(2,1)}) %reduce-scatter.12.cloned.1.call-update) | async-done | bytes 524304 | tf_op jit(solution)/shard_map/reduce_scatter | solution.py:432
  (446 shorter events, 582.6 us)
Async XLA Ops:
  7.2 1207.0 %copy-start = (bf16[4,192,2048]{2,1,0:T(8,128)(2,1)S(1)}, bf16[4,192,2048]{2,1,0:T(8,128)(2,1)}, u32[]{:S(2)}) copy-start(bf16[4,192,2048]{2,1,0:T(8,128)(2,1)} %param.34) | copy-start | bytes 9437188
  7.2 153.8 %all-gather.5.cloned.1.call-start = ((), (), s32[]{:S(2)}) async-start(), calls=%async_computation.11 | async-start | bytes 4718592 | tf_op jit(solution)/shard_map/all_gather | solution.py:221
  8.0 212.0 %all-gather.7.cloned.1.call-start = ((), (), s32[]{:S(2)}) async-start(), calls=%async_computation.12 | async-start | bytes 4718592 | tf_op jit(solution)/shard_map/all_gather | solution.py:224
  8.7 83.2 %copy-start.45 = (s32[1,512]{1,0:T(1,128)S(1)}, s32[1,512]{1,0:T(1,128)}, u32[]{:S(2)}) copy-start(s32[1,512]{1,0:T(1,128)} %param.36) | copy-start | bytes 6148
  8.7 270.4 %all-reduce.20.cloned.1.call-start = ((), (), s32[]{:S(2)}) async-start(), calls=%async_computation.13 | async-start | bytes 4194304 | tf_op jit(solution)/shard_map/psum | solution.py:276
  11.4 156.1 %copy-start.72 = (f32[512]{0:T(512)}, f32[512]{0:T(512)S(1)}, u32[]{:S(2)}) copy-start(f32[512]{0:T(512)S(1)} %fusion.110) | copy-start | bytes 6148
  34.6 132.9 %copy-start.58 = (f32[8,1,256]{2,1,0:T(1,128)}, f32[8,1,256]{2,1,0:T(1,128)S(1)}, u32[]{:S(2)}) copy-start(f32[8,1,256]{2,1,0:T(1,128)S(1)} %convert_element_type.304) | copy-start | bytes 24580
  350.2 411.0 %all-to-all-start.2 = ((bf16[32,144,2048]{2,1,0:T(8,128)(2,1)}), bf16[32,144,2048]{2,1,0:T(8,128)(2,1)}, u32[]{:S(2)}, u32[]{:S(2)}) async-start(bf16[32,144,2048]{2,1,0:T(8,128)(2,1)} %bitcast.350), calls=%async_computation.2 | async-start | bytes 37748736 | tf_op jit(solution)/shard_map/all_to_all | solution.py:184
  761.2 411.7 %all-to-all-start = ((bf16[32,144,2048]{2,1,0:T(8,128)(2,1)}), bf16[32,144,2048]{2,1,0:T(8,128)(2,1)}, u32[]{:S(2)}, u32[]{:S(2)}) async-start(bf16[32,144,2048]{2,1,0:T(8,128)(2,1)} %bitcast.347), calls=%async_computation | async-start | bytes 37748736 | tf_op jit(solution)/shard_map/all_to_all | solution.py:184
  1291.7 412.8 %all-to-all-start.3 = ((bf16[4,1152,2048]{2,0,1:T(4,128)(2,1)}), bf16[4,1152,2048]{2,0,1:T(4,128)(2,1)}, u32[]{:S(2)}, u32[]{:S(2)}) async-start(bf16[4,1152,2048]{2,0,1:T(4,128)(2,1)} %copy.141), calls=%async_computation.3 | async-start | bytes 37748736 | tf_op jit(solution)/shard_map/all_to_all | solution.py:188
  1332.9 377.7 %copy-start.65 = (s32[4096,1]{0,1:T(1,128)S(1)}, s32[4096,1]{0,1:T(1,128)}, u32[]{:S(2)}) copy-start(s32[4096,1]{0,1:T(1,128)} %get-tuple-element.563) | copy-start | bytes 49156
  1704.5 412.8 %all-to-all-start.1 = ((bf16[4,1152,2048]{2,0,1:T(4,128)(2,1)}), bf16[4,1152,2048]{2,0,1:T(4,128)(2,1)}, u32[]{:S(2)}, u32[]{:S(2)}) async-start(bf16[4,1152,2048]{2,0,1:T(4,128)(2,1)} %copy.136), calls=%async_computation.1 | async-start | bytes 37748736 | tf_op jit(solution)/shard_map/all_to_all | solution.py:188
  1710.5 495.3 %all-reduce.22.cloned.1.call-start = ((), (), s32[]{:S(2)}) async-start(), calls=%async_computation.14 | async-start | bytes 4194304 | tf_op jit(solution)/shard_map/psum | solution.py:370
  1790.8 488.6 %reduce-scatter.8.cloned.1.call-start = ((), (), s32[]{:S(2)}) async-start(), calls=%async_computation.15 | async-start | bytes 393216 | tf_op jit(solution)/shard_map/reduce_scatter | solution.py:404
  2267.1 27.2 reduce-scatter.10.cloned.1.call-start
  2267.7 90.8 %reduce-scatter.20.cloned.1.call-start = ((), (), s32[]{:S(2)}) async-start(), calls=%async_computation.21 | async-start | bytes 147456 | tf_op jit(solution)/shard_map/reduce_scatter | solution.py:444
  2268.9 153.9 %reduce-scatter.14.cloned.1.call-start = ((), (), s32[]{:S(2)}) async-start(), calls=%async_computation.18 | async-start | bytes 589824 | tf_op jit(solution)/shard_map/reduce_scatter | solution.py:435
  2284.4 226.3 %all-reduce.24.cloned.1.call-start = ((), (), s32[]{:S(2)}) async-start(), calls=%async_computation.22 | async-start | bytes 8388608 | tf_op jit(solution)/shard_map/psum | solution.py:317
  2299.9 276.0 %reduce-scatter.16.cloned.1.call-start = ((), (), s32[]{:S(2)}) async-start(), calls=%async_computation.19 | async-start | bytes 589824 | tf_op jit(solution)/shard_map/reduce_scatter | solution.py:438
  2302.6 364.3 %reduce-scatter.18.cloned.1.call-start = ((), (), s32[]{:S(2)}) async-start(), calls=%async_computation.20 | async-start | bytes 4718592 | tf_op jit(solution)/shard_map/reduce_scatter | solution.py:441
  2309.3 448.9 %reduce-scatter.12.cloned.1.call-start = ((), (), s32[]{:S(2)}) async-start(), calls=%async_computation.17 | async-start | bytes 4718592 | tf_op jit(solution)/shard_map/reduce_scatter | solution.py:432
  2352.7 161.3 %copy-start.89 = (bf16[2048]{0:T(1024)(128)(2,1)S(1)}, bf16[2048]{0:T(1024)(128)(2,1)}, u32[]{:S(2)}) copy-start(bf16[2048]{0:T(1024)(128)(2,1)} %get-tuple-element.478) | copy-start | bytes 12292
  2352.7 232.0 %copy-start.75 = (f32[512]{0:T(512)S(1)}, f32[512]{0:T(512)}, u32[]{:S(2)}) copy-start(f32[512]{0:T(512)} %copy-done.74) | copy-start | bytes 6148
  2584.7 175.6 %copy-start.1 = (bf16[4,192,2048]{2,1,0:T(8,128)(2,1)S(1)}, bf16[4,192,2048]{2,1,0:T(8,128)(2,1)}, u32[]{:S(2)}) copy-start(bf16[4,192,2048]{2,1,0:T(8,128)(2,1)} %param.34) | copy-start | bytes 9437188
  (99 other events, 1267.6 us)
Sparse Core Ops, SparseCore 0:
  10.2 81.4 all-gather.4
  93.8 78.9 all-gather.6
  226.3 49.7 all-reduce.19
  1790.9 51.8 all-reduce.21
  2267.2 12.1 reduce-scatter.7
  2281.5 11.6 reduce-scatter.9
  2297.1 61.2 reduce-scatter.19
  2361.8 60.9 reduce-scatter.13
  2425.9 84.6 all-reduce.23
  2513.8 62.0 reduce-scatter.15
  2580.0 86.8 reduce-scatter.17
  2670.4 87.7 reduce-scatter.11
where the time goes:
time: 2770 us
  waiting for transfers between devices  1790 us (65%)
  local copies, waits for them, and re-layouts  346 us (12%)
  matrix products  236 us (9%)
  blocking collectives  211 us (8%)
  other arithmetic  140 us (5%)
    all_to_all x2, waiting for transfers between devices, to_experts(): lax.all_to_all(buffer, ('fsdp', 'context'), split_axis=0, concat_axis=1,...  726 us
    all_to_all x2, waiting for transfers between devices, from_experts(): lax.all_to_all(result_rows, ('fsdp', 'context'), split_axis=1, concat_axi...  698 us
    reduce_scatter x1, waiting for transfers between devices, local(): lax.psum_scatter(grad_w_query.astype(jnp.bfloat16), ('fsdp', 'context'),...  89.2 us
    psum x1, waiting for transfers between devices, local(): lax.psum(moe_part.astype(jnp.bfloat16), 'tensor').astype(jnp.float32)  86.4 us
    gather x2, local copies, waits for them, and re-layouts, pick_pairs(): return flat_rows[target].reshape(row_count, TOPK, model_width)  80.3 us
    reduce_scatter x1, waiting for transfers between devices, local(): lax.psum_scatter(grad_w_output.astype(jnp.bfloat16), ('fsdp', 'context'),...  74.2 us
    reduce_scatter x1, waiting for transfers between devices, local(): lax.psum_scatter(grad_w_key.astype(jnp.bfloat16), ('fsdp', 'context'), sc...  63 us
  transfers between devices with their start and end apart: 16, of which 11 were waited for; matrix products, arithmetic and copies ran while one was open for 17% of the time, Pallas kernels for 0%

commit v1 on v0

--- a/solution.py
+++ b/solution.py
@@ -1,12 +1,18 @@
+import functools
 import math
 
 import jax
 import jax.numpy as jnp
 from jax import lax
+from jax.experimental import pallas as pl
+from jax.experimental.pallas import tpu as pltpu
 from jax.sharding import PartitionSpec as P
 
 HEAD_SIZE = 128
 TOPK = 8
+FSDP, CONTEXT, TENSOR = "fsdp", "context", "tensor"
+GROUPS = (FSDP, CONTEXT)
+EVERYONE = (FSDP, CONTEXT, TENSOR)
 
 
 EPSILON = 1e-06
@@ -38,11 +44,17 @@
 
 
 def doc_positions(segment):
-    length = segment.shape[0]
-    token_index = jnp.arange(length, dtype=jnp.int32)
-    starts = jnp.concatenate([jnp.ones((1,), bool), segment[1:] != segment[:-1]])
-    first_index = lax.cummax(jnp.where(starts, token_index, 0), axis=0)
-    return token_index - first_index
+    token_index = jnp.arange(segment.shape[0], dtype=jnp.int32)
+    smaller = (segment[None, :] < segment[:, None]).astype(jnp.int32)
+    return token_index - jnp.sum(smaller, axis=1)
+
+
+def earlier_counts(chosen):
+    rows = chosen.shape[0]
+    row_id = lax.broadcasted_iota(jnp.int32, (rows, rows), 0)
+    col_id = lax.broadcasted_iota(jnp.int32, (rows, rows), 1)
+    earlier = (col_id < row_id).astype(jnp.bfloat16)
+    return matmul(earlier, chosen.astype(jnp.bfloat16))
 
 
 def qk_finish(raw_values, gain_vec, cosine_table, sine_table):
@@ -66,11 +78,11 @@
     )
 
 
-def block_scores(query_vectors, keys_all, seg_all, query_seg, query_index, block_id, key_block):
+def block_scores(query_vectors, keys_all, seg_all, query_seg, query_index, key_ids, block_id, key_block):
     leading_row = block_id * key_block
     keys_part = lax.dynamic_slice_in_dim(keys_all, leading_row, key_block, 0)
     seg_part = lax.dynamic_slice_in_dim(seg_all, leading_row, key_block, 0)
-    key_index = leading_row + jnp.arange(key_block, dtype=jnp.int32)
+    key_index = lax.dynamic_slice_in_dim(key_ids, leading_row, key_block, 0)
     score_scale = query_vectors.shape[2] ** (-0.5)
     scores = (
         jnp.einsum("qhd,kd->hqk", query_vectors, keys_part, preferred_element_type=jnp.float32)
@@ -83,7 +95,7 @@
 
 
 def attention_forward(
-    query_vectors, keys_all, values_all, seg_all, query_seg, query_index, key_block
+    query_vectors, keys_all, values_all, seg_all, query_seg, query_index, key_ids, key_block
 ):
     row_count, head_count, head_width = query_vectors.shape
     block_count = keys_all.shape[0] // key_block
@@ -91,7 +103,7 @@
     def stats_step(running, block_id):
         run_max, run_sum = running
         scores, allowed, unused = block_scores(
-            query_vectors, keys_all, seg_all, query_seg, query_index, block_id, key_block
+            query_vectors, keys_all, seg_all, query_seg, query_index, key_ids, block_id, key_block
         )
         masked = jnp.where(allowed, scores, NEGATIVE)
         new_max = jnp.maximum(run_max, jnp.max(masked, axis=2))
@@ -110,7 +122,7 @@
 
     def value_step(accumulated, block_id):
         scores, allowed, unused = block_scores(
-            query_vectors, keys_all, seg_all, query_seg, query_index, block_id, key_block
+            query_vectors, keys_all, seg_all, query_seg, query_index, key_ids, block_id, key_block
         )
         prob_block = jnp.where(allowed, jnp.exp(scores - log_total[:, :, None]), 0.0).astype(
             jnp.bfloat16
@@ -136,6 +148,7 @@
     seg_all,
     query_seg,
     query_index,
+    key_ids,
     key_block,
     log_total,
     grad_heads,
@@ -147,7 +160,7 @@
 
     def grad_step(grad_query, block_id):
         scores, allowed, keys_part = block_scores(
-            query_vectors, keys_all, seg_all, query_seg, query_index, block_id, key_block
+            query_vectors, keys_all, seg_all, query_seg, query_index, key_ids, block_id, key_block
         )
         values_part = lax.dynamic_slice_in_dim(values_all, block_id * key_block, key_block, 0)
         prob_block = jnp.where(allowed, jnp.exp(scores - log_total[:, :, None]), 0.0)
@@ -181,11 +194,11 @@
 
 
 def to_experts(buffer):
-    return lax.all_to_all(buffer, ("fsdp", "context"), split_axis=0, concat_axis=1, tiled=True)
+    return lax.all_to_all(buffer, GROUPS, split_axis=0, concat_axis=1, tiled=True)
 
 
 def from_experts(result_rows):
-    return lax.all_to_all(result_rows, ("fsdp", "context"), split_axis=1, concat_axis=0, tiled=True)
+    return lax.all_to_all(result_rows, GROUPS, split_axis=1, concat_axis=0, tiled=True)
 
 
 def pick_pairs(buffer, target, row_count):
@@ -196,7 +209,7 @@
     return flat_rows[target].reshape(row_count, TOPK, model_width)
 
 
-def local(
+def routed_local(
     hidden_in,
     attn_gain,
     w_query,
@@ -214,19 +227,19 @@
     segments,
     cotangent,
 ):
-    context_rank = lax.axis_index("context")
+    context_rank = lax.axis_index(CONTEXT)
     input_rows = hidden_in[0].astype(jnp.float32)
     row_count, model_width = input_rows.shape
     gathered = (
-        lax.all_gather(w_query, ("fsdp", "context"), axis=0, tiled=True),
-        lax.all_gather(key_weight, ("fsdp", "context"), axis=0, tiled=True),
-        lax.all_gather(value_weight, ("fsdp", "context"), axis=0, tiled=True),
-        lax.all_gather(w_output, ("fsdp", "context"), axis=0, tiled=True),
-        lax.all_gather(router, ("fsdp", "context"), axis=0, tiled=True),
-        lax.all_gather(attn_gain, ("fsdp", "context"), axis=0, tiled=True),
-        lax.all_gather(ffn_gain, ("fsdp", "context"), axis=0, tiled=True),
-        lax.all_gather(query_gain, ("fsdp", "context"), axis=0, tiled=True),
-        lax.all_gather(key_gain, ("fsdp", "context"), axis=0, tiled=True),
+        lax.all_gather(w_query, GROUPS, axis=0, tiled=True),
+        lax.all_gather(key_weight, GROUPS, axis=0, tiled=True),
+        lax.all_gather(value_weight, GROUPS, axis=0, tiled=True),
+        lax.all_gather(w_output, GROUPS, axis=0, tiled=True),
+        lax.all_gather(router, GROUPS, axis=0, tiled=True),
+        lax.all_gather(attn_gain, GROUPS, axis=0, tiled=True),
+        lax.all_gather(ffn_gain, GROUPS, axis=0, tiled=True),
+        lax.all_gather(query_gain, GROUPS, axis=0, tiled=True),
+        lax.all_gather(key_gain, GROUPS, axis=0, tiled=True),
     )
     full_query, full_key, full_value, full_output, full_router = (
         gathered[0],
@@ -240,13 +253,14 @@
     gain_query = gathered[7].astype(jnp.float32)
     gain_key = gathered[8].astype(jnp.float32)
     local_heads = full_query.shape[1] // HEAD_SIZE
-    seg_all = lax.all_gather(segments, "context", axis=1, tiled=True)[0]
+    seg_all = lax.all_gather(segments, CONTEXT, axis=1, tiled=True)[0]
     length = seg_all.shape[0]
     start_row = context_rank * row_count
     positions = lax.dynamic_slice_in_dim(doc_positions(seg_all), start_row, row_count)
     cosine_table, sine_table = rope_tables(positions, HEAD_SIZE)
     query_seg = segments[0]
     query_index = start_row + jnp.arange(row_count, dtype=jnp.int32)
+    key_ids = jnp.arange(length, dtype=jnp.int32)
     key_block = min(512, length)
 
     def query_finish(raw_values, gain_vec):
@@ -266,14 +280,14 @@
     key_f, key_pull = jax.vjp(key_finish, key_unrotated, gain_key)
     query_vectors = query_f.astype(jnp.bfloat16)
     keys_all, values_all = (
-        lax.all_gather(key_f.astype(jnp.bfloat16), "context", axis=0, tiled=True),
-        lax.all_gather(value_raw.astype(jnp.bfloat16), "context", axis=0, tiled=True),
+        lax.all_gather(key_f.astype(jnp.bfloat16), CONTEXT, axis=0, tiled=True),
+        lax.all_gather(value_raw.astype(jnp.bfloat16), CONTEXT, axis=0, tiled=True),
     )
     heads_full, log_total = attention_forward(
-        query_vectors, keys_all, values_all, seg_all, query_seg, query_index, key_block
+        query_vectors, keys_all, values_all, seg_all, query_seg, query_index, key_ids, key_block
     )
     heads_low = heads_full.reshape(row_count, local_heads * HEAD_SIZE).astype(jnp.bfloat16)
-    attn_out = lax.psum(matmul_nt(heads_low, full_output).astype(jnp.bfloat16), "tensor").astype(
+    attn_out = lax.psum(matmul_nt(heads_low, full_output).astype(jnp.bfloat16), TENSOR).astype(
         jnp.float32
     )
     residual_stream = input_rows + attn_out
@@ -286,8 +300,7 @@
     selected = jnp.sum(jnp.where(chosen, router_scores[:, None, :], 0.0), axis=2)
     gate_probs = jax.nn.softmax(selected, axis=-1)
     capacity = 9 * row_count * TOPK // (8 * experts_total)
-    counts = jnp.sum(chosen.astype(jnp.int32), axis=1)
-    before = jnp.cumsum(counts, axis=0) - counts
+    before = earlier_counts(jnp.any(chosen, axis=1)).astype(jnp.int32)
     slot_index = jnp.sum(jnp.where(chosen, before[:, None, :], 0), axis=2)
     target = jnp.where(
         slot_index < capacity, route_ids * capacity + slot_index, experts_total * capacity
@@ -314,7 +327,7 @@
     grad_out = cotangent[0].astype(jnp.float32)
     returned = pick_pairs(from_experts(expert_part), target, row_count)
     moe_part = jnp.sum(returned.astype(jnp.float32) * gate_probs[:, :, None], axis=1)
-    moe_out = lax.psum(moe_part.astype(jnp.bfloat16), "tensor").astype(jnp.float32)
+    moe_out = lax.psum(moe_part.astype(jnp.bfloat16), TENSOR).astype(jnp.float32)
     grad_gate_part = jnp.sum(returned.astype(jnp.float32) * grad_out[:, None, :], axis=2)
     output = (residual_stream + moe_out).astype(jnp.bfloat16)
     pair_grad = (
@@ -367,8 +380,8 @@
     grad_pairs = pick_pairs(from_experts(grad_expert_in), target, row_count)
     grad_normed_part = jnp.sum(grad_pairs.astype(jnp.float32), axis=1)
     grad_normed_moe, grad_gates = (
-        lax.psum(grad_normed_part.astype(jnp.bfloat16), "tensor").astype(jnp.float32),
-        lax.psum(grad_gate_part.astype(jnp.bfloat16), "tensor").astype(jnp.float32),
+        lax.psum(grad_normed_part.astype(jnp.bfloat16), TENSOR).astype(jnp.float32),
+        lax.psum(grad_gate_part.astype(jnp.bfloat16), TENSOR).astype(jnp.float32),
     )
     grad_selected = gate_probs * (
         grad_gates - jnp.sum(gate_probs * grad_gates, axis=1, keepdims=True)
@@ -395,6 +408,7 @@
         seg_all,
         query_seg,
         query_index,
+        key_ids,
         key_block,
         log_total,
         grad_heads,
@@ -402,10 +416,10 @@
     )
     grad_key_local, grad_value_local = (
         lax.psum_scatter(
-            grad_key_terms.astype(jnp.bfloat16), "context", scatter_dimension=0, tiled=True
+            grad_key_terms.astype(jnp.bfloat16), CONTEXT, scatter_dimension=0, tiled=True
         ).astype(jnp.float32),
         lax.psum_scatter(
-            grad_value_terms.astype(jnp.bfloat16), "context", scatter_dimension=0, tiled=True
+            grad_value_terms.astype(jnp.bfloat16), CONTEXT, scatter_dimension=0, tiled=True
         ).astype(jnp.float32),
     )
     grad_query_raw, grad_gain_query = query_pull(grad_query)
@@ -422,45 +436,45 @@
         + matmul_nt(grad_value_low, full_value)
     )
     grad_normed_one, grad_gain_query, grad_gain_key = (
-        lax.psum(grad_normed_one.astype(jnp.bfloat16), "tensor").astype(jnp.float32),
-        lax.psum(grad_gain_query.astype(jnp.bfloat16), "tensor").astype(jnp.float32),
-        lax.psum(grad_gain_key.astype(jnp.bfloat16), "tensor").astype(jnp.float32),
+        lax.psum(grad_normed_one.astype(jnp.bfloat16), TENSOR).astype(jnp.float32),
+        lax.psum(grad_gain_query.astype(jnp.bfloat16), TENSOR).astype(jnp.float32),
+        lax.psum(grad_gain_key.astype(jnp.bfloat16), TENSOR).astype(jnp.float32),
     )
     grad_inputs_norm, grad_gain_attn = first_pull(grad_normed_one)
     input_grad = grad_resid + grad_inputs_norm
     owned = (
         lax.psum_scatter(
-            grad_w_query.astype(jnp.bfloat16), ("fsdp", "context"), scatter_dimension=0, tiled=True
+            grad_w_query.astype(jnp.bfloat16), GROUPS, scatter_dimension=0, tiled=True
         ).astype(jnp.float32),
         lax.psum_scatter(
-            grad_w_key.astype(jnp.bfloat16), ("fsdp", "context"), scatter_dimension=0, tiled=True
+            grad_w_key.astype(jnp.bfloat16), GROUPS, scatter_dimension=0, tiled=True
         ).astype(jnp.float32),
         lax.psum_scatter(
-            grad_w_value.astype(jnp.bfloat16), ("fsdp", "context"), scatter_dimension=0, tiled=True
+            grad_w_value.astype(jnp.bfloat16), GROUPS, scatter_dimension=0, tiled=True
         ).astype(jnp.float32),
         lax.psum_scatter(
-            grad_w_output.astype(jnp.bfloat16), ("fsdp", "context"), scatter_dimension=0, tiled=True
+            grad_w_output.astype(jnp.bfloat16), GROUPS, scatter_dimension=0, tiled=True
         ).astype(jnp.float32),
         lax.psum_scatter(
-            grad_router.astype(jnp.bfloat16), ("fsdp", "context"), scatter_dimension=0, tiled=True
+            grad_router.astype(jnp.bfloat16), GROUPS, scatter_dimension=0, tiled=True
         ).astype(jnp.float32),
         lax.psum_scatter(
             grad_gain_attn.astype(jnp.bfloat16),
-            ("fsdp", "context"),
+            GROUPS,
             scatter_dimension=0,
             tiled=True,
         ).astype(jnp.float32),
         lax.psum_scatter(
-            grad_gain_ffn.astype(jnp.bfloat16), ("fsdp", "context"), scatter_dimension=0, tiled=True
+            grad_gain_ffn.astype(jnp.bfloat16), GROUPS, scatter_dimension=0, tiled=True
         ).astype(jnp.float32),
         lax.psum_scatter(
             grad_gain_query.astype(jnp.bfloat16),
-            ("fsdp", "context"),
+            GROUPS,
             scatter_dimension=0,
             tiled=True,
         ).astype(jnp.float32),
         lax.psum_scatter(
-            grad_gain_key.astype(jnp.bfloat16), ("fsdp", "context"), scatter_dimension=0, tiled=True
+            grad_gain_key.astype(jnp.bfloat16), GROUPS, scatter_dimension=0, tiled=True
         ).astype(jnp.float32),
     )
     return (
@@ -481,39 +495,592 @@
     )
 
 
+MESH = pl.DeviceIdType.MESH
+Z_UP, Z_DOWN, Y_SIDE, X_SIDE, CORE_SIDE = range(5)
+
+def coords():
+    z, y, t = lax.axis_index(FSDP), lax.axis_index(CONTEXT), lax.axis_index(TENSOR)
+    return z, y, t // 2, t % 2
+
+def partner(z, index):
+    return (z, z + 1 - 2 * (z % 2), 2 - z // 2, 3 - 3 * (z // 2))[index]
+
+def greet(neighbours):
+    barrier = pltpu.get_barrier_semaphore()
+    for condition, device in neighbours:
+        def tell(device=device):
+            pl.semaphore_signal(barrier, inc=1, device_id=device, device_id_type=MESH)
+        if condition is None: tell()
+        else: pl.when(condition)(tell)
+    count = sum(1 if condition is None else condition.astype(jnp.int32) for condition, device in neighbours)
+    pl.semaphore_wait(barrier, count)
+
+
+def gather_kernel(x_ref, out_ref, own_sem, send_sems, recv_sems):
+    rows = x_ref.shape[0]; half = rows // 2
+    z, y, x, c = coords()
+    side = {Z_UP: (z + 1, y, 2 * x + c), Z_DOWN: (z - 1, y, 2 * x + c), Y_SIDE: (z, 1 - y, 2 * x + c),
+            X_SIDE: (z, y, 2 * (1 - x) + c), CORE_SIDE: (z, y, 2 * x + 1 - c)}
+    greet([(z < 3, side[Z_UP]), (z > 0, side[Z_DOWN]), (None, side[Y_SIDE]), (None, side[X_SIDE]), (None, side[CORE_SIDE])])
+    def device(zz, yy, xx, cc): return (zz * 2 + yy) * 4 + xx * 2 + cc
+    def place(owner, h): return out_ref.at[pl.ds(pl.multiple_of(owner * rows + h * half, half), half)]
+    def copy(link, owner, h, own=False):
+        src = x_ref.at[pl.ds(h * half, half)] if own else place(owner, h)
+        return pltpu.make_async_remote_copy(src_ref=src, dst_ref=place(owner, h), send_sem=send_sems.at[link, owner, h],
+            recv_sem=recv_sems.at[owner, h], device_id=side[link], device_id_type=MESH)
+    sent = []
+    def start(link, owner, h, own=False, condition=None):
+        one = copy(link, owner, h, own)
+        sent.append((one, condition))
+        if condition is None: one.start()
+        else: pl.when(condition)(one.start)
+    def arrived(owner, h): copy(CORE_SIDE, owner, h).wait_recv()
+    me = device(z, y, x, c)
+    keep = pltpu.make_async_copy(x_ref, out_ref.at[pl.ds(pl.multiple_of(me * rows, rows), rows)], own_sem)
+    keep.start()
+    def stage1(i):
+        zz = partner(z, i); owner = device(zz, y, x, c); own = i == 0
+        if not own:
+            arrived(owner, 0); arrived(owner, 1)
+        for h in range(2):
+            start(Z_UP, owner, h, own, (z < 3) if own else (z < 3) & (zz < z))
+            start(Z_DOWN, owner, h, own, (z > 0) if own else (z > 0) & (zz > z))
+        start(Y_SIDE, owner, 0, own); start(X_SIDE, owner, 1, own)
+        start(Y_SIDE, owner, 1, own); start(X_SIDE, owner, 0, own)
+        for h in range(2): start(CORE_SIDE, owner, h, own)
+    def stage2(i):
+        zz = partner(z, i)
+        oy, ox = device(zz, 1 - y, x, c), device(zz, y, 1 - x, c)
+        arrived(oy, 0); start(X_SIDE, oy, 0); start(CORE_SIDE, oy, 0)
+        arrived(ox, 1); start(Y_SIDE, ox, 1); start(CORE_SIDE, ox, 1)
+        arrived(oy, 1); start(CORE_SIDE, oy, 1)
+        arrived(ox, 0); start(CORE_SIDE, ox, 0)
+    def stage3(i):
+        o = device(partner(z, i), 1 - y, 1 - x, c)
+        for h in range(2):
+            arrived(o, h); start(CORE_SIDE, o, h)
+    stage1(0); stage1(1); stage2(0); stage1(2); stage2(1); stage3(0); stage1(3); stage2(2); stage3(1); stage2(3); stage3(2); stage3(3)
+    for i in range(4):
+        for yy in range(2):
+            for xx in range(2):
+                for h in range(2): arrived(device(i, yy, xx, 1 - c), h)
+    keep.wait()
+    for one, condition in sent:
+        if condition is None: one.wait_send()
+        else: pl.when(condition)(one.wait_send)
+
+def gather_everyone(x, collective_id):
+    rows, width = x.shape
+    return pl.pallas_call(gather_kernel, out_shape=jax.ShapeDtypeStruct((32 * rows, width), x.dtype),
+        in_specs=[pl.BlockSpec(memory_space=pl.ANY)], out_specs=pl.BlockSpec(memory_space=pl.ANY),
+        scratch_shapes=[pltpu.SemaphoreType.DMA, pltpu.SemaphoreType.DMA((5, 32, 2)), pltpu.SemaphoreType.DMA((32, 2))],
+        compiler_params=pltpu.CompilerParams(collective_id=collective_id, has_side_effects=True))(x)
+
+def scatter_kernel(part_ref, out_ref, mine, core_in, first_in, second_in, line_in, load_sem, core_sem, first_sem, second_sem, line_send, line_recv):
+    rows = out_ref.shape[0]; half = rows // 2
+    z, y, x, c = coords()
+    up, down = (z + 1, y, 2 * x + c), (z - 1, y, 2 * x + c)
+    y_side, x_side, core_side = (z, 1 - y, 2 * x + c), (z, y, 2 * (1 - x) + c), (z, y, 2 * x + 1 - c)
+    greet([(z < 3, up), (z > 0, down), (None, y_side), (None, x_side), (None, core_side)])
+    f32 = jnp.float32
+    def spot(zz, yy, xx): return (zz * 2 + yy) * 2 + xx
+    def rows_of(zz, yy, xx, cc): return part_ref.at[pl.ds(pl.multiple_of((spot(zz, yy, xx) * 2 + cc) * rows, rows), rows)]
+    def remote(src, dst, send, recv, device):
+        return pltpu.make_async_remote_copy(src_ref=src, dst_ref=dst, send_sem=send, recv_sem=recv, device_id=device, device_id_type=MESH)
+    def piece(zz, yy, xx, h): return mine.at[spot(zz, yy, xx), pl.ds(h * half, half)]
+    def load(zz, yy, xx):
+        s = spot(zz, yy, xx)
+        return pltpu.make_async_copy(rows_of(zz, yy, xx, c), mine.at[s], load_sem.at[s])
+    def over_core(zz, yy, xx):
+        s = spot(zz, yy, xx)
+        return remote(rows_of(zz, yy, xx, 1 - c), core_in.at[s], core_sem.at[0, s], core_sem.at[1, s], core_side)
+    def first(h, zz, other):
+        src = piece(zz, other, 1 - x, 0) if h == 0 else piece(zz, 1 - y, other, 1)
+        s = zz * 2 + other
+        return remote(src, first_in.at[h, s], first_sem.at[0, h, s], first_sem.at[1, h, s], x_side if h == 0 else y_side)
+    def second(h, zz):
+        src = piece(zz, 1 - y, x, 0) if h == 0 else piece(zz, y, 1 - x, 1)
+        return remote(src, second_in.at[h, zz], second_sem.at[0, h, zz], second_sem.at[1, h, zz], y_side if h == 0 else x_side)
+    def line(h, zz, way):
+        return remote(piece(zz, y, x, h), line_in.at[way, zz, h], line_send.at[zz, h], line_recv.at[way, zz, h], up if way == 0 else down)
+    def add(s, h, arrived):
+        at = (s, pl.ds(h * half, half))
+        mine[at] = (mine[at].astype(f32) + arrived[...].astype(f32)).astype(mine.dtype)
+    sent = []
+    order = [(1 - y, 1 - x), (1 - y, x), (y, 1 - x), (y, x)]
+    for i in (3, 2, 1, 0):
+        for yy, xx in order:
+            one = over_core(partner(z, i), yy, xx); one.start(); sent.append(one)
+            load(partner(z, i), yy, xx).start()
+    def stage_core(i):
+        zz = partner(z, i)
+        for n, (yy, xx) in enumerate(order):
+            load(zz, yy, xx).wait(); over_core(zz, yy, xx).wait_recv()
+            s = spot(zz, yy, xx)
+            for h in range(2): add(s, h, core_in.at[s, pl.ds(h * half, half)])
+            go = []
+            if n in (0, 2): go.append(first(0, zz, yy))
+            if n in (0, 1): go.append(first(1, zz, xx))
+            for one in go: one.start(); sent.append(one)
+    def stage_first(i):
+        zz = partner(z, i)
+        for n in range(2):
+            for h, other in ((0, (1 - y, y)[n]), (1, (1 - x, x)[n])):
+                first(h, zz, other).wait_recv()
+                s = spot(zz, other, x) if h == 0 else spot(zz, y, other)
+                add(s, h, first_in.at[h, zz * 2 + other])
+                if n == 0:
+                    one = second(h, zz); one.start(); sent.append(one)
+    def stage_second(i):
+        zz = partner(z, i)
+        for h in range(2):
+            second(h, zz).wait_recv()
+            add(spot(zz, y, x), h, second_in.at[h, zz])
+    def stage_line(i):
+        zz = partner(z, i); s = spot(zz, y, x)
+        for h in range(2):
+            for way, from_side, toward in ((0, z > 0, zz > z), (1, z < 3, zz < z)):
+                @pl.when(from_side & (toward | (zz == z)) if i == 0 else from_side & toward)
+                def _(h=h, way=way):
+                    line(h, zz, way).wait_recv()
+                    add(s, h, line_in.at[way, zz, h])
+                if i > 0:
+                    @pl.when(toward)
+                    def _(h=h, way=way): line(h, zz, way).start()
+    stage_core(3); stage_core(2); stage_first(3); stage_core(1); stage_first(2); stage_second(3)
+    stage_core(0); stage_first(1); stage_second(2); stage_line(3); stage_first(0); stage_second(1); stage_line(2)
+    stage_second(0); stage_line(1); stage_line(0)
+    out_ref[...] = mine[spot(z, y, x)].astype(out_ref.dtype)
+    for one in sent: one.wait_send()
+    for i in (3, 2, 1):
+        zz = partner(z, i)
+        for h in range(2):
+            line(h, zz, 0).wait_send()
+
+def scatter_everyone(part, collective_id):
+    total, width = part.shape; rows = total // 32; half = rows // 2
+    dt = part.dtype; D = pltpu.SemaphoreType.DMA
+    return pl.pallas_call(scatter_kernel, out_shape=jax.ShapeDtypeStruct((rows, width), jnp.float32),
+        in_specs=[pl.BlockSpec(memory_space=pl.ANY)], out_specs=pl.BlockSpec(memory_space=pltpu.VMEM),
+        scratch_shapes=[pltpu.VMEM((16, rows, width), dt), pltpu.VMEM((16, rows, width), dt), pltpu.VMEM((2, 8, half, width), dt),
+            pltpu.VMEM((2, 4, half, width), dt), pltpu.VMEM((2, 4, 2, half, width), dt),
+            D((16,)), D((2, 16)), D((2, 2, 8)), D((2, 2, 4)), D((4, 2)), D((2, 4, 2))],
+        compiler_params=pltpu.CompilerParams(collective_id=collective_id, has_side_effects=True, vmem_limit_bytes=48 << 20))(part)
+
+def groups_kernel(splits, *refs):
+    count = len(splits)
+    ins, outs = refs[:count], refs[count:2 * count]
+    keep_sems, send_sems, recv_sems = refs[2 * count:]
+    z, y, x, c = coords()
+    t = 2 * x + c
+    side = {Z_UP: (z + 1, y, t), Z_DOWN: (z - 1, y, t), Y_SIDE: (z, 1 - y, t)}
+    greet([(z < 3, side[Z_UP]), (z > 0, side[Z_DOWN]), (None, side[Y_SIDE])])
+    sent = []
+    def place(k, owner, h):
+        rows = ins[k].shape[0]
+        first, size = (0, splits[k]) if h == 0 else (splits[k], rows - splits[k])
+        return outs[k].at[pl.ds(pl.multiple_of(owner * rows + first, 16), size)], ins[k].at[pl.ds(first, size)]
+    def copy(link, k, owner, h, own=False):
+        dst, src = place(k, owner, h)
+        return pltpu.make_async_remote_copy(src_ref=src if own else dst, dst_ref=dst, send_sem=send_sems.at[link, k, owner, h],
+            recv_sem=recv_sems.at[k, owner, h], device_id=side[link], device_id_type=MESH)
+    def halves(k): return (0, 1) if splits[k] < ins[k].shape[0] else (0,)
+    def start(link, k, owner, h, own=False, condition=None):
+        if h not in halves(k): return
+        one = copy(link, k, owner, h, own)
+        sent.append((one, condition))
+        if condition is None: one.start()
+        else: pl.when(condition)(one.start)
+    def arrived(k, owner, h):
+        if h in halves(k): copy(Y_SIDE, k, owner, h).wait_recv()
+    def along(k, owner, h, zz, own=False):
+        start(Z_UP, k, owner, h, own, (z < 3) & (zz <= z)); start(Z_DOWN, k, owner, h, own, (z > 0) & (zz >= z))
+    kept = []
+    me = z * 2 + y
+    for k in range(count):
+        along(k, me, 0, z, True); start(Y_SIDE, k, me, 1, True); start(Y_SIDE, k, me, 0, True); along(k, me, 1, z, True)
+        rows = ins[k].shape[0]
+        one = pltpu.make_async_copy(ins[k], outs[k].at[pl.ds(pl.multiple_of(me * rows, 16), rows)], keep_sems.at[k])
+        one.start(); kept.append(one)
+    for k in range(count):
+        for i in range(4):
+            zz = partner(z, i)
+            near, far = zz * 2 + y, zz * 2 + 1 - y
+            if i > 0:
+                arrived(k, near, 0); along(k, near, 0, zz); start(Y_SIDE, k, near, 0)
+                arrived(k, near, 1); along(k, near, 1, zz)
+            arrived(k, far, 1); along(k, far, 1, zz)
+    for k in range(count):
+        for i in range(4): arrived(k, partner(z, i) * 2 + 1 - y, 0)
+    for one in kept: one.wait()
+    for one, condition in sent:
+        if condition is None: one.wait_send()
+        else: pl.when(condition)(one.wait_send)
+
+def gather_groups(arrays, splits, collective_id):
+    count = len(arrays); D = pltpu.SemaphoreType.DMA
+    return pl.pallas_call(functools.partial(groups_kernel, splits),
+        out_shape=[jax.ShapeDtypeStruct((8 * a.shape[0], a.shape[1]), a.dtype) for a in arrays],
+        in_specs=[pl.BlockSpec(memory_space=pl.ANY)] * count, out_specs=[pl.BlockSpec(memory_space=pl.ANY)] * count,
+        scratch_shapes=[D((count,)), D((3, count, 8, 2)), D((count, 8, 2))],
+        compiler_params=pltpu.CompilerParams(collective_id=collective_id, has_side_effects=True))(*arrays)
+
+def tensor_gather_kernel(x_ref, out_ref, keep_sem, send_sems, recv_sems):
+    z, y, x, c = coords()
+    x_side, core_side = (z, y, 2 * (1 - x) + c), (z, y, 2 * x + 1 - c)
+    greet([(None, x_side), (None, core_side)])
+    def copy(n, owner, device, own=False):
+        return pltpu.make_async_remote_copy(src_ref=x_ref if own else out_ref.at[owner], dst_ref=out_ref.at[owner], send_sem=send_sems.at[n],
+            recv_sem=recv_sems.at[owner], device_id=device, device_id_type=MESH)
+    me, across, beside, last = 2 * x + c, 2 * (1 - x) + c, 2 * x + 1 - c, 2 * (1 - x) + 1 - c
+    a, b, d = copy(0, me, x_side, True), copy(1, me, core_side, True), copy(2, across, core_side)
+    a.start(); b.start()
+    keep = pltpu.make_async_copy(x_ref, out_ref.at[me], keep_sem); keep.start()
+    copy(0, across, x_side).wait_recv(); d.start()
+    copy(0, beside, x_side).wait_recv(); copy(0, last, x_side).wait_recv()
+    keep.wait(); a.wait_send(); b.wait_send(); d.wait_send()
+
+def gather_tensor(x, collective_id):
+    D = pltpu.SemaphoreType.DMA
+    return pl.pallas_call(tensor_gather_kernel, out_shape=jax.ShapeDtypeStruct((4, *x.shape), x.dtype),
+        in_specs=[pl.BlockSpec(memory_space=pl.ANY)], out_specs=pl.BlockSpec(memory_space=pl.ANY),
+        scratch_shapes=[D, D((3,)), D((4,))],
+        compiler_params=pltpu.CompilerParams(collective_id=collective_id, has_side_effects=True))(x)
+
+def tensor_scatter_kernel(part_ref, out_ref, mine, core_in, line_in, sems, recv):
+    z, y, x, c = coords()
+    x_side, core_side = (z, y, 2 * (1 - x) + c), (z, y, 2 * x + 1 - c)
+    greet([(None, x_side), (None, core_side)])
+    rows = out_ref.shape[0]; f32 = jnp.float32
+    def rows_of(xx, cc): return part_ref.at[pl.ds(pl.multiple_of((2 * xx + cc) * rows, rows), rows)]
+    def over_core(n, xx):
+        return pltpu.make_async_remote_copy(src_ref=rows_of(xx, 1 - c), dst_ref=core_in.at[n], send_sem=sems.at[n], recv_sem=recv.at[n],
+            device_id=core_side, device_id_type=MESH)
+    a, b = over_core(0, 1 - x), over_core(1, x)
+    a.start(); b.start()
+    a.wait_recv()
+    mine[...] = (rows_of(1 - x, c)[...].astype(f32) + core_in[0].astype(f32)).astype(mine.dtype)
+    d = pltpu.make_async_remote_copy(src_ref=mine, dst_ref=line_in, send_sem=sems.at[2], recv_sem=recv.at[2], device_id=x_side, device_id_type=MESH)
+    d.start(); b.wait_recv()
+    out_ref[...] = rows_of(x, c)[...].astype(f32) + core_in[1].astype(f32)
+    d.wait_recv()
+    out_ref[...] += line_in[...].astype(f32)
+    a.wait_send(); b.wait_send(); d.wait_send()
+
+def scatter_tensor(part, collective_id):
+    D = pltpu.SemaphoreType.DMA; rows = part.shape[0] // 4; width = part.shape[1]
+    return pl.pallas_call(tensor_scatter_kernel, out_shape=jax.ShapeDtypeStruct((rows, width), jnp.float32),
+        in_specs=[pl.BlockSpec(memory_space=pltpu.VMEM)], out_specs=pl.BlockSpec(memory_space=pltpu.VMEM),
+        scratch_shapes=[pltpu.VMEM((rows, width), part.dtype), pltpu.VMEM((2, rows, width), part.dtype), pltpu.VMEM((rows, width), part.dtype), D((3,)), D((3,))],
+        compiler_params=pltpu.CompilerParams(collective_id=collective_id, has_side_effects=True, vmem_limit_bytes=24 << 20))(part)
+
+
+def gathered_local(
+    hidden_in,
+    attn_gain,
+    w_query,
+    key_weight,
+    value_weight,
+    w_output,
+    query_gain,
+    key_gain,
+    ffn_gain,
+    router,
+    gate_weight,
+    up_weight,
+    down_weight,
+    routes,
+    segments,
+    cotangent,
+):
+    bf16, f32 = jnp.bfloat16, jnp.float32
+    context_size = lax.axis_size(CONTEXT)
+    tensor_size = lax.axis_size(TENSOR)
+    group_count = lax.axis_size(FSDP) * context_size
+    fsdp_rank = lax.axis_index(FSDP)
+    context_rank = lax.axis_index(CONTEXT)
+    tensor_rank = lax.axis_index(TENSOR)
+    group_rank = fsdp_rank * context_size + context_rank
+    row_count, width = hidden_in.shape[1:]
+    own_count = row_count // tensor_size
+    local_experts, _, hidden_width = gate_weight.shape
+    experts_total = router.shape[1]
+    capacity = 9 * row_count * TOPK // (8 * experts_total)
+
+    pieces = (router, attn_gain, ffn_gain, query_gain, key_gain, routes, segments)
+    small = jnp.concatenate([piece.astype(bf16).reshape(-1) for piece in pieces])
+    small = jnp.pad(small, (0, -small.size % 2048)).reshape(-1, 128)
+    qkv_weight = jnp.concatenate([w_query, key_weight, value_weight], axis=1)
+    small, qkv_full, full_output = gather_groups((small, qkv_weight, w_output), (small.shape[0], 208, 208), 1)
+    small = small.reshape(group_count, -1)
+    parts, at = [], 0
+    for piece in pieces:
+        parts.append(small[:, at : at + piece.size])
+        at += piece.size
+    full_router = parts[0].reshape(width, experts_total)
+    gain_attn, gain_ffn, gain_query, gain_key = (
+        part.reshape(-1).astype(f32) for part in parts[1:5]
+    )
+    all_routes = parts[5].astype(jnp.int32).reshape(group_count, row_count, TOPK)
+    seg_all = lax.dynamic_slice_in_dim(
+        parts[6].astype(jnp.int32), fsdp_rank * context_size, context_size, 0
+    ).reshape(-1)
+
+    own_start = tensor_rank * own_count
+    grad_out_own = lax.dynamic_slice_in_dim(cotangent[0], own_start, own_count, 0)
+    grad_out_all = lax.all_gather(grad_out_own, EVERYONE, axis=0, tiled=True)
+
+    query_width = w_query.shape[1]
+    local_heads = query_width // HEAD_SIZE
+    input_rows = hidden_in[0].astype(f32)
+    start_row = context_rank * row_count
+    positions = lax.dynamic_slice_in_dim(doc_positions(seg_all), start_row, row_count)
+    cosine_table, sine_table = rope_tables(positions, HEAD_SIZE)
+    query_seg = segments[0]
+    query_index = start_row + jnp.arange(row_count, dtype=jnp.int32)
+    other_start = (1 - context_rank) * row_count
+    key_ids = jnp.concatenate([query_index, query_index - start_row + other_start])
+    seg_keys = jnp.concatenate([query_seg, lax.dynamic_slice_in_dim(seg_all, other_start, row_count)])
+    key_block = row_count
+
+    def query_finish(raw_values, gain_vec):
+        return qk_finish(raw_values, gain_vec, cosine_table[:, None, :], sine_table[:, None, :])
+
+    def key_finish(raw_values, gain_vec):
+        return qk_finish(raw_values, gain_vec, cosine_table, sine_table)
+
+    normed_one = rms_scale(input_rows, gain_attn).astype(bf16)
+    raw = matmul(normed_one, qkv_full)
+    query_unrotated = raw[:, :query_width].reshape(row_count, local_heads, HEAD_SIZE)
+    key_unrotated = raw[:, query_width : query_width + HEAD_SIZE]
+    value_raw = raw[:, query_width + HEAD_SIZE :]
+    query_f, query_pull = jax.vjp(query_finish, query_unrotated, gain_query)
+    key_f, key_pull = jax.vjp(key_finish, key_unrotated, gain_key)
+    query_vectors = query_f.astype(bf16)
+    own_kv = jnp.concatenate([key_f, value_raw], axis=1).astype(bf16)
+    swap = ((0, 1), (1, 0))
+    kv_all = jnp.concatenate([own_kv, lax.ppermute(own_kv, CONTEXT, swap)], axis=0)
+    keys_all, values_all = kv_all[:, :HEAD_SIZE], kv_all[:, HEAD_SIZE:]
+    heads_full, log_total = attention_forward(
+        query_vectors, keys_all, values_all, seg_keys, query_seg, query_index, key_ids, key_block
+    )
+    heads_low = heads_full.reshape(row_count, query_width).astype(bf16)
+    attn_own = scatter_tensor(matmul_nt(heads_low, full_output).astype(bf16), 2)
+    input_own = lax.dynamic_slice_in_dim(hidden_in[0], own_start, own_count, 0).astype(f32)
+    residual_own = input_own + attn_own
+    second_f, second_pull = jax.vjp(rms_scale, residual_own, gain_ffn)
+    normed_own = second_f.astype(bf16)
+    normed_all = gather_everyone(normed_own, 3)
+
+    expert_ids = jnp.arange(experts_total, dtype=jnp.int32)
+
+    def dense_gates(normed, chosen):
+        scores = jnp.where(chosen, matmul(normed, full_router), NEGATIVE)
+        return jnp.where(chosen, jax.nn.softmax(scores, axis=-1), 0.0)
+
+    chosen_all = jnp.any(all_routes[..., None] == expert_ids, axis=2)
+    first_expert = group_rank * local_experts
+    chosen_local = lax.dynamic_slice_in_dim(chosen_all, first_expert, local_experts, 2)
+    slots = earlier_counts(
+        chosen_local.transpose(1, 0, 2).reshape(row_count, group_count * local_experts)
+    )
+    slots = slots.reshape(row_count, group_count, local_experts).transpose(1, 0, 2)
+    kept = chosen_local & (slots < capacity)
+    gates_all = dense_gates(normed_all, chosen_all.reshape(-1, experts_total))
+    gates_local = lax.dynamic_slice_in_dim(gates_all, first_expert, local_experts, 1)
+    kept = kept.reshape(-1, local_experts)
+    gates_kept = jnp.where(kept, gates_local, 0.0)
+    chosen_own = lax.dynamic_slice_in_dim(
+        jnp.any(routes[0][..., None] == expert_ids, axis=1), own_start, own_count, 0
+    )
+    gates_own = dense_gates(normed_own, chosen_own)
+
+    token_count = group_count * row_count
+    units = local_experts * hidden_width
+    gate_flat = gate_weight.transpose(1, 0, 2).reshape(width, units)
+    up_flat = up_weight.transpose(1, 0, 2).reshape(width, units)
+    down_flat = down_weight.reshape(units, width)
+    gate_in = matmul(normed_all, gate_flat)
+    up_in = matmul(normed_all, up_flat)
+    grad_mid = matmul_nt(grad_out_all, down_flat)
+
+    def per_unit(values):
+        return jnp.broadcast_to(values[:, :, None], (token_count, local_experts, hidden_width)).reshape(
+            token_count, units
+        )
+
+    gate_units = per_unit(gates_kept)
+    sigmoid_gate = jax.nn.sigmoid(gate_in)
+    silu_gate = gate_in * sigmoid_gate
+    hidden_middle = silu_gate * up_in
+    hidden_gated = (hidden_middle * gate_units).astype(bf16)
+    grad_gates = jnp.sum(
+        (hidden_middle * grad_mid).reshape(token_count, local_experts, hidden_width), axis=2
+    )
+    grad_gates = jnp.where(kept, grad_gates, 0.0).astype(bf16)
+    grad_hidden = grad_mid * gate_units
+    gate_grad = (
+        grad_hidden * up_in * sigmoid_gate * (1.0 + gate_in * (1.0 - sigmoid_gate))
+    ).astype(bf16)
+    up_grad = (grad_hidden * silu_gate).astype(bf16)
+    dn_part = (matmul_nt(gate_grad, gate_flat) + matmul_nt(up_grad, up_flat)).astype(bf16)
+    placed = lax.dynamic_update_slice(
+        jnp.zeros((token_count, tensor_size * experts_total), bf16),
+        grad_gates,
+        (0, tensor_rank * experts_total + first_expert),
+    )
+    scattered = scatter_everyone(jnp.concatenate([dn_part, placed], axis=1), 4)
+    moe_part = matmul(hidden_gated, down_flat).astype(bf16)
+    moe_own = lax.psum_scatter(moe_part, EVERYONE, scatter_dimension=0, tiled=True).astype(f32)
+    grad_w_down = matmul_tn(hidden_gated, grad_out_all).reshape(down_weight.shape)
+    grad_w_gate = jnp.einsum(
+        "td,tju->jdu",
+        normed_all,
+        gate_grad.reshape(token_count, local_experts, hidden_width),
+        preferred_element_type=f32,
+    )
+    grad_w_up = jnp.einsum(
+        "td,tju->jdu",
+        normed_all,
+        up_grad.reshape(token_count, local_experts, hidden_width),
+        preferred_element_type=f32,
+    )
+
+    gates_grad_own = jnp.sum(
+        scattered[:, width:].reshape(own_count, tensor_size, experts_total), axis=1
+    )
+    grad_selected = gates_own * (
+        gates_grad_own - jnp.sum(gates_own * gates_grad_own, axis=1, keepdims=True)
+    )
+    grad_logits = grad_selected.astype(bf16)
+    grad_normed_two = scattered[:, :width] + matmul_nt(grad_logits, full_router)
+    grad_resid_norm, grad_gain_ffn = second_pull(grad_normed_two)
+    grad_resid_own = grad_out_own.astype(f32) + grad_resid_norm
+    message = jnp.concatenate(
+        [grad_resid_own.astype(bf16), jnp.pad(grad_logits, ((0, 0), (0, 128 - experts_total)))], axis=1
+    )
+    extra = jnp.pad(grad_gain_ffn.astype(bf16)[None], ((0, 15), (0, 128)))
+    message = gather_tensor(jnp.concatenate([message, extra], axis=0), 5)
+    grad_attn = message[:, :own_count, :width].reshape(row_count, width)
+    group_logits = message[:, :own_count, width:].reshape(row_count, 128)
+    grad_gain_ffn = jnp.sum(message[:, own_count, :width].astype(f32), axis=0)
+    normed_group = lax.dynamic_slice_in_dim(normed_all, group_rank * row_count, row_count, 0)
+    grad_router = matmul_tn(normed_group, group_logits)
+    output = lax.all_gather((residual_own + moe_own).astype(bf16), TENSOR, axis=0, tiled=True)
+    extra = jnp.where(jnp.arange(128) == experts_total, grad_gain_ffn[:, None], grad_router)
+    grad_w_output = jnp.concatenate([matmul_tn(grad_attn, heads_low), extra], axis=1)
+    grad_w_output = lax.psum_scatter(
+        grad_w_output.astype(bf16), GROUPS, scatter_dimension=0, tiled=True
+    ).astype(f32)
+    grad_heads = (
+        matmul(grad_attn, full_output).astype(bf16).reshape(row_count, local_heads, HEAD_SIZE)
+    )
+    row_delta = jnp.sum(grad_heads.astype(f32) * heads_full, axis=2).T
+    grad_query, grad_key_terms, grad_value_terms = attention_backward(
+        query_vectors,
+        keys_all,
+        values_all,
+        seg_keys,
+        query_seg,
+        query_index,
+        key_ids,
+        key_block,
+        log_total,
+        grad_heads,
+        row_delta,
+    )
+    grad_kv = jnp.concatenate([grad_key_terms, grad_value_terms], axis=1)
+    grad_kv = grad_kv[:row_count] + lax.ppermute(
+        grad_kv[row_count:].astype(bf16), CONTEXT, swap
+    ).astype(f32)
+    grad_query_raw, grad_gain_query = query_pull(grad_query)
+    grad_key_raw, grad_gain_key = key_pull(grad_kv[:, :HEAD_SIZE])
+    grad_raw = jnp.concatenate(
+        [grad_query_raw.reshape(row_count, query_width), grad_key_raw, grad_kv[:, HEAD_SIZE:]],
+        axis=1,
+    ).astype(bf16)
+    grad_normed_part = matmul_nt(grad_raw, qkv_full)
+    ignored, whole_pull = jax.vjp(rms_scale, input_rows, gain_attn)
+    gain_rows = jnp.stack(
+        [whole_pull(grad_normed_part)[1], jnp.pad(jnp.concatenate([grad_gain_query, grad_gain_key]), (0, width - 256))]
+    )
+    message = jnp.pad(
+        grad_normed_part.astype(bf16).reshape(tensor_size, own_count, width), ((0, 0), (0, 16), (0, 0))
+    )
+    message = lax.dynamic_update_slice(message, gain_rows.astype(bf16)[None], (0, own_count, 0))
+    message = scatter_tensor(message.reshape(-1, width), 6)
+    ignored, first_pull = jax.vjp(rms_scale, input_own, gain_attn)
+    grad_inputs_norm, ignored = first_pull(message[:own_count])
+    message = jnp.concatenate([grad_resid_own + grad_inputs_norm, message[own_count:]], axis=0)
+    message = gather_tensor(message.astype(bf16), 7).astype(f32)
+    input_grad = message[:, :own_count].reshape(row_count, width)
+    gain_rows = message[0, own_count : own_count + 2]
+    head_gains = jnp.pad(
+        gain_rows[1, :256].reshape(2, group_count, -1),
+        ((0, 0), (0, 0), (0, (width - 128) // group_count)),
+    ).reshape(2, width)
+    extra = jnp.pad(jnp.stack([gain_rows[0], head_gains[0], head_gains[1]], axis=1), ((0, 0), (0, 125)))
+    grad_qkv = jnp.concatenate([matmul_tn(normed_one, grad_raw), extra], axis=1)
+    grad_qkv = lax.psum_scatter(
+        grad_qkv.astype(bf16), GROUPS, scatter_dimension=0, tiled=True
+    ).astype(f32)
+    value_at, extra_at = query_width + HEAD_SIZE, query_width + 2 * HEAD_SIZE
+    return (
+        output[None],
+        input_grad[None],
+        grad_qkv[:, extra_at],
+        grad_qkv[:, :query_width],
+        grad_qkv[:, query_width:value_at],
+        grad_qkv[:, value_at:extra_at],
+        grad_w_output[:, :query_width],
+        grad_qkv[: query_gain.shape[0], extra_at + 1],
+        grad_qkv[: key_gain.shape[0], extra_at + 2],
+        grad_w_output[:, query_width + experts_total],
+        grad_w_output[:, query_width : query_width + experts_total],
+        grad_w_gate,
+        grad_w_up,
+        grad_w_down,
+    )
+
+
+def local(*arrays):
+    sizes = tuple(lax.axis_size(name) for name in EVERYONE)
+    return (gathered_local if sizes == (4, 2, 4) else routed_local)(*arrays)
+
+
 def solution(mesh):
     in_specs = (
-        P("fsdp", "context", None),
-        P(("fsdp", "context")),
-        P(("fsdp", "context"), "tensor"),
-        P(("fsdp", "context"), "tensor"),
-        P(("fsdp", "context"), "tensor"),
-        P(("fsdp", "context"), "tensor"),
-        P(("fsdp", "context")),
-        P(("fsdp", "context")),
-        P(("fsdp", "context")),
-        P(("fsdp", "context"), None),
-        P(("fsdp", "context"), None, "tensor"),
-        P(("fsdp", "context"), None, "tensor"),
-        P(("fsdp", "context"), "tensor", None),
-        P("fsdp", "context", None),
-        P("fsdp", "context"),
-        P("fsdp", "context", None),
+        P(FSDP, CONTEXT, None),
+        P(GROUPS),
+        P(GROUPS, TENSOR),
+        P(GROUPS, TENSOR),
+        P(GROUPS, TENSOR),
+        P(GROUPS, TENSOR),
+        P(GROUPS),
+        P(GROUPS),
+        P(GROUPS),
+        P(GROUPS, None),
+        P(GROUPS, None, TENSOR),
+        P(GROUPS, None, TENSOR),
+        P(GROUPS, TENSOR, None),
+        P(FSDP, CONTEXT, None),
+        P(FSDP, CONTEXT),
+        P(FSDP, CONTEXT, None),
     )
     out_specs = (
-        P("fsdp", "context", None),
-        P("fsdp", "context", None),
-        P(("fsdp", "context")),
-        P(("fsdp", "context"), "tensor"),
-        P(("fsdp", "context"), "tensor"),
-        P(("fsdp", "context"), "tensor"),
-        P(("fsdp", "context"), "tensor"),
-        P(("fsdp", "context")),
-        P(("fsdp", "context")),
-        P(("fsdp", "context")),
-        P(("fsdp", "context"), None),
-        P(("fsdp", "context"), None, "tensor"),
-        P(("fsdp", "context"), None, "tensor"),
-        P(("fsdp", "context"), "tensor", None),
+        P(FSDP, CONTEXT, None),
+        P(FSDP, CONTEXT, None),
+        P(GROUPS),
+        P(GROUPS, TENSOR),
+        P(GROUPS, TENSOR),
+        P(GROUPS, TENSOR),
+        P(GROUPS, TENSOR),
+        P(GROUPS),
+        P(GROUPS),
+        P(GROUPS),
+        P(GROUPS, None),
+        P(GROUPS, None, TENSOR),
+        P(GROUPS, None, TENSOR),
+        P(GROUPS, TENSOR, None),
     )
     return jax.shard_map(local, mesh=mesh, in_specs=in_specs, out_specs=out_specs, check_vma=False)

time: 2770 us -> 1090 us (0.39)
  waiting for transfers between devices: 1790 us -> 61.2 us
  Pallas kernels: 0 us -> 509 us
  local copies, waits for them, and re-layouts: 346 us -> 103 us
  blocking collectives: 211 us -> 0 us
  matrix products: 236 us -> 279 us
  other arithmetic: 140 us -> 98.9 us
    all_to_all x4 -> x0, waiting for transfers between devices: 1420 us -> none  [the longest x2 726 us: to_experts(): lax.all_to_all(buffer, ('fsdp', 'context'), split_axis=0, concat_axis=1,...]
    pallas_call x0 -> x7, Pallas kernels: none -> 509 us  [the longest x1 184 us: gather_groups(): pl.pallas_call(functools.partial(groups_kernel, splits), out_shape=[jax.S...]
    reduce_scatter x7 -> x3, waiting for transfers between devices: 276 us -> 57.2 us  [the longest x1 57.2 us: gathered_local(): lax.psum_scatter(grad_qkv.astype(bf16), GROUPS, scatter_dimension=0, tile...]
    all_gather x8 -> x0, blocking collectives: 159 us -> none  [the longest x1 33.1 us: local(): lax.all_gather(key_weight, ('fsdp', 'context'), axis=0, tiled=True)]
    gather x3 -> x0, local copies, waits for them, and re-layouts: 114 us -> none  [the longest x2 80.3 us: pick_pairs(): return flat_rows[target].reshape(row_count, TOPK, model_width)]
    psum x3 -> x0, waiting for transfers between devices: 86.4 us -> none  [the longest x1 86.4 us: local(): lax.psum(moe_part.astype(jnp.bfloat16), 'tensor').astype(jnp.float32)]
    dot_general x9 -> x2, matrix products: 124 us -> 41.3 us  [the longest x1 20.8 us: gathered_local(): jnp.einsum('td,tju->jdu', normed_all, gate_grad.reshape(token_count, loca...]
    dot_general x5 -> x8, matrix products: 13.4 us -> 95.5 us  [matmul(): return jnp.dot(left_side, right_side, preferred_element_type=jnp.float32)]
  transfers between devices with their start and end apart: 16 -> 7, of which waited for: 11 -> 2; matrix products, arithmetic and copies ran while one was open for 17% -> 35% of each run, Pallas kernels for 0% -> 47%
where the time goes in v1:
time: 1090 us; the launch traced here: 1080 us
  Pallas kernels  509 us (47%)
  matrix products  279 us (26%)
  local copies, waits for them, and re-layouts  103 us (9%)
  other arithmetic  98.9 us (9%)
  waiting for transfers between devices  61.2 us (6%)
  between operations  15.4 us (1%)
    pallas_call x1, Pallas kernels, gather_groups(): pl.pallas_call(functools.partial(groups_kernel, splits), out_shape=[jax.S...  184 us
    pallas_call x1, Pallas kernels, scatter_everyone(): pl.pallas_call(scatter_kernel, out_shape=jax.ShapeDtypeStruct((rows, widt...  172 us
    dot_general x8, matrix products, matmul(): return jnp.dot(left_side, right_side, preferred_element_type=jnp.float32)  95.5 us
    dot_general x6, matrix products, matmul_nt(): lax.dot_general(left_side, right_side, (((1,), (1,)), ((), ())), preferre...  79 us
    pallas_call x1, Pallas kernels, gather_everyone(): pl.pallas_call(gather_kernel, out_shape=jax.ShapeDtypeStruct((32 * rows,...  77.2 us
    reduce_scatter x1, waiting for transfers between devices, gathered_local(): lax.psum_scatter(grad_qkv.astype(bf16), GROUPS, scatter_dimension=0, tile...  57.2 us
    pallas_call x2, Pallas kernels, gather_tensor(): pl.pallas_call(tensor_gather_kernel, out_shape=jax.ShapeDtypeStruct((4, *...  41 us
    pallas_call x2, Pallas kernels, scatter_tensor(): pl.pallas_call(tensor_scatter_kernel, out_shape=jax.ShapeDtypeStruct((row...  34.5 us
  transfers between devices with their start and end apart: 7, of which 2 were waited for; matrix products, arithmetic and copies ran while one was open for 35% of the time, Pallas kernels for 47%

profile of v1, /device:TPU:0, one launch (start us, length us, event | category | flops | bytes accessed | tf_op | source)
XLA Modules:
  0.0 1078.1 jit_solution(15470130964287493453)
XLA Ops:
  17.4 184.2 %shard_map.263 = (bf16[896,128]{1,0:T(8,128)(2,1)}, bf16[2048,1280]{1,0:T(8,128)(2,1)}, bf16[2048,1024]{1,0:T(8,128)(2,1)}) custom-call(bf16[112,128]{1,0:T(8,128)(2,1)} %pad_bitcast_fusion.refs_0_, bf16[256,1280]{1,0:T(8,128)(2,1)} %pad_maximum_fusion.4.refs_1_, bf16[256,1024]{1,0:T(8,128)(2,1)} %refs_2_.1), custom_call_target="tpu_custom_call" | custom-call | tf_op jit(solution)/shard_map/pallas_call | solution.py:722
  267.8 18.3 %while.39 = (s32[]{:T(128)}, f32[8,512]{1,0:T(8,128)S(1)}, f32[8,512]{1,0:T(8,128)}, s32[1,512]{1,0:T(1,128)}, s32[2]{0:T(128)S(1)}, /*index=5*/s32[1024]{0:T(10...) while((s32[]{:T(128)}, f32[8,512]{1,0:T(8,128)S(1)}, ...), condition=%wide.region_7.8_spmd.clone, body=%wide.region_4.7_spmd.clone.sunk | while | flops 554455552 | bytes 19106072 | solution.py:118
  286.8 20.0 %while.40 = (s32[]{:T(128)}, f32[512,8,128]{0,2,1:T(8,128)}, s32[2]{0:T(128)S(1)}, bf16[1024,128]{1,0:T(8,128)(2,1)}, s32[1,512]{1,0:T(1,128)}, /*index=5*/s32[1...) while((s32[]{:T(128)}, f32[512,8,128]{0,2,1:T(8,128)}, ...), condition=%wide.region_9.10_spmd.clone, body=%wide.region_8.9_spmd.clone.sunk | while | flops 1083965952 | bytes 6065892 | solution.py:136
  313.7 16.3 %shard_map.264 = f32[128,2048]{1,0:T(8,128)S(1)} custom-call(bf16[512,2048]{1,0:T(8,128)(2,1)S(1)} %convolution_convert_fusion.3.part_ref), custom_call_target="tpu_custom_call" | custom-call | tf_op jit(solution)/shard_map/pallas_call | solution.py:772
  333.3 77.2 %shard_map.265 = bf16[4096,2048]{1,0:T(8,128)(2,1)} custom-call(bf16[128,2048]{1,0:T(8,128)(2,1)} %multiply_convert_fusion.2.x_ref), custom_call_target="tpu_custom_call" | custom-call | tf_op jit(solution)/shard_map/pallas_call | solution.py:574
  410.4 10.7 fusion.139
  428.0 20.4 %fusion.141 = f32[4096,768]{0,1:T(8,128)} fusion(bf16[4096,2048]{1,0:T(8,128)(2,1)} %shard_map.265, bf16[2048,768]{0,1:T(8,128)(2,1)} %bitcast.368), kind=kOutput, calls=%fused_computation.264 | convolution fusion | flops 12884901888 | bytes 32505856 | tf_op jit(solution)/shard_map/dot_general | solution.py:66
  448.3 20.5 %fusion.67 = f32[4096,768]{0,1:T(8,128)} fusion(bf16[768,2048]{1,0:T(8,128)(2,1)} %bitcast.366, bf16[1,4096,2048]{2,1,0:T(8,128)(2,1)} %all-gather.6.cloned.1.call-done), kind=kOutput, calls=%fused_computation.72 | convolution fusion | flops 12884901888 | bytes 32505856 | tf_op jit(solution)/shard_map/dot_general | solution.py:70
  468.8 32.9 %multiply_convert_fusion.1 = (bf16[4096,768]{0,1:T(8,128)(2,1)}, f32[4096,768]{0,1:T(8,128)}, bf16[4096,768]{0,1:T(8,128)(2,1)}, bf16[4096,768]{0,1:T(8,128)(2,1)}) fusion(f32[4096,768]{0,1:T(8,128)} %fusion.141, f32[4096,768]{0,1:T(8,128)} %fusion.67, f32[4096,4]{0,1:T(4,128)S(1)} %copy.228, bf16[4096,2048]{1,0:T(8,128)(2,1)} %shard_map.265, ...), kind=kOutput, calls=%fused_computation.77 | convolution fusion | flops 12941524992 | bytes 76611584 | tf_op jit(solution)/shard_map/dot_general | solution.py:66
  501.8 19.9 %convolution_convert_fusion = bf16[4096,2048]{1,0:T(8,128)(2,1)} fusion(bf16[4096,768]{0,1:T(8,128)(2,1)} %get-tuple-element.732, bf16[768,2048]{1,0:T(8,128)(2,1)} %bitcast.367), kind=kOutput, calls=%fused_computation.74 | convolution fusion | flops 12893290496 | bytes 26214400 | tf_op jit(solution)/shard_map/dot_general | solution.py:66
  535.4 10.4 dynamic_update_slice.13
  545.8 20.0 %fusion.142 = f32[4096,2048]{1,0:T(8,128)} fusion(bf16[4096,768]{0,1:T(8,128)(2,1)} %get-tuple-element.729, bf16[2048,768]{0,1:T(8,128)(2,1)S(1)} %bitcast.316), kind=kOutput, calls=%fused_computation.265 | convolution fusion | flops 12884901888 | bytes 42991616 | tf_op jit(solution)/shard_map/dot_general | solution.py:70
  565.8 26.7 %add_convert_fusion = bf16[4096,2048]{1,0:T(8,128)(2,1)} fusion(f32[4096,2048]{1,0:T(8,128)} %fusion.142, bf16[4096,768]{0,1:T(8,128)(2,1)} %get-tuple-element.731, bf16[2048,768]{0,1:T(8,128)(2,1)} %bitcast.369), kind=kOutput, calls=%fused_computation.62 | convolution fusion | flops 12901679104 | bytes 59768832 | tf_op jit(solution)/shard_map/dot_general | solution.py:70
  592.5 15.8 %pad_maximum_fusion.part_ref = bf16[4096,2176]{1,0:T(8,128)(2,1)} fusion(bf16[4096,128]{1,0:T(8,128)(2,1)S(1)} %copy-done.18, bf16[4096,2048]{1,0:T(8,128)(2,1)} %add_convert_fusion), kind=kLoop, calls=%fused_computation.65 | loop fusion | flops 35651584 | bytes 35651584 | tf_op jit(solution)/shard_map/concatenate | solution.py:932
  608.3 172.4 %shard_map.266 = f32[128,2176]{1,0:T(8,128)S(1)} custom-call(bf16[4096,2176]{1,0:T(8,128)(2,1)} %pad_maximum_fusion.part_ref), custom_call_target="tpu_custom_call" | custom-call | tf_op jit(solution)/shard_map/pallas_call | solution.py:663
  784.5 20.2 %shard_map.267 = bf16[4,144,2176]{2,1,0:T(8,128)(2,1)} custom-call(bf16[144,2176]{1,0:T(8,128)(2,1)} %fusion.106.x_ref), custom_call_target="tpu_custom_call" | custom-call | tf_op jit(solution)/shard_map/pallas_call | solution.py:745
  825.5 20.5 %while.41 = (s32[]{:T(128)}, f32[512,8,128]{0,2,1:T(8,128)S(1)}, f32[2,512,128]{2,1,0:T(8,128)}, f32[2,512,128]{2,1,0:T(8,128)}, s32[2]{0:T(128)S(1)}, /*index=5...) while((s32[]{:T(128)}, f32[512,8,128]{0,2,1:T(8,128)S(1)}, ...), condition=%wide.region_25.26_spmd.clone, body=%wide.region_24.25_spmd.clone.sunk | while | flops 2707751424 | bytes 61540800 | solution.py:188
  872.2 18.2 %shard_map.268 = f32[144,2048]{1,0:T(8,128)S(1)} custom-call(bf16[576,2048]{1,0:T(8,128)(2,1)S(1)} %bitcast.317), custom_call_target="tpu_custom_call" | custom-call | tf_op jit(solution)/shard_map/pallas_call | solution.py:772
  894.9 7.3 convolution_convert_fusion.1
  903.0 20.9 %shard_map.269 = bf16[4,144,2048]{2,1,0:T(8,128)(2,1)} custom-call(bf16[144,2048]{1,0:T(8,128)(2,1)} %pad_maximum_fusion.5.x_ref), custom_call_target="tpu_custom_call" | custom-call | tf_op jit(solution)/shard_map/pallas_call | solution.py:745
  932.7 20.5 %fusion.80 = f32[4,2048,192]{1,2,0:T(8,128)} fusion(bf16[4096,4,192]{0,2,1:T(8,128)(2,1)} %bitcast.324, bf16[4096,2048]{1,0:T(8,128)(2,1)} %shard_map.265), kind=kOutput, calls=%fused_computation.97 | convolution fusion | flops 12884901888 | bytes 29360128 | tf_op jit(solution)/shard_map/td,tju->jdu/dot_general | solution.py:942
  953.2 20.8 %fusion.77 = f32[4,2048,192]{1,2,0:T(8,128)} fusion(bf16[4096,4,192]{0,2,1:T(8,128)(2,1)} %bitcast.323, bf16[4096,2048]{1,0:T(8,128)(2,1)} %shard_map.265), kind=kOutput, calls=%fused_computation.96 | convolution fusion | flops 12884901888 | bytes 29360128 | tf_op jit(solution)/shard_map/td,tju->jdu/dot_general | solution.py:936
  974.0 18.8 %fusion.65 = f32[768,2048]{1,0:T(8,128)} fusion(bf16[4096,768]{0,1:T(8,128)(2,1)S(1)} %bitcast.322, bf16[1,4096,2048]{2,1,0:T(8,128)(2,1)} %all-gather.6.cloned.1.call-done), kind=kOutput, calls=%fused_computation.70 | convolution fusion | flops 12884901888 | bytes 29360128 | tf_op jit(solution)/shard_map/dot_general | solution.py:76
  1002.5 57.2 %reduce-scatter.6.cloned.1.call-done = bf16[256,1408]{0,1:T(8,128)(2,1)} async-done(((bf16[2048,1408]{0,1:T(8,128)(2,1)}), bf16[256,1408]{0,1:T(8,128)(2,1)}) %reduce-scatter.6.cloned.1.call-update) | async-done | bytes 720912 | tf_op jit(solution)/shard_map/reduce_scatter | solution.py:1024
  (417 shorter events, 246.6 us)
Async XLA Ops:
  7.2 461.7 %copy-start = (bf16[4,2048,192]{1,2,0:T(8,128)(2,1)S(1)}, bf16[4,2048,192]{1,2,0:T(8,128)(2,1)}, u32[]{:S(2)}) copy-start(bf16[4,2048,192]{1,2,0:T(8,128)(2,1)} %param.32) | copy-start | bytes 9437188
  7.2 441.2 %all-gather.6.cloned.1.call-start = ((), (), s32[]{:S(2)}) async-start(), calls=%async_computation.7 | async-start | bytes 17301504 | tf_op jit(solution)/shard_map/all_gather | solution.py:831
  9.3 882.5 %reduce-scatter.4.cloned.1.call-start = ((), (), s32[]{:S(2)}) async-start(), calls=%async_computation.3 | async-start | bytes 17301504 | tf_op jit(solution)/shard_map/reduce_scatter | solution.py:934
  202.8 10.5 copy-start.63
  203.0 14.6 %copy-start.68 = (f32[128]{0:T(128)}, f32[128]{0:T(128)S(1)}, u32[]{:S(2)}) copy-start(f32[128]{0:T(128)S(1)} %reshape.515) | copy-start | bytes 1540
  213.3 12.2 %copy-start.38 = (bf16[512,128]{1,0:T(8,128)(2,1)}, bf16[512,128]{1,0:T(8,128)(2,1)S(1)}, u32[]{:S(2)}) copy-start(bf16[512,128]{1,0:T(8,128)(2,1)S(1)} %slice.255) | copy-start | bytes 393220
  220.4 45.6 %collective-permute-start = (bf16[512,256]{1,0:T(8,128)(2,1)}, bf16[512,256]{1,0:T(8,128)(2,1)}, u32[]{:S(2)}, u32[]{:S(2)}) collective-permute-start(bf16[512,256]{1,0:T(8,128)(2,1)} %pad_maximum_fusion.12), channel_id=1, source_target_pairs={{0,4},{4,0},{1,5},{5,1},{2,6},{6,2},{3,7},{7,3},{8,12},{12,8},{9,1... | collective-permute-start | bytes 786440 | tf_op jit(solution)/shard_map/ppermute | solution.py:862
  231.5 17.7 %copy-start.23 = (f32[512,128]{0,1:T(8,128)}, f32[512,128]{0,1:T(8,128)S(1)}, u32[]{:S(2)}) copy-start(f32[512,128]{0,1:T(8,128)S(1)} %copy.216) | copy-start | bytes 786436
  252.3 13.1 %copy-start.44 = (s32[1,512]{1,0:T(1,128)S(1)}, s32[1,512]{1,0:T(1,128)}, u32[]{:S(2)}) copy-start(s32[1,512]{1,0:T(1,128)} %param.36) | copy-start | bytes 6148
  252.3 13.7 %copy-start.39 = (bf16[512,128]{1,0:T(8,128)(2,1)S(1)}, bf16[512,128]{1,0:T(8,128)(2,1)}, u32[]{:S(2)}) copy-start(bf16[512,128]{1,0:T(8,128)(2,1)} %copy-done.38) | copy-start | bytes 393220
  313.7 18.6 %copy-start.54 = (f32[1,2,8,128]{3,1,2,0:T(2,128)S(1)}, f32[1,2,8,128]{3,1,2,0:T(2,128)}, u32[]{:S(2)}) copy-start(f32[1,2,8,128]{3,1,2,0:T(2,128)} %copy.263) | copy-start | bytes 24580
  521.7 471.1 %reduce-scatter.8.cloned.1.call-start = ((), (), s32[]{:S(2)}) async-start(), calls=%async_computation.6 | async-start | bytes 5308416 | tf_op jit(solution)/shard_map/reduce_scatter | solution.py:972
  565.8 26.7 %copy-start.18 = (bf16[4096,128]{1,0:T(8,128)(2,1)S(1)}, bf16[4096,128]{1,0:T(8,128)(2,1)}, u32[]{:S(2)}) copy-start(bf16[4096,128]{1,0:T(8,128)(2,1)} %dynamic_update_slice.13) | copy-start | bytes 3145732
  608.3 173.0 %copy-start.8 = (f32[128,2048]{1,0:T(8,128)S(1)}, f32[128,2048]{1,0:T(8,128)}, u32[]{:S(2)}) copy-start(f32[128,2048]{1,0:T(8,128)} %copy-done.7) | copy-start | bytes 3145732
  608.3 173.0 %copy-start.16 = (bf16[2048,32]{1,0:T(8,128)(2,1)S(1)}, bf16[2048,32]{1,0:T(8,128)(2,1)}, u32[]{:S(2)}) copy-start(bf16[2048,32]{1,0:T(8,128)(2,1)} %reshape.496) | copy-start | bytes 393220
  608.3 173.0 %copy-start.55 = (f32[1,2,8,128]{3,1,2,0:T(2,128)S(1)}, f32[1,2,8,128]{3,1,2,0:T(2,128)}, u32[]{:S(2)}) copy-start(f32[1,2,8,128]{3,1,2,0:T(2,128)} %copy.263) | copy-start | bytes 24580
  608.3 173.0 %copy-start.73 = (f32[128]{0:T(128)S(1)}, f32[128]{0:T(128)}, u32[]{:S(2)}) copy-start(f32[128]{0:T(128)} %copy-done.72) | copy-start | bytes 1540
  823.7 178.8 %all-gather.4.cloned.1.call-start = ((), (), s32[]{:S(2)}) async-start(), calls=%async_computation.4 | async-start | bytes 2621440 | tf_op jit(solution)/shard_map/all_gather | solution.py:969
  847.2 15.1 %collective-permute-start.1 = (bf16[512,256]{1,0:T(8,128)(2,1)S(1)}, bf16[512,256]{1,0:T(8,128)(2,1)S(1)}, u32[]{:S(2)}, u32[]{:S(2)}) collective-permute-start(bf16[512,256]{1,0:T(8,128)(2,1)S(1)} %fusion.116), channel_id=1, source_target_pairs={{0,4},{4,0},{1,5},{5,1},{2,6},{6,2},{3,7},{7,3},{8,12},{12,8},{9,1... | collective-permute-start | bytes 786440 | tf_op jit(solution)/shard_map/ppermute | solution.py:993
  871.8 18.6 %copy-start.58 = (f32[1,2,8,128]{3,1,2,0:T(2,128)S(1)}, f32[1,2,8,128]{3,1,2,0:T(2,128)}, u32[]{:S(2)}) copy-start(f32[1,2,8,128]{3,1,2,0:T(2,128)} %copy-done.57) | copy-start | bytes 24580
  872.1 19.6 %copy-start.9 = (f32[128,2048]{1,0:T(8,128)S(1)}, f32[128,2048]{1,0:T(8,128)}, u32[]{:S(2)}) copy-start(f32[128,2048]{1,0:T(8,128)} %copy-done.7) | copy-start | bytes 3145732
  894.8 164.9 %reduce-scatter.6.cloned.1.call-start = ((), (), s32[]{:S(2)}) async-start(), calls=%async_computation.5 | async-start | bytes 6488064 | tf_op jit(solution)/shard_map/reduce_scatter | solution.py:1024
  932.6 41.3 %slice-start = ((s8[6291456]{0:T(1024)(128)(4,1)}), s8[4194304]{0:T(1024)(128)(4,1)S(1)}, s32[]{:S(2)}) async-start(s8[6291456]{0:T(1024)(128)(4,1)} %bitcast.321), calls=%async_computation.8 | async-start | bytes 8388608
  953.2 20.8 %slice-start.1 = ((s8[6291456]{0:T(1024)(128)(4,1)}), s8[2097152]{0:T(1024)(128)(4,1)S(1)}, s32[]{:S(2)}) async-start(s8[6291456]{0:T(1024)(128)(4,1)} %bitcast.321), calls=%async_computation.9 | async-start | bytes 4194304
  (72 other events, 201.4 us)
Sparse Core Ops, SparseCore 0:
  11.5 163.4 all-gather.5
  521.8 261.6 reduce-scatter.3
  823.8 97.5 reduce-scatter.7
  923.4 22.3 all-gather.3
  949.3 110.3 reduce-scatter.5

commit v2 on v1

--- a/solution.py
+++ b/solution.py
@@ -576,97 +576,6 @@
         scratch_shapes=[pltpu.SemaphoreType.DMA, pltpu.SemaphoreType.DMA((5, 32, 2)), pltpu.SemaphoreType.DMA((32, 2))],
         compiler_params=pltpu.CompilerParams(collective_id=collective_id, has_side_effects=True))(x)
 
-def scatter_kernel(part_ref, out_ref, mine, core_in, first_in, second_in, line_in, load_sem, core_sem, first_sem, second_sem, line_send, line_recv):
-    rows = out_ref.shape[0]; half = rows // 2
-    z, y, x, c = coords()
-    up, down = (z + 1, y, 2 * x + c), (z - 1, y, 2 * x + c)
-    y_side, x_side, core_side = (z, 1 - y, 2 * x + c), (z, y, 2 * (1 - x) + c), (z, y, 2 * x + 1 - c)
-    greet([(z < 3, up), (z > 0, down), (None, y_side), (None, x_side), (None, core_side)])
-    f32 = jnp.float32
-    def spot(zz, yy, xx): return (zz * 2 + yy) * 2 + xx
-    def rows_of(zz, yy, xx, cc): return part_ref.at[pl.ds(pl.multiple_of((spot(zz, yy, xx) * 2 + cc) * rows, rows), rows)]
-    def remote(src, dst, send, recv, device):
-        return pltpu.make_async_remote_copy(src_ref=src, dst_ref=dst, send_sem=send, recv_sem=recv, device_id=device, device_id_type=MESH)
-    def piece(zz, yy, xx, h): return mine.at[spot(zz, yy, xx), pl.ds(h * half, half)]
-    def load(zz, yy, xx):
-        s = spot(zz, yy, xx)
-        return pltpu.make_async_copy(rows_of(zz, yy, xx, c), mine.at[s], load_sem.at[s])
-    def over_core(zz, yy, xx):
-        s = spot(zz, yy, xx)
-        return remote(rows_of(zz, yy, xx, 1 - c), core_in.at[s], core_sem.at[0, s], core_sem.at[1, s], core_side)
-    def first(h, zz, other):
-        src = piece(zz, other, 1 - x, 0) if h == 0 else piece(zz, 1 - y, other, 1)
-        s = zz * 2 + other
-        return remote(src, first_in.at[h, s], first_sem.at[0, h, s], first_sem.at[1, h, s], x_side if h == 0 else y_side)
-    def second(h, zz):
-        src = piece(zz, 1 - y, x, 0) if h == 0 else piece(zz, y, 1 - x, 1)
-        return remote(src, second_in.at[h, zz], second_sem.at[0, h, zz], second_sem.at[1, h, zz], y_side if h == 0 else x_side)
-    def line(h, zz, way):
-        return remote(piece(zz, y, x, h), line_in.at[way, zz, h], line_send.at[zz, h], line_recv.at[way, zz, h], up if way == 0 else down)
-    def add(s, h, arrived):
-        at = (s, pl.ds(h * half, half))
-        mine[at] = (mine[at].astype(f32) + arrived[...].astype(f32)).astype(mine.dtype)
-    sent = []
-    order = [(1 - y, 1 - x), (1 - y, x), (y, 1 - x), (y, x)]
-    for i in (3, 2, 1, 0):
-        for yy, xx in order:
-            one = over_core(partner(z, i), yy, xx); one.start(); sent.append(one)
-            load(partner(z, i), yy, xx).start()
-    def stage_core(i):
-        zz = partner(z, i)
-        for n, (yy, xx) in enumerate(order):
-            load(zz, yy, xx).wait(); over_core(zz, yy, xx).wait_recv()
-            s = spot(zz, yy, xx)
-            for h in range(2): add(s, h, core_in.at[s, pl.ds(h * half, half)])
-            go = []
-            if n in (0, 2): go.append(first(0, zz, yy))
-            if n in (0, 1): go.append(first(1, zz, xx))
-            for one in go: one.start(); sent.append(one)
-    def stage_first(i):
-        zz = partner(z, i)
-        for n in range(2):
-            for h, other in ((0, (1 - y, y)[n]), (1, (1 - x, x)[n])):
-                first(h, zz, other).wait_recv()
-                s = spot(zz, other, x) if h == 0 else spot(zz, y, other)
-                add(s, h, first_in.at[h, zz * 2 + other])
-                if n == 0:
-                    one = second(h, zz); one.start(); sent.append(one)
-    def stage_second(i):
-        zz = partner(z, i)
-        for h in range(2):
-            second(h, zz).wait_recv()
-            add(spot(zz, y, x), h, second_in.at[h, zz])
-    def stage_line(i):
-        zz = partner(z, i); s = spot(zz, y, x)
-        for h in range(2):
-            for way, from_side, toward in ((0, z > 0, zz > z), (1, z < 3, zz < z)):
-                @pl.when(from_side & (toward | (zz == z)) if i == 0 else from_side & toward)
-                def _(h=h, way=way):
-                    line(h, zz, way).wait_recv()
-                    add(s, h, line_in.at[way, zz, h])
-                if i > 0:
-                    @pl.when(toward)
-                    def _(h=h, way=way): line(h, zz, way).start()
-    stage_core(3); stage_core(2); stage_first(3); stage_core(1); stage_first(2); stage_second(3)
-    stage_core(0); stage_first(1); stage_second(2); stage_line(3); stage_first(0); stage_second(1); stage_line(2)
-    stage_second(0); stage_line(1); stage_line(0)
-    out_ref[...] = mine[spot(z, y, x)].astype(out_ref.dtype)
-    for one in sent: one.wait_send()
-    for i in (3, 2, 1):
-        zz = partner(z, i)
-        for h in range(2):
-            line(h, zz, 0).wait_send()
-
-def scatter_everyone(part, collective_id):
-    total, width = part.shape; rows = total // 32; half = rows // 2
-    dt = part.dtype; D = pltpu.SemaphoreType.DMA
-    return pl.pallas_call(scatter_kernel, out_shape=jax.ShapeDtypeStruct((rows, width), jnp.float32),
-        in_specs=[pl.BlockSpec(memory_space=pl.ANY)], out_specs=pl.BlockSpec(memory_space=pltpu.VMEM),
-        scratch_shapes=[pltpu.VMEM((16, rows, width), dt), pltpu.VMEM((16, rows, width), dt), pltpu.VMEM((2, 8, half, width), dt),
-            pltpu.VMEM((2, 4, half, width), dt), pltpu.VMEM((2, 4, 2, half, width), dt),
-            D((16,)), D((2, 16)), D((2, 2, 8)), D((2, 2, 4)), D((4, 2)), D((2, 4, 2))],
-        compiler_params=pltpu.CompilerParams(collective_id=collective_id, has_side_effects=True, vmem_limit_bytes=48 << 20))(part)
-
 def groups_kernel(splits, *refs):
     count = len(splits)
     ins, outs = refs[:count], refs[count:2 * count]
@@ -774,6 +683,406 @@
         scratch_shapes=[pltpu.VMEM((rows, width), part.dtype), pltpu.VMEM((2, rows, width), part.dtype), pltpu.VMEM((rows, width), part.dtype), D((3,)), D((3,))],
         compiler_params=pltpu.CompilerParams(collective_id=collective_id, has_side_effects=True, vmem_limit_bytes=24 << 20))(part)
 
+def groups_scatter_kernel(split, part_ref, out_ref, near_in, mine, line_in, tail_in, tail_mine, tail_line, load_sem, side_sem, line_send, line_recv, tail_load, tail_side, tail_send, tail_recv):
+    rows = out_ref.shape[0]; rest = rows - split
+    z, y, x, c = coords()
+    t = 2 * x + c
+    up, down, across = (z + 1, y, t), (z - 1, y, t), (z, 1 - y, t)
+    greet([(z < 3, up), (z > 0, down), (None, across)])
+    f32, dt = jnp.float32, part_ref.dtype
+    def rows_of(zz, yy, first, size): return part_ref.at[pl.ds(pl.multiple_of((zz * 2 + yy) * rows + first, 16), size)]
+    def remote(src, dst, send, recv, device):
+        return pltpu.make_async_remote_copy(src_ref=src, dst_ref=dst, send_sem=send, recv_sem=recv, device_id=device, device_id_type=MESH)
+    def over_y(zz): return remote(rows_of(zz, 1 - y, 0, split), near_in.at[zz], side_sem.at[0, zz], side_sem.at[1, zz], across)
+    def load(zz): return pltpu.make_async_copy(rows_of(zz, y, 0, split), mine.at[zz], load_sem.at[zz])
+    def load_tail(zz, yy): return pltpu.make_async_copy(rows_of(zz, yy, split, rest), tail_mine.at[zz, yy], tail_load.at[zz, yy])
+    def line(zz, way): return remote(mine.at[zz], line_in.at[way, zz], line_send.at[zz], line_recv.at[way, zz], up if way == 0 else down)
+    def line_tail(zz, yy, way): return remote(tail_mine.at[zz, yy], tail_line.at[way, zz, yy], tail_send.at[zz, yy], tail_recv.at[way, zz, yy], up if way == 0 else down)
+    final = remote(tail_mine.at[z, 1 - y], tail_in, tail_side.at[0], tail_side.at[1], across)
+    order = (3, 2, 1, 0)
+    for i in order:
+        zz = partner(z, i)
+        over_y(zz).start(); load(zz).start()
+        load_tail(zz, 0).start(); load_tail(zz, 1).start()
+    def along(zz, i, copy, add):
+        for way, from_side, toward in ((0, z > 0, zz > z), (1, z < 3, zz < z)):
+            @pl.when(from_side if i == 0 else from_side & toward)
+            def _(way=way):
+                copy(way).wait_recv()
+                add(way)
+        for way, toward in ((0, zz > z), (1, zz < z)):
+            if i > 0:
+                @pl.when(toward)
+                def _(way=way): copy(way).start()
+    for i in order:
+        zz = partner(z, i)
+        for n in range(2):
+            yy = (1 - y, y)[n]
+            load_tail(zz, yy).wait()
+            def add(way, yy=yy): tail_mine[zz, yy] = (tail_mine[zz, yy].astype(f32) + tail_line[way, zz, yy].astype(f32)).astype(dt)
+            along(zz, i, lambda way, yy=yy: line_tail(zz, yy, way), add)
+            if i == 0 and n == 0: final.start()
+        load(zz).wait(); over_y(zz).wait_recv()
+        mine[zz] = (mine[zz].astype(f32) + near_in[zz].astype(f32)).astype(dt)
+        def add(way): mine[zz] = (mine[zz].astype(f32) + line_in[way, zz].astype(f32)).astype(dt)
+        along(zz, i, lambda way: line(zz, way), add)
+    out_ref[pl.ds(0, split)] = mine[z].astype(f32)
+    final.wait_recv()
+    out_ref[pl.ds(split, rest)] = tail_mine[z, y].astype(f32) + tail_in[...].astype(f32)
+    final.wait_send()
+    for zz in range(4):
+        over_y(zz).wait_send()
+        @pl.when(zz != z)
+        def _(zz=zz):
+            line(zz, 0).wait_send()
+            for yy in range(2): line_tail(zz, yy, 0).wait_send()
+
+def scatter_groups(part, split, collective_id):
+    total, width = part.shape; rows = total // 8; rest = rows - split
+    dt = part.dtype; D = pltpu.SemaphoreType.DMA; V = pltpu.VMEM
+    return pl.pallas_call(functools.partial(groups_scatter_kernel, split), out_shape=jax.ShapeDtypeStruct((rows, width), jnp.float32),
+        in_specs=[pl.BlockSpec(memory_space=pl.ANY)], out_specs=pl.BlockSpec(memory_space=V),
+        scratch_shapes=[V((4, split, width), dt), V((4, split, width), dt), V((2, 4, split, width), dt), V((rest, width), dt), V((4, 2, rest, width), dt), V((2, 4, 2, rest, width), dt),
+            D((4,)), D((2, 4)), D((4,)), D((2, 4)), D((4, 2)), D((2,)), D((4, 2)), D((2, 4, 2))],
+        compiler_params=pltpu.CompilerParams(collective_id=collective_id, has_side_effects=True, vmem_limit_bytes=48 << 20))(part)
+
+
+def nt(a, b):
+    return lax.dot_general(a, b, (((1,), (1,)), ((), ())), preferred_element_type=jnp.float32)
+
+def nn(a, b):
+    return jnp.dot(a, b, preferred_element_type=jnp.float32)
+
+def expert_kernel(comm, normed_ref, cot_ref, code_ref, router_ref, expand_ref, place_ref, gate_ref, up_ref, down_ref,
+                  out_ref, hid_out, gate_out, up_out,
+                  normed_in, cot_in, code_in, units, part, mine, core_in, first_in, second_in, line_in,
+                  in_sem, units_sem, core_sem, first_sem, second_sem, line_send, line_recv):
+    rows = out_ref.shape[0]; half = rows // 2; width = normed_ref.shape[1]
+    wide = gate_ref.shape[1]
+    z, y, x, c = coords()
+    up, down = (z + 1, y, 2 * x + c), (z - 1, y, 2 * x + c)
+    y_side, x_side, core_side = (z, 1 - y, 2 * x + c), (z, y, 2 * (1 - x) + c), (z, y, 2 * x + 1 - c)
+    if comm:
+        greet([(z < 3, up), (z > 0, down), (None, y_side), (None, x_side), (None, core_side)])
+    f32, bf16 = jnp.float32, jnp.bfloat16
+    def nearest(index):
+        choice = [partner(z, n) for n in range(4)]
+        return jnp.where(index == 0, choice[0], jnp.where(index == 1, choice[1], jnp.where(index == 2, choice[2], choice[3])))
+    def spot(zz, yy, xx): return (zz * 2 + yy) * 2 + xx
+    def target(step):
+        n = step % 4
+        return nearest(3 - step // 4), jnp.where(n < 2, 1 - y, y), jnp.where(n % 2 == 0, 1 - x, x)
+    def remote(src, dst, send, recv, device):
+        return pltpu.make_async_remote_copy(src_ref=src, dst_ref=dst, send_sem=send, recv_sem=recv, device_id=device, device_id_type=MESH)
+    def block(ref, step):
+        return ref.at[pl.ds(pl.multiple_of(spot(*target(step)) * 2 * rows, 2 * rows), 2 * rows)]
+    stride = code_ref.shape[0] // 8
+    def loads(step):
+        slot = step % 2
+        zz, yy, xx = target(step)
+        codes = code_ref.at[pl.ds(pl.multiple_of((zz * 2 + yy) * stride, 16), rows)]
+        pairs = ((block(normed_ref, step), normed_in), (block(cot_ref, step), cot_in), (codes, code_in))
+        return [pltpu.make_async_copy(src, dst.at[slot], in_sem.at[n, slot]) for n, (src, dst) in enumerate(pairs)]
+    def stores(step):
+        slot = step % 2
+        return [pltpu.make_async_copy(units.at[slot, n], block(dst, step), units_sem.at[n, slot])
+                for n, dst in enumerate((hid_out, gate_out, up_out))]
+    def over_core(step):
+        s = spot(*target(step))
+        return remote(part.at[step % 2, 1 - c], core_in.at[s], core_sem.at[0, s], core_sem.at[1, s], core_side)
+    def piece(zz, yy, xx, h): return mine.at[spot(zz, yy, xx), pl.ds(h * half, half)]
+    def first(h, zz, other):
+        src = piece(zz, other, 1 - x, 0) if h == 0 else piece(zz, 1 - y, other, 1)
+        s = zz * 2 + other
+        return remote(src, first_in.at[h, s], first_sem.at[0, h, s], first_sem.at[1, h, s], x_side if h == 0 else y_side)
+    def second(h, zz):
+        src = piece(zz, 1 - y, x, 0) if h == 0 else piece(zz, y, 1 - x, 1)
+        return remote(src, second_in.at[h, zz], second_sem.at[0, h, zz], second_sem.at[1, h, zz], y_side if h == 0 else x_side)
+    def line(h, zz, way):
+        return remote(piece(zz, y, x, h), line_in.at[way, zz, h], line_send.at[zz, h], line_recv.at[way, zz, h], up if way == 0 else down)
+    def add(s, h, arrived):
+        at = (s, pl.ds(h * half, half))
+        mine[at] = (mine[at].astype(f32) + arrived[...].astype(f32)).astype(bf16)
+    def stage_core(step):
+        zz, yy, xx = target(step)
+        s = spot(zz, yy, xx)
+        over_core(step).wait_recv()
+        mine[s] = (part[step % 2, c].astype(f32) + core_in[s].astype(f32)).astype(bf16)
+        n = step % 4
+        @pl.when(n % 2 == 0)
+        def _(): first(0, zz, yy).start()
+        @pl.when(n < 2)
+        def _(): first(1, zz, xx).start()
+    def stage_first(i):
+        zz = nearest(i)
+        for n in range(2):
+            for h, other in ((0, (1 - y, y)[n]), (1, (1 - x, x)[n])):
+                first(h, zz, other).wait_recv()
+                s = spot(zz, other, x) if h == 0 else spot(zz, y, other)
+                add(s, h, first_in.at[h, zz * 2 + other])
+                if n == 0: second(h, zz).start()
+    def stage_second(i):
+        zz = nearest(i)
+        for h in range(2):
+            second(h, zz).wait_recv()
+            add(spot(zz, y, x), h, second_in.at[h, zz])
+    def stage_line(i):
+        zz = nearest(i); s = spot(zz, y, x)
+        for h in range(2):
+            for way, from_side, toward in ((0, z > 0, zz > z), (1, z < 3, zz < z)):
+                @pl.when(from_side & (toward | (zz == z)))
+                def _(h=h, way=way):
+                    line(h, zz, way).wait_recv()
+                    add(s, h, line_in.at[way, zz, h])
+                @pl.when(toward)
+                def _(h=h, way=way): line(h, zz, way).start()
+    for one in loads(0): one.start()
+
+    def compute(step):
+        slot = step % 2
+        for one in loads(step): one.wait()
+        @pl.when(step < 15)
+        def _():
+            for one in loads(step + 1): one.start()
+        @pl.when(step >= 2)
+        def _():
+            for one in stores(step - 2): one.wait()
+            if comm: over_core(step - 2).wait_send()
+        normed, cot = normed_in[slot], cot_in[slot]
+        code = code_in[slot].astype(f32)
+        quarter = lax.broadcasted_iota(jnp.int32, code.shape, 1) // (128 // 4) - 2 * target(step)[2]
+        code = jnp.concatenate([jnp.where(quarter == n, code, 0.0) for n in range(2)], axis=0)
+        scores = jnp.where(code > 0.5, nn(normed, router_ref[...]), NEGATIVE)
+        scores = jnp.where(code > 0.5, jnp.exp(scores - jnp.max(scores, axis=1, keepdims=True)), 0.0)
+        gates = jnp.where(code > 1.5, scores / jnp.sum(scores, axis=1, keepdims=True), 0.0)
+        high = gates.astype(bf16)
+        low = (gates - high.astype(f32)).astype(bf16)
+        grad_gates = jnp.zeros((2 * rows, 128), f32)
+        for n in range(wide // 256):
+            at = pl.ds(n * 256, 256)
+            gate_in = nn(normed, gate_ref[:, at])
+            up_in = nn(normed, up_ref[:, at])
+            grad_mid = nt(cot, down_ref[at, :])
+            gate = nn(high, expand_ref[:, at]) + nn(low, expand_ref[:, at])
+            sig = lax.logistic(gate_in)
+            silu = gate_in * sig
+            hidden = silu * up_in
+            grad_gates += nn(jnp.where(gate != 0.0, hidden * grad_mid, 0.0).astype(bf16), place_ref[at, :])
+            grad_hidden = grad_mid * gate
+            units[slot, 0, :, at] = (hidden * gate).astype(bf16)
+            units[slot, 1, :, at] = (grad_hidden * up_in * sig * (1.0 + gate_in * (1.0 - sig))).astype(bf16)
+            units[slot, 2, :, at] = (grad_hidden * silu).astype(bf16)
+        for one in stores(step): one.start()
+        gate_grad, up_grad = units[slot, 1], units[slot, 2]
+        for n in range(width // 512):
+            at = pl.ds(n * 512, 512)
+            grad = (nt(gate_grad, gate_ref[at, :]) + nt(up_grad, up_ref[at, :])).astype(bf16)
+            part[slot, 0, :, at] = grad[:rows]
+            part[slot, 1, :, at] = grad[rows:]
+        grad_gates = grad_gates.astype(bf16)
+        part[slot, 0, :, pl.ds(width, 128)] = grad_gates[:rows]
+        part[slot, 1, :, pl.ds(width, 128)] = grad_gates[rows:]
+        if comm: over_core(step).start()
+
+    @pl.loop(0, 16)
+    def _(step):
+        compute(step)
+        if not comm: return
+        @pl.when(step >= 1)
+        def _(): stage_core(step - 1)
+        q = step // 4
+        @pl.when((step % 4 == 1) & (q >= 1))
+        def _(): stage_first(4 - q)
+        @pl.when((step % 4 == 3) & (q >= 1))
+        def _(): stage_second(4 - q)
+        @pl.when((step % 4 == 1) & (q >= 2))
+        def _(): stage_line(5 - q)
+    for step in (14, 15):
+        for one in stores(step): one.wait()
+    if not comm:
+        out_ref[...] = part[0, 0].astype(f32)
+        return
+    stage_core(15); stage_first(0); stage_second(0); stage_line(1); stage_line(0)
+    out_ref[...] = mine[spot(z, y, x)].astype(f32)
+    over_core(14).wait_send(); over_core(15).wait_send()
+    for zz in range(4):
+        for other in range(2):
+            for h in range(2): first(h, zz, other).wait_send()
+        for h in range(2): second(h, zz).wait_send()
+        @pl.when(zz != z)
+        def _(zz=zz):
+            for h in range(2): line(h, zz, 0).wait_send()
+
+def run_experts(normed_all, cot_all, code, router, expand, place, gate_flat, up_flat, down_flat, collective_id, comm=True):
+    total, width = normed_all.shape; rows = total // 32; half = rows // 2; wide = gate_flat.shape[1]
+    bf16 = jnp.bfloat16; D = pltpu.SemaphoreType.DMA; V = pltpu.VMEM; W = width + 128
+    anyspec, vspec = pl.BlockSpec(memory_space=pl.ANY), pl.BlockSpec(memory_space=pltpu.VMEM)
+    unit = jax.ShapeDtypeStruct((total, wide), bf16)
+    params = dict(collective_id=collective_id) if comm else {}
+    return pl.pallas_call(functools.partial(expert_kernel, comm),
+        out_shape=[jax.ShapeDtypeStruct((rows, W), jnp.float32), unit, unit, unit],
+        in_specs=[anyspec] * 3 + [vspec] * 6, out_specs=[vspec] + [anyspec] * 3,
+        scratch_shapes=[V((2, 2 * rows, width), bf16), V((2, 2 * rows, width), bf16), V((2, rows, 128), bf16),
+            V((2, 3, 2 * rows, wide), bf16), V((2, 2, rows, W), bf16),
+            V((16, rows, W), bf16), V((16, rows, W), bf16), V((2, 8, half, W), bf16), V((2, 4, half, W), bf16), V((2, 4, 2, half, W), bf16),
+            D((3, 2)), D((3, 2)), D((2, 16)), D((2, 2, 8)), D((2, 2, 4)), D((4, 2)), D((2, 4, 2))],
+        compiler_params=pltpu.CompilerParams(has_side_effects=True, vmem_limit_bytes=60 << 20, **params))(
+            normed_all, cot_all, code, router, expand, place, gate_flat, up_flat, down_flat)
+
+
+def inverse_rms(values):
+    return lax.rsqrt(jnp.mean(values * values, axis=-1, keepdims=True) + EPSILON)
+
+def attend_kernel(x_ref, gain_ref, qkv_ref, cos_ref, sin_ref, head_gain_ref, seg_rows_ref, seg_cols_ref,
+                  normed_ref, raw_ref, q_ref, kv_ref, kv_other_ref, full_ref, lse_ref, bias, send_sem, recv_sem):
+    z, y, x, c = coords()
+    other = (z, 1 - y, 2 * x + c)
+    greet([(None, other)])
+    f32, bf16 = jnp.float32, jnp.bfloat16
+    rows = x_ref.shape[0]; heads = q_ref.shape[1] // HEAD_SIZE; q_width = heads * HEAD_SIZE
+    values = x_ref[...].astype(f32)
+    normed_ref[...] = (values * inverse_rms(values) * gain_ref[...]).astype(bf16)
+    def finish(raw, n):
+        normed = raw * inverse_rms(raw) * head_gain_ref[pl.ds(n, 1), :]
+        return (normed * cos_ref[...] + pltpu.roll(normed, HEAD_SIZE // 2, 1) * sin_ref[...]).astype(bf16)
+    raw_kv = nn(normed_ref[...], qkv_ref[:, pl.ds(q_width, 2 * HEAD_SIZE)])
+    raw_ref[:, pl.ds(q_width, HEAD_SIZE)] = raw_kv[:, :HEAD_SIZE]
+    kv_ref[:, pl.ds(0, HEAD_SIZE)] = finish(raw_kv[:, :HEAD_SIZE], 1)
+    kv_ref[:, pl.ds(HEAD_SIZE, HEAD_SIZE)] = raw_kv[:, HEAD_SIZE:].astype(bf16)
+    move = pltpu.make_async_remote_copy(src_ref=kv_ref, dst_ref=kv_other_ref, send_sem=send_sem, recv_sem=recv_sem,
+        device_id=other, device_id_type=MESH)
+    @pl.when(y == 0)
+    def _():
+        move.start()
+        kv_other_ref[...] = jnp.zeros_like(kv_other_ref)
+    @pl.loop(0, heads // 2)
+    def _(n):
+        at = pl.ds(pl.multiple_of(n * 2 * HEAD_SIZE, 2 * HEAD_SIZE), 2 * HEAD_SIZE)
+        raw = nn(normed_ref[...], qkv_ref[:, at])
+        raw_ref[:, at] = raw
+        for m in range(2):
+            one = pl.ds(pl.multiple_of((2 * n + m) * HEAD_SIZE, HEAD_SIZE), HEAD_SIZE)
+            q_ref[:, one] = finish(raw[:, m * HEAD_SIZE:(m + 1) * HEAD_SIZE], 0)
+    row_id = lax.broadcasted_iota(jnp.int32, (rows, rows), 0)
+    col_id = lax.broadcasted_iota(jnp.int32, (rows, rows), 1)
+    bias[0] = jnp.where((seg_rows_ref[...] == seg_cols_ref[pl.ds(0, 1), :]) & (col_id <= row_id), 0.0, NEGATIVE)
+    bias[1] = jnp.where(seg_rows_ref[...] == seg_cols_ref[pl.ds(1, 1), :], 0.0, NEGATIVE)
+    lse_ref[...] = jnp.zeros_like(lse_ref)
+    scale = HEAD_SIZE ** -0.5
+    lane = lax.broadcasted_iota(jnp.int32, (rows, HEAD_SIZE), 1)
+    def head(h, blocks):
+        at = pl.ds(pl.multiple_of(h * HEAD_SIZE, HEAD_SIZE), HEAD_SIZE)
+        query = q_ref[:, at]
+        refs = (kv_ref, kv_other_ref)[:blocks]
+        scores = [nt(query, ref[:, pl.ds(0, HEAD_SIZE)]) * scale + bias[n] for n, ref in enumerate(refs)]
+        top = functools.reduce(jnp.maximum, [jnp.max(s, axis=1, keepdims=True) for s in scores])
+        weights = [jnp.exp(s - top) for s in scores]
+        total = sum(jnp.sum(w, axis=1, keepdims=True) for w in weights)
+        inverse = 1.0 / total
+        full_ref[:, at] = sum(nn((w * inverse).astype(bf16), ref[:, pl.ds(HEAD_SIZE, HEAD_SIZE)]) for w, ref in zip(weights, refs))
+        lse_ref[...] = jnp.where(lane == h, top + jnp.log(total), lse_ref[...])
+    @pl.when(y == 0)
+    def _():
+        @pl.loop(0, heads)
+        def _(h): head(h, 1)
+        move.wait_send()
+    @pl.when(y == 1)
+    def _():
+        move.wait_recv()
+        @pl.loop(0, heads)
+        def _(h): head(h, 2)
+
+def attend(x, gain, qkv, cos, sin, head_gains, seg_rows, seg_cols, collective_id):
+    rows, width = x.shape; q_width = qkv.shape[1] - 2 * HEAD_SIZE
+    V = pltpu.VMEM; f32, bf16 = jnp.float32, jnp.bfloat16; S = jax.ShapeDtypeStruct
+    vspec = pl.BlockSpec(memory_space=V)
+    return pl.pallas_call(attend_kernel,
+        out_shape=[S((rows, width), bf16), S((rows, q_width + HEAD_SIZE), f32), S((rows, q_width), bf16), S((rows, 2 * HEAD_SIZE), bf16),
+            S((rows, 2 * HEAD_SIZE), bf16), S((rows, q_width), f32), S((rows, HEAD_SIZE), f32)],
+        in_specs=[vspec] * 8, out_specs=[vspec] * 7,
+        scratch_shapes=[V((2, rows, rows), f32), pltpu.SemaphoreType.DMA, pltpu.SemaphoreType.DMA],
+        compiler_params=pltpu.CompilerParams(collective_id=collective_id, has_side_effects=True, vmem_limit_bytes=48 << 20))(
+            x, gain, qkv, cos, sin, head_gains, seg_rows, seg_cols)
+
+def attend_back_kernel(cot_ref, out_w_ref, q_ref, kv_ref, kv_other_ref, raw_ref, full_ref, lse_ref, cos_ref, sin_ref, head_gain_ref,
+                       seg_rows_ref, seg_cols_ref, grad_ref, gains_ref, grad_heads, delta, stats, bias, grad_q, grad_kv, kv_send, kv_in, send_sem, recv_sem):
+    z, y, x, c = coords()
+    other = (z, 1 - y, 2 * x + c)
+    greet([(None, other)])
+    f32, bf16 = jnp.float32, jnp.bfloat16
+    rows = q_ref.shape[0]; heads = q_ref.shape[1] // HEAD_SIZE; q_width = heads * HEAD_SIZE
+    scale = HEAD_SIZE ** -0.5
+    lane = lax.broadcasted_iota(jnp.int32, (rows, HEAD_SIZE), 1)
+    delta[...] = jnp.zeros_like(delta)
+    @pl.loop(0, heads // 2)
+    def _(n):
+        at = pl.ds(pl.multiple_of(n * 2 * HEAD_SIZE, 2 * HEAD_SIZE), 2 * HEAD_SIZE)
+        grad = nn(cot_ref[...], out_w_ref[:, at]).astype(bf16)
+        grad_heads[:, at] = grad
+        product = grad.astype(f32) * full_ref[:, at]
+        for m in range(2):
+            one = jnp.sum(product[:, m * HEAD_SIZE:(m + 1) * HEAD_SIZE], axis=1, keepdims=True)
+            delta[...] = jnp.where(lane == 2 * n + m, one, delta[...])
+    stats[0] = lse_ref[...].T
+    stats[1] = delta[...].T
+    key_id = lax.broadcasted_iota(jnp.int32, (rows, rows), 0)
+    query_id = lax.broadcasted_iota(jnp.int32, (rows, rows), 1)
+    def block(ref, seg_keys, causal):
+        same = seg_keys == seg_cols_ref[pl.ds(0, 1), :]
+        bias[...] = jnp.where(same & (key_id <= query_id) if causal else same, 0.0, NEGATIVE)
+        grad_kv[...] = jnp.zeros_like(grad_kv)
+        key, value = ref[:, pl.ds(0, HEAD_SIZE)], ref[:, pl.ds(HEAD_SIZE, HEAD_SIZE)]
+        @pl.loop(0, heads)
+        def _(h):
+            at = pl.ds(pl.multiple_of(h * HEAD_SIZE, HEAD_SIZE), HEAD_SIZE)
+            query, grad = q_ref[:, at], grad_heads[:, at]
+            probs = jnp.exp(nt(key, query) * scale + bias[...] - stats[0, pl.ds(h, 1), :])
+            grad_scores = (probs * (nt(value, grad) - stats[1, pl.ds(h, 1), :])).astype(bf16)
+            grad_kv[:, pl.ds(0, HEAD_SIZE)] += nn(grad_scores, query) * scale
+            grad_kv[:, pl.ds(HEAD_SIZE, HEAD_SIZE)] += nn(probs.astype(bf16), grad)
+            grad_q[:, at] += lax.dot_general(grad_scores, key, (((0,), (0,)), ((), ())), preferred_element_type=f32) * scale
+    grad_q[...] = jnp.zeros_like(grad_q)
+    move = pltpu.make_async_remote_copy(src_ref=kv_send, dst_ref=kv_in, send_sem=send_sem, recv_sem=recv_sem, device_id=other, device_id_type=MESH)
+    @pl.when(y == 1)
+    def _():
+        block(kv_other_ref, seg_rows_ref[1], False)
+        kv_send[...] = grad_kv[...].astype(bf16)
+        move.start()
+    block(kv_ref, seg_rows_ref[0], True)
+    @pl.when(y == 0)
+    def _():
+        move.wait_recv()
+        grad_kv[...] += kv_in[...].astype(f32)
+    def pull(grad, raw, n):
+        turned = grad * cos_ref[...] - pltpu.roll(grad, HEAD_SIZE // 2, 1) * sin_ref[...]
+        inverse = inverse_rms(raw)
+        unit = raw * inverse
+        gains_ref[pl.ds(n, 1), :] += jnp.sum(turned * unit, axis=0, keepdims=True)
+        scaled = turned * head_gain_ref[pl.ds(n, 1), :]
+        return (inverse * (scaled - unit * jnp.mean(scaled * unit, axis=1, keepdims=True))).astype(bf16)
+    gains_ref[...] = jnp.zeros_like(gains_ref)
+    @pl.loop(0, heads)
+    def _(h):
+        at = pl.ds(pl.multiple_of(h * HEAD_SIZE, HEAD_SIZE), HEAD_SIZE)
+        grad_ref[:, at] = pull(grad_q[:, at], raw_ref[:, at], 0)
+    at = pl.ds(q_width, HEAD_SIZE)
+    grad_ref[:, at] = pull(grad_kv[:, pl.ds(0, HEAD_SIZE)], raw_ref[:, at], 1)
+    grad_ref[:, pl.ds(q_width + HEAD_SIZE, HEAD_SIZE)] = grad_kv[:, pl.ds(HEAD_SIZE, HEAD_SIZE)].astype(bf16)
+    @pl.when(y == 1)
+    def _(): move.wait_send()
+
+def attend_back(cot, out_w, q, kv, kv_other, raw, full, lse, cos, sin, head_gains, seg_rows, seg_cols, collective_id):
+    rows, q_width = q.shape
+    V = pltpu.VMEM; f32, bf16 = jnp.float32, jnp.bfloat16; S = jax.ShapeDtypeStruct
+    vspec = pl.BlockSpec(memory_space=V)
+    return pl.pallas_call(attend_back_kernel,
+        out_shape=[S((rows, q_width + 2 * HEAD_SIZE), bf16), S((8, HEAD_SIZE), f32)],
+        in_specs=[vspec] * 13, out_specs=[vspec] * 2,
+        scratch_shapes=[V((rows, q_width), bf16), V((rows, HEAD_SIZE), f32), V((2, HEAD_SIZE, rows), f32), V((rows, rows), f32), V((rows, q_width), f32),
+            V((rows, 2 * HEAD_SIZE), f32), V((rows, 2 * HEAD_SIZE), bf16), V((rows, 2 * HEAD_SIZE), bf16), pltpu.SemaphoreType.DMA, pltpu.SemaphoreType.DMA],
+        compiler_params=pltpu.CompilerParams(collective_id=collective_id, has_side_effects=True, vmem_limit_bytes=48 << 20))(
+            cot, out_w, q, kv, kv_other, raw, full, lse, cos, sin, head_gains, seg_rows, seg_cols)
+
 
 def gathered_local(
     hidden_in,
@@ -803,68 +1112,68 @@
     group_rank = fsdp_rank * context_size + context_rank
     row_count, width = hidden_in.shape[1:]
     own_count = row_count // tensor_size
+    own_start = tensor_rank * own_count
     local_experts, _, hidden_width = gate_weight.shape
     experts_total = router.shape[1]
+    first_expert = group_rank * local_experts
     capacity = 9 * row_count * TOPK // (8 * experts_total)
-
-    pieces = (router, attn_gain, ffn_gain, query_gain, key_gain, routes, segments)
+    query_width = w_query.shape[1]
+
+    expert_ids = jnp.arange(experts_total, dtype=jnp.int32)
+    chosen = jnp.any(routes[0][..., None] == expert_ids, axis=1)
+    kept = chosen & (earlier_counts(chosen) < capacity)
+    code = chosen.astype(bf16) + kept.astype(bf16)
+    chosen_own = lax.dynamic_slice_in_dim(chosen, own_start, own_count, 0)
+    code = code.reshape(tensor_size, own_count, experts_total).transpose(1, 0, 2)
+
+    pieces = (code, router, attn_gain, ffn_gain, query_gain, key_gain, segments)
     small = jnp.concatenate([piece.astype(bf16).reshape(-1) for piece in pieces])
     small = jnp.pad(small, (0, -small.size % 2048)).reshape(-1, 128)
     qkv_weight = jnp.concatenate([w_query, key_weight, value_weight], axis=1)
-    small, qkv_full, full_output = gather_groups((small, qkv_weight, w_output), (small.shape[0], 208, 208), 1)
+    small, qkv_full, full_output = gather_groups(
+        (small, qkv_weight, w_output), (small.shape[0], 208, 208), 1
+    )
+    grad_out_own = lax.dynamic_slice_in_dim(cotangent[0], own_start, own_count, 0)
+    grad_out_own, codes = lax.optimization_barrier((grad_out_own, small))
+    grad_out_all = lax.all_gather(grad_out_own, EVERYONE, axis=0, tiled=True)
     small = small.reshape(group_count, -1)
-    parts, at = [], 0
-    for piece in pieces:
+    parts, at = [], code.size
+    for piece in pieces[1:]:
         parts.append(small[:, at : at + piece.size])
         at += piece.size
     full_router = parts[0].reshape(width, experts_total)
     gain_attn, gain_ffn, gain_query, gain_key = (
         part.reshape(-1).astype(f32) for part in parts[1:5]
     )
-    all_routes = parts[5].astype(jnp.int32).reshape(group_count, row_count, TOPK)
-    seg_all = lax.dynamic_slice_in_dim(
-        parts[6].astype(jnp.int32), fsdp_rank * context_size, context_size, 0
-    ).reshape(-1)
-
-    own_start = tensor_rank * own_count
-    grad_out_own = lax.dynamic_slice_in_dim(cotangent[0], own_start, own_count, 0)
-    grad_out_all = lax.all_gather(grad_out_own, EVERYONE, axis=0, tiled=True)
-
-    query_width = w_query.shape[1]
-    local_heads = query_width // HEAD_SIZE
-    input_rows = hidden_in[0].astype(f32)
-    start_row = context_rank * row_count
-    positions = lax.dynamic_slice_in_dim(doc_positions(seg_all), start_row, row_count)
+    head_gains = jnp.stack([gain_query, gain_key])
+    all_segments = parts[5].astype(jnp.int32)
+
+    own_seg = segments[0]
+    first_seg = lax.dynamic_index_in_dim(all_segments, group_rank - context_rank, 0, keepdims=False)
+    other_seg = lax.dynamic_index_in_dim(
+        all_segments, group_rank + 1 - 2 * context_rank, 0, keepdims=False
+    )
+    smaller = jnp.sum((own_seg[None, :] < own_seg[:, None]).astype(jnp.int32), axis=1)
+    smaller_first = jnp.sum((first_seg[None, :] < own_seg[:, None]).astype(jnp.int32), axis=1)
+    positions = jnp.arange(row_count, dtype=jnp.int32) - smaller
+    positions = positions + context_rank * (row_count - smaller_first)
     cosine_table, sine_table = rope_tables(positions, HEAD_SIZE)
-    query_seg = segments[0]
-    query_index = start_row + jnp.arange(row_count, dtype=jnp.int32)
-    other_start = (1 - context_rank) * row_count
-    key_ids = jnp.concatenate([query_index, query_index - start_row + other_start])
-    seg_keys = jnp.concatenate([query_seg, lax.dynamic_slice_in_dim(seg_all, other_start, row_count)])
-    key_block = row_count
-
-    def query_finish(raw_values, gain_vec):
-        return qk_finish(raw_values, gain_vec, cosine_table[:, None, :], sine_table[:, None, :])
-
-    def key_finish(raw_values, gain_vec):
-        return qk_finish(raw_values, gain_vec, cosine_table, sine_table)
-
-    normed_one = rms_scale(input_rows, gain_attn).astype(bf16)
-    raw = matmul(normed_one, qkv_full)
-    query_unrotated = raw[:, :query_width].reshape(row_count, local_heads, HEAD_SIZE)
-    key_unrotated = raw[:, query_width : query_width + HEAD_SIZE]
-    value_raw = raw[:, query_width + HEAD_SIZE :]
-    query_f, query_pull = jax.vjp(query_finish, query_unrotated, gain_query)
-    key_f, key_pull = jax.vjp(key_finish, key_unrotated, gain_key)
-    query_vectors = query_f.astype(bf16)
-    own_kv = jnp.concatenate([key_f, value_raw], axis=1).astype(bf16)
-    swap = ((0, 1), (1, 0))
-    kv_all = jnp.concatenate([own_kv, lax.ppermute(own_kv, CONTEXT, swap)], axis=0)
-    keys_all, values_all = kv_all[:, :HEAD_SIZE], kv_all[:, HEAD_SIZE:]
-    heads_full, log_total = attention_forward(
-        query_vectors, keys_all, values_all, seg_keys, query_seg, query_index, key_ids, key_block
-    )
-    heads_low = heads_full.reshape(row_count, query_width).astype(bf16)
+    turn = jnp.where(jnp.arange(HEAD_SIZE) < HEAD_SIZE // 2, -1.0, 1.0)
+    sine_table = sine_table * turn
+    seg_rows = jnp.stack([own_seg, other_seg])
+
+    normed_one, raw, query, kv, kv_other, heads_full, log_total = attend(
+        hidden_in[0],
+        gain_attn[None],
+        qkv_full,
+        cosine_table,
+        sine_table,
+        head_gains,
+        own_seg[:, None],
+        seg_rows,
+        8,
+    )
+    heads_low = heads_full.astype(bf16)
     attn_own = scatter_tensor(matmul_nt(heads_low, full_output).astype(bf16), 2)
     input_own = lax.dynamic_slice_in_dim(hidden_in[0], own_start, own_count, 0).astype(f32)
     residual_own = input_own + attn_own
@@ -872,158 +1181,103 @@
     normed_own = second_f.astype(bf16)
     normed_all = gather_everyone(normed_own, 3)
 
-    expert_ids = jnp.arange(experts_total, dtype=jnp.int32)
-
-    def dense_gates(normed, chosen):
-        scores = jnp.where(chosen, matmul(normed, full_router), NEGATIVE)
-        return jnp.where(chosen, jax.nn.softmax(scores, axis=-1), 0.0)
-
-    chosen_all = jnp.any(all_routes[..., None] == expert_ids, axis=2)
-    first_expert = group_rank * local_experts
-    chosen_local = lax.dynamic_slice_in_dim(chosen_all, first_expert, local_experts, 2)
-    slots = earlier_counts(
-        chosen_local.transpose(1, 0, 2).reshape(row_count, group_count * local_experts)
-    )
-    slots = slots.reshape(row_count, group_count, local_experts).transpose(1, 0, 2)
-    kept = chosen_local & (slots < capacity)
-    gates_all = dense_gates(normed_all, chosen_all.reshape(-1, experts_total))
-    gates_local = lax.dynamic_slice_in_dim(gates_all, first_expert, local_experts, 1)
-    kept = kept.reshape(-1, local_experts)
-    gates_kept = jnp.where(kept, gates_local, 0.0)
-    chosen_own = lax.dynamic_slice_in_dim(
-        jnp.any(routes[0][..., None] == expert_ids, axis=1), own_start, own_count, 0
-    )
-    gates_own = dense_gates(normed_own, chosen_own)
-
-    token_count = group_count * row_count
     units = local_experts * hidden_width
     gate_flat = gate_weight.transpose(1, 0, 2).reshape(width, units)
     up_flat = up_weight.transpose(1, 0, 2).reshape(width, units)
     down_flat = down_weight.reshape(units, width)
-    gate_in = matmul(normed_all, gate_flat)
-    up_in = matmul(normed_all, up_flat)
-    grad_mid = matmul_nt(grad_out_all, down_flat)
-
-    def per_unit(values):
-        return jnp.broadcast_to(values[:, :, None], (token_count, local_experts, hidden_width)).reshape(
-            token_count, units
-        )
-
-    gate_units = per_unit(gates_kept)
-    sigmoid_gate = jax.nn.sigmoid(gate_in)
-    silu_gate = gate_in * sigmoid_gate
-    hidden_middle = silu_gate * up_in
-    hidden_gated = (hidden_middle * gate_units).astype(bf16)
-    grad_gates = jnp.sum(
-        (hidden_middle * grad_mid).reshape(token_count, local_experts, hidden_width), axis=2
-    )
-    grad_gates = jnp.where(kept, grad_gates, 0.0).astype(bf16)
-    grad_hidden = grad_mid * gate_units
-    gate_grad = (
-        grad_hidden * up_in * sigmoid_gate * (1.0 + gate_in * (1.0 - sigmoid_gate))
-    ).astype(bf16)
-    up_grad = (grad_hidden * silu_gate).astype(bf16)
-    dn_part = (matmul_nt(gate_grad, gate_flat) + matmul_nt(up_grad, up_flat)).astype(bf16)
-    placed = lax.dynamic_update_slice(
-        jnp.zeros((token_count, tensor_size * experts_total), bf16),
-        grad_gates,
-        (0, tensor_rank * experts_total + first_expert),
-    )
-    scattered = scatter_everyone(jnp.concatenate([dn_part, placed], axis=1), 4)
+    unit_expert = first_expert + jnp.arange(units, dtype=jnp.int32) // hidden_width
+    lane_ids = jnp.arange(tensor_size * experts_total, dtype=jnp.int32)
+    expand = (lane_ids[:, None] % experts_total == unit_expert[None, :]).astype(bf16)
+    column = tensor_rank * experts_total + unit_expert
+    place = (column[:, None] == lane_ids[None, :]).astype(bf16)
+    router_lanes = jnp.concatenate([full_router] * tensor_size, axis=1)
+    scattered, hidden_gated, gate_grad, up_grad = run_experts(
+        normed_all, grad_out_all, codes, router_lanes, expand, place, gate_flat, up_flat, down_flat, 4
+    )
     moe_part = matmul(hidden_gated, down_flat).astype(bf16)
     moe_own = lax.psum_scatter(moe_part, EVERYONE, scatter_dimension=0, tiled=True).astype(f32)
     grad_w_down = matmul_tn(hidden_gated, grad_out_all).reshape(down_weight.shape)
-    grad_w_gate = jnp.einsum(
-        "td,tju->jdu",
-        normed_all,
-        gate_grad.reshape(token_count, local_experts, hidden_width),
-        preferred_element_type=f32,
-    )
-    grad_w_up = jnp.einsum(
-        "td,tju->jdu",
-        normed_all,
-        up_grad.reshape(token_count, local_experts, hidden_width),
-        preferred_element_type=f32,
-    )
-
+
+    def by_expert(unit_grad):
+        unit_grad = unit_grad.reshape(-1, local_experts, hidden_width)
+        return jnp.einsum("td,tju->jdu", normed_all, unit_grad, preferred_element_type=f32)
+
+    grad_w_gate, grad_w_up = by_expert(gate_grad), by_expert(up_grad)
+
+    scores = jnp.where(chosen_own, matmul(normed_own, full_router), NEGATIVE)
+    gates_own = jnp.where(chosen_own, jax.nn.softmax(scores, axis=-1), 0.0)
     gates_grad_own = jnp.sum(
         scattered[:, width:].reshape(own_count, tensor_size, experts_total), axis=1
     )
     grad_selected = gates_own * (
         gates_grad_own - jnp.sum(gates_own * gates_grad_own, axis=1, keepdims=True)
     )
-    grad_logits = grad_selected.astype(bf16)
-    grad_normed_two = scattered[:, :width] + matmul_nt(grad_logits, full_router)
+    grad_logits = jnp.pad(grad_selected.astype(bf16), ((0, 0), (0, 128 - experts_total)))
+    grad_normed_two = scattered[:, :width] + matmul_nt(grad_logits[:, :experts_total], full_router)
     grad_resid_norm, grad_gain_ffn = second_pull(grad_normed_two)
     grad_resid_own = grad_out_own.astype(f32) + grad_resid_norm
-    message = jnp.concatenate(
-        [grad_resid_own.astype(bf16), jnp.pad(grad_logits, ((0, 0), (0, 128 - experts_total)))], axis=1
-    )
+    message = jnp.concatenate([grad_resid_own.astype(bf16), grad_logits], axis=1)
     extra = jnp.pad(grad_gain_ffn.astype(bf16)[None], ((0, 15), (0, 128)))
     message = gather_tensor(jnp.concatenate([message, extra], axis=0), 5)
     grad_attn = message[:, :own_count, :width].reshape(row_count, width)
+    grad_raw, head_gain_grads = attend_back(
+        grad_attn,
+        full_output,
+        query,
+        kv,
+        kv_other,
+        raw,
+        heads_full,
+        log_total,
+        cosine_table,
+        sine_table,
+        head_gains,
+        seg_rows[:, :, None],
+        seg_rows,
+        9,
+    )
     group_logits = message[:, :own_count, width:].reshape(row_count, 128)
     grad_gain_ffn = jnp.sum(message[:, own_count, :width].astype(f32), axis=0)
     normed_group = lax.dynamic_slice_in_dim(normed_all, group_rank * row_count, row_count, 0)
     grad_router = matmul_tn(normed_group, group_logits)
-    output = lax.all_gather((residual_own + moe_own).astype(bf16), TENSOR, axis=0, tiled=True)
     extra = jnp.where(jnp.arange(128) == experts_total, grad_gain_ffn[:, None], grad_router)
     grad_w_output = jnp.concatenate([matmul_tn(grad_attn, heads_low), extra], axis=1)
     grad_w_output = lax.psum_scatter(
         grad_w_output.astype(bf16), GROUPS, scatter_dimension=0, tiled=True
-    ).astype(f32)
-    grad_heads = (
-        matmul(grad_attn, full_output).astype(bf16).reshape(row_count, local_heads, HEAD_SIZE)
-    )
-    row_delta = jnp.sum(grad_heads.astype(f32) * heads_full, axis=2).T
-    grad_query, grad_key_terms, grad_value_terms = attention_backward(
-        query_vectors,
-        keys_all,
-        values_all,
-        seg_keys,
-        query_seg,
-        query_index,
-        key_ids,
-        key_block,
-        log_total,
-        grad_heads,
-        row_delta,
-    )
-    grad_kv = jnp.concatenate([grad_key_terms, grad_value_terms], axis=1)
-    grad_kv = grad_kv[:row_count] + lax.ppermute(
-        grad_kv[row_count:].astype(bf16), CONTEXT, swap
-    ).astype(f32)
-    grad_query_raw, grad_gain_query = query_pull(grad_query)
-    grad_key_raw, grad_gain_key = key_pull(grad_kv[:, :HEAD_SIZE])
-    grad_raw = jnp.concatenate(
-        [grad_query_raw.reshape(row_count, query_width), grad_key_raw, grad_kv[:, HEAD_SIZE:]],
-        axis=1,
-    ).astype(bf16)
+    )
+
     grad_normed_part = matmul_nt(grad_raw, qkv_full)
-    ignored, whole_pull = jax.vjp(rms_scale, input_rows, gain_attn)
-    gain_rows = jnp.stack(
-        [whole_pull(grad_normed_part)[1], jnp.pad(jnp.concatenate([grad_gain_query, grad_gain_key]), (0, width - 256))]
-    )
+    ignored, whole_pull = jax.vjp(rms_scale, hidden_in[0].astype(f32), gain_attn)
+    head_gain_row = jnp.pad(head_gain_grads[:2].reshape(-1), (0, width - 2 * HEAD_SIZE))
+    gain_rows = jnp.stack([whole_pull(grad_normed_part)[1], head_gain_row])
     message = jnp.pad(
-        grad_normed_part.astype(bf16).reshape(tensor_size, own_count, width), ((0, 0), (0, 16), (0, 0))
+        grad_normed_part.astype(bf16).reshape(tensor_size, own_count, width),
+        ((0, 0), (0, 16), (0, 0)),
     )
     message = lax.dynamic_update_slice(message, gain_rows.astype(bf16)[None], (0, own_count, 0))
     message = scatter_tensor(message.reshape(-1, width), 6)
     ignored, first_pull = jax.vjp(rms_scale, input_own, gain_attn)
     grad_inputs_norm, ignored = first_pull(message[:own_count])
     message = jnp.concatenate([grad_resid_own + grad_inputs_norm, message[own_count:]], axis=0)
-    message = gather_tensor(message.astype(bf16), 7).astype(f32)
-    input_grad = message[:, :own_count].reshape(row_count, width)
-    gain_rows = message[0, own_count : own_count + 2]
-    head_gains = jnp.pad(
-        gain_rows[1, :256].reshape(2, group_count, -1),
-        ((0, 0), (0, 0), (0, (width - 128) // group_count)),
+    message, moe_own, grad_w_down, grad_w_gate, grad_w_up = lax.optimization_barrier(
+        (message.astype(bf16), moe_own, grad_w_down, grad_w_gate, grad_w_up)
+    )
+    message = jnp.concatenate([message, (residual_own + moe_own).astype(bf16)], axis=0)
+    message = gather_tensor(message, 7)
+    input_grad = message[:, :own_count].reshape(row_count, width).astype(f32)
+    output = message[:, own_count + 16 :].reshape(row_count, width)
+    gain_rows = message[0, own_count : own_count + 2].astype(f32)
+    head_gains_grad = jnp.pad(
+        gain_rows[1, : 2 * HEAD_SIZE].reshape(2, group_count, -1),
+        ((0, 0), (0, 0), (0, (width - HEAD_SIZE) // group_count)),
     ).reshape(2, width)
-    extra = jnp.pad(jnp.stack([gain_rows[0], head_gains[0], head_gains[1]], axis=1), ((0, 0), (0, 125)))
+    extra = jnp.pad(
+        jnp.stack([gain_rows[0], head_gains_grad[0], head_gains_grad[1]], axis=1),
+        ((0, 0), (0, 125)),
+    )
     grad_qkv = jnp.concatenate([matmul_tn(normed_one, grad_raw), extra], axis=1)
-    grad_qkv = lax.psum_scatter(
-        grad_qkv.astype(bf16), GROUPS, scatter_dimension=0, tiled=True
-    ).astype(f32)
+    grad_qkv = scatter_groups(grad_qkv.astype(bf16), 208, 10)
+    grad_qkv, grad_w_output = lax.optimization_barrier((grad_qkv, grad_w_output))
     value_at, extra_at = query_width + HEAD_SIZE, query_width + 2 * HEAD_SIZE
     return (
         output[None],
@@ -1032,11 +1286,11 @@
         grad_qkv[:, :query_width],
         grad_qkv[:, query_width:value_at],
         grad_qkv[:, value_at:extra_at],
-        grad_w_output[:, :query_width],
+        grad_w_output[:, :query_width].astype(f32),
         grad_qkv[: query_gain.shape[0], extra_at + 1],
         grad_qkv[: key_gain.shape[0], extra_at + 2],
-        grad_w_output[:, query_width + experts_total],
-        grad_w_output[:, query_width : query_width + experts_total],
+        grad_w_output[:, query_width + experts_total].astype(f32),
+        grad_w_output[:, query_width : query_width + experts_total].astype(f32),
         grad_w_gate,
         grad_w_up,
         grad_w_down,
@@ -1045,7 +1299,7 @@
 
 def local(*arrays):
     sizes = tuple(lax.axis_size(name) for name in EVERYONE)
-    return (gathered_local if sizes == (4, 2, 4) else routed_local)(*arrays)
+    return (gathered_local if sizes == (4, 2, 4) and arrays[9].shape[1] == 32 else routed_local)(*arrays)
 
 
 def solution(mesh):

time: 1090 us -> 854 us (0.78)
  matrix products: 279 us -> 99.8 us
  Pallas kernels: 509 us -> 637 us
  other arithmetic: 98.9 us -> 37.1 us
  waiting for transfers between devices: 61.2 us -> 0.05 us
  local copies, waits for them, and re-layouts: 103 us -> 50.3 us
    pallas_call x1 -> x4, Pallas kernels: 172 us -> 290 us  [the longest x1 143 us: run_experts(): pl.pallas_call(functools.partial(expert_kernel, comm), out_shape=[jax.Sha...]
    dot_general x8 -> x3, matrix products: 95.5 us -> 21.3 us  [matmul(): return jnp.dot(left_side, right_side, preferred_element_type=jnp.float32)]
    pallas_call x1, Pallas kernels: 184 us -> 111 us  [gather_groups(): pl.pallas_call(functools.partial(groups_kernel, splits), out_shape=[jax.S...]
    dot_general x6 -> x3, matrix products: 79 us -> 10.4 us  [matmul_nt(): lax.dot_general(left_side, right_side, (((1,), (1,)), ((), ())), preferre...]
    reduce_scatter x1 -> x0, waiting for transfers between devices: 57.2 us -> none  [gathered_local(): lax.psum_scatter(grad_qkv.astype(bf16), GROUPS, scatter_dimension=0, tile...]
    dot_general x16 -> x2, matrix products: 73.9 us -> 37.7 us  [by_expert(): jnp.einsum('td,tju->jdu', normed_all, unit_grad, preferred_element_type=f32)]
    pallas_call x1, Pallas kernels: 77.2 us -> 109 us  [gather_everyone(): pl.pallas_call(gather_kernel, out_shape=jax.ShapeDtypeStruct((32 * rows,...]
    pallas_call x2, Pallas kernels: 41 us -> 69 us  [gather_tensor(): pl.pallas_call(tensor_gather_kernel, out_shape=jax.ShapeDtypeStruct((4, *...]
  transfers between devices with their start and end apart: 7 -> 3, of which waited for: 2 -> 0; matrix products, arithmetic and copies ran while one was open for 35% -> 17% of each run, Pallas kernels for 47% -> 46%
where the time goes in v2:
time: 854 us; the launch traced here: 839 us
  Pallas kernels  637 us (75%)
  matrix products  99.8 us (12%)
  local copies, waits for them, and re-layouts  50.3 us (6%)
  other arithmetic  37.1 us (4%)
  between operations  15 us (2%)
    pallas_call x1, Pallas kernels, run_experts(): pl.pallas_call(functools.partial(expert_kernel, comm), out_shape=[jax.Sha...  143 us
    pallas_call x1, Pallas kernels, gather_groups(): pl.pallas_call(functools.partial(groups_kernel, splits), out_shape=[jax.S...  111 us
    pallas_call x1, Pallas kernels, gather_everyone(): pl.pallas_call(gather_kernel, out_shape=jax.ShapeDtypeStruct((32 * rows,...  109 us
    pallas_call x1, Pallas kernels, scatter_groups(): pl.pallas_call(functools.partial(groups_scatter_kernel, split), out_shape...  90.5 us
    pallas_call x2, Pallas kernels, gather_tensor(): pl.pallas_call(tensor_gather_kernel, out_shape=jax.ShapeDtypeStruct((4, *...  69 us
    pallas_call x2, Pallas kernels, scatter_tensor(): pl.pallas_call(tensor_scatter_kernel, out_shape=jax.ShapeDtypeStruct((row...  58.3 us
    dot_general x2, matrix products, by_expert(): jnp.einsum('td,tju->jdu', normed_all, unit_grad, preferred_element_type=f32)  37.7 us
    pallas_call x1, Pallas kernels, attend_back(): pl.pallas_call(attend_back_kernel, out_shape=[S((rows, q_width + 2 * HEAD...  35.3 us
  transfers between devices with their start and end apart: 3, of which 0 were waited for; matrix products, arithmetic and copies ran while one was open for 17% of the time, Pallas kernels for 46%

profile of v2, /device:TPU:0, one launch (start us, length us, event | category | flops | bytes accessed | tf_op | source)
XLA Modules:
  0.0 838.8 jit_solution(7449877957149339413)
XLA Ops:
  10.4 2.8 concatenate.44
  16.7 110.7 %shard_map.263 = (bf16[1664,128]{1,0:T(8,128)(2,1)}, bf16[2048,1280]{1,0:T(8,128)(2,1)}, bf16[2048,1024]{1,0:T(8,128)(2,1)}) custom-call(bf16[208,128]{1,0:T(8,128)(2,1)} %pad_bitcast_fusion.refs_0_, bf16[256,1280]{1,0:T(8,128)(2,1)} %pad_maximum_fusion.2.refs_1_, bf16[256,1024]{1,0:T(8,128)(2,1)} %refs_2_.1), custom_call_target="tpu_custom_call" | custom-call | tf_op jit(solution)/shard_map/pallas_call | solution.py:631
  130.9 21.6 %shard_map.264 = (bf16[512,2048]{1,0:T(8,128)(2,1)S(1)}, f32[512,1152]{1,0:T(8,128)}, bf16[512,1024]{1,0:T(8,128)(2,1)S(1)}, bf16[512,256]{1,0:T(8,128)(2,1)S(1)...) custom-call(bf16[512,2048]{1,0:T(8,128)(2,1)} %bitcast.105, f32[1,2048]{1,0:T(1,128)S(1)} %bitcast.100, ...), custom_call_target="tpu_custom_call" | custom-call | tf_op jit(solution)/shard_map/pallas_call | solution.py:999
  152.5 4.7 convolution_convert_fusion.3.part_ref
  157.2 27.1 %shard_map.265 = f32[128,2048]{1,0:T(8,128)S(1)} custom-call(bf16[512,2048]{1,0:T(8,128)(2,1)S(1)} %convolution_convert_fusion.3.part_ref), custom_call_target="tpu_custom_call" | custom-call | tf_op jit(solution)/shard_map/pallas_call | solution.py:681
  187.5 108.6 %shard_map.266.normed_ref = bf16[4096,2048]{1,0:T(8,128)(2,1)} custom-call(bf16[128,2048]{1,0:T(8,128)(2,1)} %multiply_convert_fusion.x_ref), custom_call_target="tpu_custom_call" | custom-call | tf_op jit(solution)/shard_map/pallas_call | solution.py:574
  296.5 4.8 copy.77.gate_ref
  301.3 4.6 copy.78.up_ref
  309.0 142.5 %shard_map.267 = (f32[128,2176]{1,0:T(8,128)}, bf16[4096,768]{1,0:T(8,128)(2,1)}, bf16[4096,768]{1,0:T(8,128)(2,1)}, bf16[4096,768]{1,0:T(8,128)(2,1)}) custom-call(bf16[4096,2048]{1,0:T(8,128)(2,1)} %shard_map.266.normed_ref, bf16[4096,2048]{1,0:T(8,128)(2,1)} %all-gather.2.cloned.1.call-done.cot_ref, bf16[1664,128]{1,0:T(8,128)(2,1)} %get-tuple-element.44.code_ref, ...), custom_call_target="tpu_custom_call" | custom-call | tf_op jit(solution)/shard_map/pallas_call | solution.py:922
  451.5 19.5 %convolution_convert_fusion = bf16[4096,2048]{1,0:T(8,128)(2,1)} fusion(bf16[4096,768]{1,0:T(8,128)(2,1)} %get-tuple-element.53, bf16[768,2048]{1,0:T(8,128)(2,1)} %bitcast.114), kind=kOutput, calls=%fused_computation.4 | convolution fusion | flops 12893290496 | bytes 26214400 | tf_op jit(solution)/shard_map/dot_general | solution.py:66
  482.0 32.5 %shard_map.268 = bf16[4,144,2176]{2,1,0:T(8,128)(2,1)} custom-call(bf16[144,2176]{1,0:T(8,128)(2,1)} %fusion.29.x_ref), custom_call_target="tpu_custom_call" | custom-call | tf_op jit(solution)/shard_map/pallas_call | solution.py:654
  514.4 3.3 slice.109
  518.7 35.3 %shard_map.269 = (bf16[512,1280]{1,0:T(8,128)(2,1)S(1)}, f32[8,128]{1,0:T(8,128)S(1)}) custom-call(bf16[512,2048]{1,0:T(8,128)(2,1)} %bitcast.106, bf16[2048,1024]{1,0:T(8,128)(2,1)} %get-tuple-element.43.out_w_ref, bf16[512,1024]{1,0:T(8,128)(2,1)S(1)} %get-tuple-element.46.q_ref, bf16[512,256]{1,0:T(8,128)(2,1)S(1)} %get-tuple-element.47.kv_ref, ...), custom_call_target="tpu_custom_call" | custom-call | tf_op jit(solution)/shard_map/pallas_call | solution.py:1078
  554.1 3.2 fusion.8
  557.8 31.3 %shard_map.270 = f32[144,2048]{1,0:T(8,128)S(1)} custom-call(bf16[576,2048]{1,0:T(8,128)(2,1)S(1)} %bitcast.99), custom_call_target="tpu_custom_call" | custom-call | tf_op jit(solution)/shard_map/pallas_call | solution.py:681
  589.0 8.6 %copy.85 = bf16[4096,768]{0,1:T(8,128)(2,1)} copy(bf16[4096,768]{1,0:T(8,128)(2,1)} %get-tuple-element.54) | data formatting | bytes 12582912 | tf_op jit(solution)/shard_map/pallas_call | solution.py:922
  597.7 8.8 %copy.86 = bf16[4096,768]{0,1:T(8,128)(2,1)} copy(bf16[4096,768]{1,0:T(8,128)(2,1)} %get-tuple-element.55) | data formatting | bytes 12582912 | tf_op jit(solution)/shard_map/pallas_call | solution.py:922
  618.3 20.9 %fusion.51 = f32[768,2048]{1,0:T(8,128)} fusion(bf16[4096,768]{1,0:T(8,128)(2,1)} %get-tuple-element.53, bf16[4096,2048]{1,0:T(8,128)(2,1)} %all-gather.2.cloned.1.call-done.cot_ref), kind=kOutput, calls=%fused_computation.136 | convolution fusion | flops 12884901888 | bytes 29360128 | tf_op jit(solution)/shard_map/dot_general | solution.py:76
  639.2 4.8 convolution_convert_fusion.1
  643.9 20.5 %fusion.9 = f32[4,2048,192]{1,2,0:T(8,128)} fusion(bf16[4096,4,192]{0,2,1:T(8,128)(2,1)} %bitcast.109, bf16[4096,2048]{1,0:T(8,128)(2,1)} %shard_map.266.normed_ref), kind=kOutput, calls=%fused_computation.16 | convolution fusion | flops 12884901888 | bytes 29360128 | tf_op jit(solution)/shard_map/td,tju->jdu/dot_general | solution.py:1203
  664.4 17.2 %fusion.12 = f32[4,2048,192]{1,2,0:T(8,128)} fusion(bf16[4096,4,192]{0,2,1:T(8,128)(2,1)} %bitcast.110, bf16[4096,2048]{1,0:T(8,128)(2,1)S(1)} %bitcast.102), kind=kOutput, calls=%fused_computation.17 | convolution fusion | flops 12884901888 | bytes 29360128 | tf_op jit(solution)/shard_map/td,tju->jdu/dot_general | solution.py:1203
  684.0 36.5 %shard_map.271 = bf16[4,272,2048]{2,1,0:T(8,128)(2,1)} custom-call(bf16[272,2048]{1,0:T(8,128)(2,1)} %pad_maximum_fusion.1.x_ref), custom_call_target="tpu_custom_call" | custom-call | tf_op jit(solution)/shard_map/pallas_call | solution.py:654
  722.6 5.6 fusion.5.part_ref
  728.3 90.5 %shard_map.272 = f32[256,1408]{1,0:T(8,128)S(1)} custom-call(bf16[2048,1408]{1,0:T(8,128)(2,1)} %fusion.5.part_ref), custom_call_target="tpu_custom_call" | custom-call | tf_op jit(solution)/shard_map/pallas_call | solution.py:743
  (165 shorter events, 57.9 us)
Async XLA Ops:
  7.2 6.6 copy-start
  7.2 301.8 %all-gather.2.cloned.1.call-start = ((), (), s32[]{:S(2)}) async-start(), calls=%async_computation.2 | async-start | bytes 17301504 | tf_op jit(solution)/shard_map/all_gather | solution.py:1138
  8.4 120.5 %copy-start.18 = (s32[1,512]{1,0:T(1,128)S(1)}, s32[1,512]{1,0:T(1,128)}, u32[]{:S(2)}) copy-start(s32[1,512]{1,0:T(1,128)} %param.30) | copy-start | bytes 6148
  127.4 554.2 %reduce-scatter.3.cloned.1.call-start = ((), (), s32[]{:S(2)}) async-start(), calls=%async_computation.3 | async-start | bytes 17301504 | tf_op jit(solution)/shard_map/reduce_scatter | solution.py:1198
  130.9 21.6 %copy-start.15 = (bf16[2048,1024]{1,0:T(8,128)(2,1)S(1)}, bf16[2048,1024]{1,0:T(8,128)(2,1)}, u32[]{:S(2)}) copy-start(bf16[2048,1024]{1,0:T(8,128)(2,1)} %get-tuple-element.43.out_w_ref) | copy-start | bytes 12582916
  152.5 4.7 copy-start.2
  187.5 108.6 %slice-start.8 = ((bf16[8,26624]{1,0:T(8,128)(2,1)}), bf16[8,8192]{1,0:T(8,128)(2,1)S(1)}, s32[]{:S(2)}) async-start(bf16[8,26624]{1,0:T(8,128)(2,1)} %copy-done.17), calls=%async_computation.13 | async-start | bytes 262144 | tf_op jit(solution)/shard_map/slice | solution.py:1142
  296.5 11.2 %copy-start.13 = (bf16[2048,32]{1,0:T(8,128)(2,1)}, bf16[2048,32]{1,0:T(8,128)(2,1)S(1)}, u32[]{:S(2)}) copy-start(bf16[2048,32]{1,0:T(8,128)(2,1)S(1)} %reshape.328) | copy-start | bytes 393220
  471.0 350.1 %reduce-scatter.5.cloned.1.call-start = ((), (), s32[]{:S(2)}) async-start(), calls=%async_computation.4 | async-start | bytes 5308416 | tf_op jit(solution)/shard_map/reduce_scatter | solution.py:1245
  514.4 39.6 %slice-start.6 = ((s8[5242880]{0:T(1024)(128)(4,1)}), s8[4194304]{0:T(1024)(128)(4,1)S(1)}, s32[]{:S(2)}) async-start(s8[5242880]{0:T(1024)(128)(4,1)} %bitcast.111), calls=%async_computation.11 | async-start | bytes 8388608
  518.7 35.4 %copy-start.9 = (bf16[1,512,2048]{2,1,0:T(8,128)(2,1)S(1)}, bf16[1,512,2048]{2,1,0:T(8,128)(2,1)}, u32[]{:S(2)}) copy-start(bf16[1,512,2048]{2,1,0:T(8,128)(2,1)} %param.16) | copy-start | bytes 6291460
  518.7 35.4 %slice-start.7 = ((s8[5242880]{0:T(1024)(128)(4,1)}), s8[1048576]{0:T(1024)(128)(4,1)S(1)}, s32[]{:S(2)}) async-start(s8[5242880]{0:T(1024)(128)(4,1)} %bitcast.111), calls=%async_computation.12 | async-start | bytes 2097152
  597.7 11.2 %copy-start.8 = (f32[128,2048]{1,0:T(8,128)S(1)}, f32[128,2048]{1,0:T(8,128)}, u32[]{:S(2)}) copy-start(f32[128,2048]{1,0:T(8,128)} %copy-done.6) | copy-start | bytes 3145732
  597.7 11.2 %copy-start.11 = (f32[128,2048]{1,0:T(8,128)S(1)}, f32[128,2048]{1,0:T(8,128)}, u32[]{:S(2)}) copy-start(f32[128,2048]{1,0:T(8,128)} %copy-done.10) | copy-start | bytes 3145732
  608.9 4.3 copy-start.16
  618.3 20.9 %copy-start.3 = (bf16[512,2048]{1,0:T(8,128)(2,1)S(1)}, bf16[512,2048]{1,0:T(8,128)(2,1)}, u32[]{:S(2)}) copy-start(bf16[512,2048]{1,0:T(8,128)(2,1)} %copy-done.2) | copy-start | bytes 6291460
  618.3 20.9 %copy-start.5 = (bf16[512,1280]{1,0:T(8,128)(2,1)S(1)}, bf16[512,1280]{1,0:T(8,128)(2,1)}, u32[]{:S(2)}) copy-start(bf16[512,1280]{1,0:T(8,128)(2,1)} %copy-done.4) | copy-start | bytes 3932164
  639.2 25.2 %slice-start = ((s8[16777216]{0:T(1024)(128)(4,1)}), s8[4194304]{0:T(1024)(128)(4,1)S(1)}, s32[]{:S(2)}) async-start(s8[16777216]{0:T(1024)(128)(4,1)} %bitcast.101), calls=%async_computation.5 | async-start | bytes 8388608
  643.9 20.5 %slice-start.1 = ((s8[16777216]{0:T(1024)(128)(4,1)}), s8[4194304]{0:T(1024)(128)(4,1)S(1)}, s32[]{:S(2)}) async-start(s8[16777216]{0:T(1024)(128)(4,1)} %bitcast.101), calls=%async_computation.6 | async-start | bytes 8388608
  643.9 20.5 %slice-start.2 = ((s8[16777216]{0:T(1024)(128)(4,1)}), s8[4194304]{0:T(1024)(128)(4,1)S(1)}, s32[]{:S(2)}) async-start(s8[16777216]{0:T(1024)(128)(4,1)} %bitcast.101), calls=%async_computation.7 | async-start | bytes 8388608
  643.9 20.5 %slice-start.3 = ((s8[16777216]{0:T(1024)(128)(4,1)}), s8[4194304]{0:T(1024)(128)(4,1)S(1)}, s32[]{:S(2)}) async-start(s8[16777216]{0:T(1024)(128)(4,1)} %bitcast.101), calls=%async_computation.8 | async-start | bytes 8388608
  722.3 96.5 %slice-start.4 = ((s8[4456448]{0:T(1024)(128)(4,1)}), s8[262144]{0:T(1024)(128)(4,1)S(1)}, s32[]{:S(2)}) async-start(s8[4456448]{0:T(1024)(128)(4,1)} %bitcast.103), calls=%async_computation.9 | async-start | bytes 524288
  722.6 96.2 %slice-start.5 = ((s8[4456448]{0:T(1024)(128)(4,1)}), s8[4194304]{0:T(1024)(128)(4,1)S(1)}, s32[]{:S(2)}) async-start(s8[4456448]{0:T(1024)(128)(4,1)} %bitcast.103), calls=%async_computation.10 | async-start | bytes 8388608
  821.1 6.9 copy-start.14
  (7 other events, 17.4 us)
Sparse Core Ops, SparseCore 0:
  127.5 157.2 all-gather.1
  471.1 209.6 reduce-scatter.2
  684.5 125.9 reduce-scatter.4

commit v3 on v2

--- a/solution.py
+++ b/solution.py
@@ -683,159 +683,157 @@
         scratch_shapes=[pltpu.VMEM((rows, width), part.dtype), pltpu.VMEM((2, rows, width), part.dtype), pltpu.VMEM((rows, width), part.dtype), D((3,)), D((3,))],
         compiler_params=pltpu.CompilerParams(collective_id=collective_id, has_side_effects=True, vmem_limit_bytes=24 << 20))(part)
 
-def groups_scatter_kernel(split, part_ref, out_ref, near_in, mine, line_in, tail_in, tail_mine, tail_line, load_sem, side_sem, line_send, line_recv, tail_load, tail_side, tail_send, tail_recv):
-    rows = out_ref.shape[0]; rest = rows - split
+
+def nt(a, b):
+    return lax.dot_general(a, b, (((1,), (1,)), ((), ())), preferred_element_type=jnp.float32)
+
+def nn(a, b):
+    return jnp.dot(a, b, preferred_element_type=jnp.float32)
+
+def nearest(z, index):
+    choice = [partner(z, n) for n in range(4)]
+    return jnp.where(index == 0, choice[0], jnp.where(index == 1, choice[1], jnp.where(index == 2, choice[2], choice[3])))
+
+def spot(zz, yy, xx): return (zz * 2 + yy) * 2 + xx
+
+def step_target(step):
     z, y, x, c = coords()
-    t = 2 * x + c
-    up, down, across = (z + 1, y, t), (z - 1, y, t), (z, 1 - y, t)
-    greet([(z < 3, up), (z > 0, down), (None, across)])
-    f32, dt = jnp.float32, part_ref.dtype
-    def rows_of(zz, yy, first, size): return part_ref.at[pl.ds(pl.multiple_of((zz * 2 + yy) * rows + first, 16), size)]
+    n = step % 4
+    return nearest(z, 3 - step // 4), jnp.where(n < 2, 1 - y, y), jnp.where(n % 2 == 0, 1 - x, x)
+
+def step_block(ref, step):
+    size = ref.shape[0] // 16
+    return ref.at[pl.ds(pl.multiple_of(spot(*step_target(step)) * size, size), size)]
+
+class Reduction:
+    def __init__(self, part, mine, core_in, first_in, second_in, line_in, core_sem, first_sem, second_sem, line_send, line_recv):
+        self.part, self.mine, self.core_in, self.first_in, self.second_in, self.line_in = part, mine, core_in, first_in, second_in, line_in
+        self.core_sem, self.first_sem, self.second_sem, self.line_send, self.line_recv = core_sem, first_sem, second_sem, line_send, line_recv
+        self.half = part.shape[2] // 2
+        z, y, x, c = self.at = coords()
+        self.up, self.down = (z + 1, y, 2 * x + c), (z - 1, y, 2 * x + c)
+        self.y_side, self.x_side, self.core_side = (z, 1 - y, 2 * x + c), (z, y, 2 * (1 - x) + c), (z, y, 2 * x + 1 - c)
+
+    @staticmethod
+    def scratch(rows, width, dtype):
+        V, D, half = pltpu.VMEM, pltpu.SemaphoreType.DMA, rows // 2
+        return [V((2, 2, rows, width), dtype), V((16, rows, width), dtype), V((16, rows, width), dtype), V((2, 8, half, width), dtype),
+            V((2, 4, half, width), dtype), V((2, 4, 2, half, width), dtype), D((2, 16)), D((2, 2, 8)), D((2, 2, 4)), D((4, 2)), D((2, 4, 2))]
+
+    def greet(self):
+        z = self.at[0]
+        greet([(z < 3, self.up), (z > 0, self.down), (None, self.y_side), (None, self.x_side), (None, self.core_side)])
+
+    @staticmethod
     def remote(src, dst, send, recv, device):
         return pltpu.make_async_remote_copy(src_ref=src, dst_ref=dst, send_sem=send, recv_sem=recv, device_id=device, device_id_type=MESH)
-    def over_y(zz): return remote(rows_of(zz, 1 - y, 0, split), near_in.at[zz], side_sem.at[0, zz], side_sem.at[1, zz], across)
-    def load(zz): return pltpu.make_async_copy(rows_of(zz, y, 0, split), mine.at[zz], load_sem.at[zz])
-    def load_tail(zz, yy): return pltpu.make_async_copy(rows_of(zz, yy, split, rest), tail_mine.at[zz, yy], tail_load.at[zz, yy])
-    def line(zz, way): return remote(mine.at[zz], line_in.at[way, zz], line_send.at[zz], line_recv.at[way, zz], up if way == 0 else down)
-    def line_tail(zz, yy, way): return remote(tail_mine.at[zz, yy], tail_line.at[way, zz, yy], tail_send.at[zz, yy], tail_recv.at[way, zz, yy], up if way == 0 else down)
-    final = remote(tail_mine.at[z, 1 - y], tail_in, tail_side.at[0], tail_side.at[1], across)
-    order = (3, 2, 1, 0)
-    for i in order:
-        zz = partner(z, i)
-        over_y(zz).start(); load(zz).start()
-        load_tail(zz, 0).start(); load_tail(zz, 1).start()
-    def along(zz, i, copy, add):
-        for way, from_side, toward in ((0, z > 0, zz > z), (1, z < 3, zz < z)):
-            @pl.when(from_side if i == 0 else from_side & toward)
-            def _(way=way):
-                copy(way).wait_recv()
-                add(way)
-        for way, toward in ((0, zz > z), (1, zz < z)):
-            if i > 0:
-                @pl.when(toward)
-                def _(way=way): copy(way).start()
-    for i in order:
-        zz = partner(z, i)
-        for n in range(2):
-            yy = (1 - y, y)[n]
-            load_tail(zz, yy).wait()
-            def add(way, yy=yy): tail_mine[zz, yy] = (tail_mine[zz, yy].astype(f32) + tail_line[way, zz, yy].astype(f32)).astype(dt)
-            along(zz, i, lambda way, yy=yy: line_tail(zz, yy, way), add)
-            if i == 0 and n == 0: final.start()
-        load(zz).wait(); over_y(zz).wait_recv()
-        mine[zz] = (mine[zz].astype(f32) + near_in[zz].astype(f32)).astype(dt)
-        def add(way): mine[zz] = (mine[zz].astype(f32) + line_in[way, zz].astype(f32)).astype(dt)
-        along(zz, i, lambda way: line(zz, way), add)
-    out_ref[pl.ds(0, split)] = mine[z].astype(f32)
-    final.wait_recv()
-    out_ref[pl.ds(split, rest)] = tail_mine[z, y].astype(f32) + tail_in[...].astype(f32)
-    final.wait_send()
-    for zz in range(4):
-        over_y(zz).wait_send()
-        @pl.when(zz != z)
-        def _(zz=zz):
-            line(zz, 0).wait_send()
-            for yy in range(2): line_tail(zz, yy, 0).wait_send()
-
-def scatter_groups(part, split, collective_id):
-    total, width = part.shape; rows = total // 8; rest = rows - split
-    dt = part.dtype; D = pltpu.SemaphoreType.DMA; V = pltpu.VMEM
-    return pl.pallas_call(functools.partial(groups_scatter_kernel, split), out_shape=jax.ShapeDtypeStruct((rows, width), jnp.float32),
-        in_specs=[pl.BlockSpec(memory_space=pl.ANY)], out_specs=pl.BlockSpec(memory_space=V),
-        scratch_shapes=[V((4, split, width), dt), V((4, split, width), dt), V((2, 4, split, width), dt), V((rest, width), dt), V((4, 2, rest, width), dt), V((2, 4, 2, rest, width), dt),
-            D((4,)), D((2, 4)), D((4,)), D((2, 4)), D((4, 2)), D((2,)), D((4, 2)), D((2, 4, 2))],
-        compiler_params=pltpu.CompilerParams(collective_id=collective_id, has_side_effects=True, vmem_limit_bytes=48 << 20))(part)
-
-
-def nt(a, b):
-    return lax.dot_general(a, b, (((1,), (1,)), ((), ())), preferred_element_type=jnp.float32)
-
-def nn(a, b):
-    return jnp.dot(a, b, preferred_element_type=jnp.float32)
-
-def expert_kernel(comm, normed_ref, cot_ref, code_ref, router_ref, expand_ref, place_ref, gate_ref, up_ref, down_ref,
-                  out_ref, hid_out, gate_out, up_out,
-                  normed_in, cot_in, code_in, units, part, mine, core_in, first_in, second_in, line_in,
-                  in_sem, units_sem, core_sem, first_sem, second_sem, line_send, line_recv):
-    rows = out_ref.shape[0]; half = rows // 2; width = normed_ref.shape[1]
-    wide = gate_ref.shape[1]
-    z, y, x, c = coords()
-    up, down = (z + 1, y, 2 * x + c), (z - 1, y, 2 * x + c)
-    y_side, x_side, core_side = (z, 1 - y, 2 * x + c), (z, y, 2 * (1 - x) + c), (z, y, 2 * x + 1 - c)
-    if comm:
-        greet([(z < 3, up), (z > 0, down), (None, y_side), (None, x_side), (None, core_side)])
-    f32, bf16 = jnp.float32, jnp.bfloat16
-    def nearest(index):
-        choice = [partner(z, n) for n in range(4)]
-        return jnp.where(index == 0, choice[0], jnp.where(index == 1, choice[1], jnp.where(index == 2, choice[2], choice[3])))
-    def spot(zz, yy, xx): return (zz * 2 + yy) * 2 + xx
-    def target(step):
-        n = step % 4
-        return nearest(3 - step // 4), jnp.where(n < 2, 1 - y, y), jnp.where(n % 2 == 0, 1 - x, x)
-    def remote(src, dst, send, recv, device):
-        return pltpu.make_async_remote_copy(src_ref=src, dst_ref=dst, send_sem=send, recv_sem=recv, device_id=device, device_id_type=MESH)
-    def block(ref, step):
-        return ref.at[pl.ds(pl.multiple_of(spot(*target(step)) * 2 * rows, 2 * rows), 2 * rows)]
-    stride = code_ref.shape[0] // 8
-    def loads(step):
-        slot = step % 2
-        zz, yy, xx = target(step)
-        codes = code_ref.at[pl.ds(pl.multiple_of((zz * 2 + yy) * stride, 16), rows)]
-        pairs = ((block(normed_ref, step), normed_in), (block(cot_ref, step), cot_in), (codes, code_in))
-        return [pltpu.make_async_copy(src, dst.at[slot], in_sem.at[n, slot]) for n, (src, dst) in enumerate(pairs)]
-    def stores(step):
-        slot = step % 2
-        return [pltpu.make_async_copy(units.at[slot, n], block(dst, step), units_sem.at[n, slot])
-                for n, dst in enumerate((hid_out, gate_out, up_out))]
-    def over_core(step):
-        s = spot(*target(step))
-        return remote(part.at[step % 2, 1 - c], core_in.at[s], core_sem.at[0, s], core_sem.at[1, s], core_side)
-    def piece(zz, yy, xx, h): return mine.at[spot(zz, yy, xx), pl.ds(h * half, half)]
-    def first(h, zz, other):
-        src = piece(zz, other, 1 - x, 0) if h == 0 else piece(zz, 1 - y, other, 1)
+
+    def over_core(self, step):
+        s = spot(*step_target(step))
+        return self.remote(self.part.at[step % 2, 1 - self.at[3]], self.core_in.at[s], self.core_sem.at[0, s], self.core_sem.at[1, s], self.core_side)
+
+    def piece(self, zz, yy, xx, h): return self.mine.at[spot(zz, yy, xx), pl.ds(h * self.half, self.half)]
+
+    def first(self, h, zz, other):
+        z, y, x, c = self.at
+        src = self.piece(zz, other, 1 - x, 0) if h == 0 else self.piece(zz, 1 - y, other, 1)
         s = zz * 2 + other
-        return remote(src, first_in.at[h, s], first_sem.at[0, h, s], first_sem.at[1, h, s], x_side if h == 0 else y_side)
-    def second(h, zz):
-        src = piece(zz, 1 - y, x, 0) if h == 0 else piece(zz, y, 1 - x, 1)
-        return remote(src, second_in.at[h, zz], second_sem.at[0, h, zz], second_sem.at[1, h, zz], y_side if h == 0 else x_side)
-    def line(h, zz, way):
-        return remote(piece(zz, y, x, h), line_in.at[way, zz, h], line_send.at[zz, h], line_recv.at[way, zz, h], up if way == 0 else down)
-    def add(s, h, arrived):
-        at = (s, pl.ds(h * half, half))
-        mine[at] = (mine[at].astype(f32) + arrived[...].astype(f32)).astype(bf16)
-    def stage_core(step):
-        zz, yy, xx = target(step)
+        return self.remote(src, self.first_in.at[h, s], self.first_sem.at[0, h, s], self.first_sem.at[1, h, s], self.x_side if h == 0 else self.y_side)
+
+    def second(self, h, zz):
+        z, y, x, c = self.at
+        src = self.piece(zz, 1 - y, x, 0) if h == 0 else self.piece(zz, y, 1 - x, 1)
+        return self.remote(src, self.second_in.at[h, zz], self.second_sem.at[0, h, zz], self.second_sem.at[1, h, zz], self.y_side if h == 0 else self.x_side)
+
+    def line(self, h, zz, way):
+        z, y, x, c = self.at
+        return self.remote(self.piece(zz, y, x, h), self.line_in.at[way, zz, h], self.line_send.at[zz, h], self.line_recv.at[way, zz, h], self.up if way == 0 else self.down)
+
+    def add(self, s, h, arrived):
+        at = (s, pl.ds(h * self.half, self.half))
+        self.mine[at] = (self.mine[at].astype(jnp.float32) + arrived[...].astype(jnp.float32)).astype(self.mine.dtype)
+
+    def stage_core(self, step):
+        zz, yy, xx = step_target(step)
         s = spot(zz, yy, xx)
-        over_core(step).wait_recv()
-        mine[s] = (part[step % 2, c].astype(f32) + core_in[s].astype(f32)).astype(bf16)
+        self.over_core(step).wait_recv()
+        self.mine[s] = (self.part[step % 2, self.at[3]].astype(jnp.float32) + self.core_in[s].astype(jnp.float32)).astype(self.mine.dtype)
         n = step % 4
         @pl.when(n % 2 == 0)
-        def _(): first(0, zz, yy).start()
+        def _(): self.first(0, zz, yy).start()
         @pl.when(n < 2)
-        def _(): first(1, zz, xx).start()
-    def stage_first(i):
-        zz = nearest(i)
+        def _(): self.first(1, zz, xx).start()
+
+    def stage_first(self, i):
+        z, y, x, c = self.at
+        zz = nearest(z, i)
         for n in range(2):
             for h, other in ((0, (1 - y, y)[n]), (1, (1 - x, x)[n])):
-                first(h, zz, other).wait_recv()
-                s = spot(zz, other, x) if h == 0 else spot(zz, y, other)
-                add(s, h, first_in.at[h, zz * 2 + other])
-                if n == 0: second(h, zz).start()
-    def stage_second(i):
-        zz = nearest(i)
+                self.first(h, zz, other).wait_recv()
+                self.add(spot(zz, other, x) if h == 0 else spot(zz, y, other), h, self.first_in.at[h, zz * 2 + other])
+                if n == 0: self.second(h, zz).start()
+
+    def stage_second(self, i):
+        z, y, x, c = self.at
+        zz = nearest(z, i)
         for h in range(2):
-            second(h, zz).wait_recv()
-            add(spot(zz, y, x), h, second_in.at[h, zz])
-    def stage_line(i):
-        zz = nearest(i); s = spot(zz, y, x)
+            self.second(h, zz).wait_recv()
+            self.add(spot(zz, y, x), h, self.second_in.at[h, zz])
+
+    def stage_line(self, i):
+        z, y, x, c = self.at
+        zz = nearest(z, i)
         for h in range(2):
             for way, from_side, toward in ((0, z > 0, zz > z), (1, z < 3, zz < z)):
                 @pl.when(from_side & (toward | (zz == z)))
                 def _(h=h, way=way):
-                    line(h, zz, way).wait_recv()
-                    add(s, h, line_in.at[way, zz, h])
+                    self.line(h, zz, way).wait_recv()
+                    self.add(spot(zz, y, x), h, self.line_in.at[way, zz, h])
                 @pl.when(toward)
-                def _(h=h, way=way): line(h, zz, way).start()
+                def _(h=h, way=way): self.line(h, zz, way).start()
+
+    def follow(self, step):
+        @pl.when(step >= 1)
+        def _(): self.stage_core(step - 1)
+        q = step // 4
+        @pl.when((step % 4 == 1) & (q >= 1))
+        def _(): self.stage_first(4 - q)
+        @pl.when((step % 4 == 3) & (q >= 1))
+        def _(): self.stage_second(4 - q)
+        @pl.when((step % 4 == 1) & (q >= 2))
+        def _(): self.stage_line(5 - q)
+
+    def finish(self, out_ref):
+        z, y, x, c = self.at
+        self.stage_core(15); self.stage_line(1); self.stage_first(0); self.stage_second(0); self.stage_line(0)
+        out_ref[...] = self.mine[spot(z, y, x)].astype(jnp.float32)
+        self.over_core(14).wait_send(); self.over_core(15).wait_send()
+        for zz in range(4):
+            for other in range(2):
+                for h in range(2): self.first(h, zz, other).wait_send()
+            for h in range(2): self.second(h, zz).wait_send()
+            @pl.when(zz != z)
+            def _(zz=zz):
+                for h in range(2): self.line(h, zz, 0).wait_send()
+
+def expert_kernel(normed_ref, cot_ref, code_ref, router_ref, expand_ref, place_ref, gate_ref, up_ref, down_ref,
+                  out_ref, hid_out, gate_out, up_out, normed_in, cot_in, code_in, units, in_sem, units_sem, *scratch):
+    reduction = Reduction(*scratch)
+    reduction.greet()
+    part = reduction.part
+    rows, width, wide = out_ref.shape[0], normed_ref.shape[1], gate_ref.shape[1]
+    f32, bf16 = jnp.float32, jnp.bfloat16
+    stride = code_ref.shape[0] // 8
+    def loads(step):
+        slot = step % 2
+        zz, yy, xx = step_target(step)
+        codes = code_ref.at[pl.ds(pl.multiple_of((zz * 2 + yy) * stride, 16), rows)]
+        pairs = ((step_block(normed_ref, step), normed_in), (step_block(cot_ref, step), cot_in), (codes, code_in))
+        return [pltpu.make_async_copy(src, dst.at[slot], in_sem.at[n, slot]) for n, (src, dst) in enumerate(pairs)]
+    def stores(step):
+        slot = step % 2
+        return [pltpu.make_async_copy(units.at[slot, n], step_block(dst, step), units_sem.at[n, slot])
+                for n, dst in enumerate((hid_out, gate_out, up_out))]
     for one in loads(0): one.start()
 
     def compute(step):
@@ -847,10 +845,10 @@
         @pl.when(step >= 2)
         def _():
             for one in stores(step - 2): one.wait()
-            if comm: over_core(step - 2).wait_send()
+            reduction.over_core(step - 2).wait_send()
         normed, cot = normed_in[slot], cot_in[slot]
         code = code_in[slot].astype(f32)
-        quarter = lax.broadcasted_iota(jnp.int32, code.shape, 1) // (128 // 4) - 2 * target(step)[2]
+        quarter = lax.broadcasted_iota(jnp.int32, code.shape, 1) // (128 // 4) - 2 * step_target(step)[2]
         code = jnp.concatenate([jnp.where(quarter == n, code, 0.0) for n in range(2)], axis=0)
         scores = jnp.where(code > 0.5, nn(normed, router_ref[...]), NEGATIVE)
         scores = jnp.where(code > 0.5, jnp.exp(scores - jnp.max(scores, axis=1, keepdims=True)), 0.0)
@@ -882,52 +880,90 @@
         grad_gates = grad_gates.astype(bf16)
         part[slot, 0, :, pl.ds(width, 128)] = grad_gates[:rows]
         part[slot, 1, :, pl.ds(width, 128)] = grad_gates[rows:]
-        if comm: over_core(step).start()
+        reduction.over_core(step).start()
 
     @pl.loop(0, 16)
     def _(step):
         compute(step)
-        if not comm: return
-        @pl.when(step >= 1)
-        def _(): stage_core(step - 1)
-        q = step // 4
-        @pl.when((step % 4 == 1) & (q >= 1))
-        def _(): stage_first(4 - q)
-        @pl.when((step % 4 == 3) & (q >= 1))
-        def _(): stage_second(4 - q)
-        @pl.when((step % 4 == 1) & (q >= 2))
-        def _(): stage_line(5 - q)
+        reduction.follow(step)
     for step in (14, 15):
         for one in stores(step): one.wait()
-    if not comm:
-        out_ref[...] = part[0, 0].astype(f32)
-        return
-    stage_core(15); stage_first(0); stage_second(0); stage_line(1); stage_line(0)
-    out_ref[...] = mine[spot(z, y, x)].astype(f32)
-    over_core(14).wait_send(); over_core(15).wait_send()
-    for zz in range(4):
-        for other in range(2):
-            for h in range(2): first(h, zz, other).wait_send()
-        for h in range(2): second(h, zz).wait_send()
-        @pl.when(zz != z)
-        def _(zz=zz):
-            for h in range(2): line(h, zz, 0).wait_send()
-
-def run_experts(normed_all, cot_all, code, router, expand, place, gate_flat, up_flat, down_flat, collective_id, comm=True):
-    total, width = normed_all.shape; rows = total // 32; half = rows // 2; wide = gate_flat.shape[1]
+    reduction.finish(out_ref)
+
+def run_experts(normed_all, cot_all, codes, router, expand, place, gate_flat, up_flat, down_flat, collective_id):
+    total, width = normed_all.shape; rows = total // 32; wide = gate_flat.shape[1]
     bf16 = jnp.bfloat16; D = pltpu.SemaphoreType.DMA; V = pltpu.VMEM; W = width + 128
-    anyspec, vspec = pl.BlockSpec(memory_space=pl.ANY), pl.BlockSpec(memory_space=pltpu.VMEM)
+    anyspec, vspec = pl.BlockSpec(memory_space=pl.ANY), pl.BlockSpec(memory_space=V)
     unit = jax.ShapeDtypeStruct((total, wide), bf16)
-    params = dict(collective_id=collective_id) if comm else {}
-    return pl.pallas_call(functools.partial(expert_kernel, comm),
+    return pl.pallas_call(expert_kernel,
         out_shape=[jax.ShapeDtypeStruct((rows, W), jnp.float32), unit, unit, unit],
         in_specs=[anyspec] * 3 + [vspec] * 6, out_specs=[vspec] + [anyspec] * 3,
         scratch_shapes=[V((2, 2 * rows, width), bf16), V((2, 2 * rows, width), bf16), V((2, rows, 128), bf16),
-            V((2, 3, 2 * rows, wide), bf16), V((2, 2, rows, W), bf16),
-            V((16, rows, W), bf16), V((16, rows, W), bf16), V((2, 8, half, W), bf16), V((2, 4, half, W), bf16), V((2, 4, 2, half, W), bf16),
-            D((3, 2)), D((3, 2)), D((2, 16)), D((2, 2, 8)), D((2, 2, 4)), D((4, 2)), D((2, 4, 2))],
-        compiler_params=pltpu.CompilerParams(has_side_effects=True, vmem_limit_bytes=60 << 20, **params))(
-            normed_all, cot_all, code, router, expand, place, gate_flat, up_flat, down_flat)
+            V((2, 3, 2 * rows, wide), bf16), D((3, 2)), D((3, 2)), *Reduction.scratch(rows, W, bf16)],
+        compiler_params=pltpu.CompilerParams(collective_id=collective_id, has_side_effects=True, vmem_limit_bytes=60 << 20))(
+            normed_all, cot_all, codes, router, expand, place, gate_flat, up_flat, down_flat)
+
+def output_kernel(normed_ref, cot_ref, hid_ref, gate_ref, up_ref, down_ref, out_ref, gate_out, up_out, down_out,
+                  wide_in, thin_in, in_sem, out_sem, *scratch):
+    reduction = Reduction(*scratch)
+    reduction.greet()
+    part = reduction.part
+    rows, width, units = out_ref.shape[0], normed_ref.shape[1], hid_ref.shape[1]
+    f32, bf16 = jnp.float32, jnp.bfloat16
+    def loads(step):
+        slot = step % 2
+        return ([pltpu.make_async_copy(step_block(src, step), wide_in.at[slot, n], in_sem.at[n, slot]) for n, src in enumerate((normed_ref, cot_ref))]
+            + [pltpu.make_async_copy(step_block(src, step), thin_in.at[slot, n], in_sem.at[2 + n, slot]) for n, src in enumerate((hid_ref, gate_ref, up_ref))])
+    for one in loads(0): one.start()
+
+    def inner(gate_sum, up_sum, down_sum):
+        gate_sum[...] = jnp.zeros_like(gate_sum)
+        up_sum[...] = jnp.zeros_like(up_sum)
+        down_sum[...] = jnp.zeros_like(down_sum)
+
+        @pl.loop(0, 16)
+        def _(step):
+            slot = step % 2
+            for one in loads(step): one.wait()
+            @pl.when(step < 15)
+            def _():
+                for one in loads(step + 1): one.start()
+            @pl.when(step >= 2)
+            def _(): reduction.over_core(step - 2).wait_send()
+            hid = thin_in[slot, 0]
+            for n in range(width // 512):
+                at = pl.ds(n * 512, 512)
+                value = nn(hid, down_ref[:, at]).astype(bf16)
+                part[slot, 0, :, at] = value[:rows]
+                part[slot, 1, :, at] = value[rows:]
+            reduction.over_core(step).start()
+            for n in range(units // 256):
+                at = pl.ds(n * 256, 256)
+                down_sum[at, :] += nn(thin_in[slot, 0, :, at].T, wide_in[slot, 1])
+            for n in range(width // 256):
+                at = pl.ds(n * 256, 256)
+                turned = wide_in[slot, 0, :, at].T
+                gate_sum[at, :] += nn(turned, thin_in[slot, 1])
+                up_sum[at, :] += nn(turned, thin_in[slot, 2])
+            reduction.follow(step)
+        kept = [pltpu.make_async_copy(src, dst, out_sem.at[n])
+                for n, (src, dst) in enumerate(((gate_sum, gate_out), (up_sum, up_out), (down_sum, down_out)))]
+        for one in kept: one.start()
+        reduction.finish(out_ref)
+        for one in kept: one.wait()
+    pl.run_scoped(inner, pltpu.VMEM((width, units), f32), pltpu.VMEM((width, units), f32), pltpu.VMEM((units, width), f32))
+
+def run_outputs(normed_all, cot_all, hidden_gated, gate_grad, up_grad, down_flat, collective_id):
+    total, width = normed_all.shape; rows = total // 32; units = hidden_gated.shape[1]
+    f32, bf16 = jnp.float32, jnp.bfloat16; D = pltpu.SemaphoreType.DMA; V = pltpu.VMEM; S = jax.ShapeDtypeStruct
+    anyspec, vspec = pl.BlockSpec(memory_space=pl.ANY), pl.BlockSpec(memory_space=V)
+    return pl.pallas_call(output_kernel,
+        out_shape=[S((rows, width), f32), S((width, units), f32), S((width, units), f32), S((units, width), f32)],
+        in_specs=[anyspec] * 5 + [vspec], out_specs=[vspec] + [anyspec] * 3,
+        scratch_shapes=[V((2, 2, 2 * rows, width), bf16), V((2, 3, 2 * rows, units), bf16), D((5, 2)), D((3,)),
+            *Reduction.scratch(rows, width, bf16)],
+        compiler_params=pltpu.CompilerParams(collective_id=collective_id, has_side_effects=True, vmem_limit_bytes=62 << 20))(
+            normed_all, cot_all, hidden_gated, gate_grad, up_grad, down_flat)
 
 
 def inverse_rms(values):
@@ -1194,16 +1230,6 @@
     scattered, hidden_gated, gate_grad, up_grad = run_experts(
         normed_all, grad_out_all, codes, router_lanes, expand, place, gate_flat, up_flat, down_flat, 4
     )
-    moe_part = matmul(hidden_gated, down_flat).astype(bf16)
-    moe_own = lax.psum_scatter(moe_part, EVERYONE, scatter_dimension=0, tiled=True).astype(f32)
-    grad_w_down = matmul_tn(hidden_gated, grad_out_all).reshape(down_weight.shape)
-
-    def by_expert(unit_grad):
-        unit_grad = unit_grad.reshape(-1, local_experts, hidden_width)
-        return jnp.einsum("td,tju->jdu", normed_all, unit_grad, preferred_element_type=f32)
-
-    grad_w_gate, grad_w_up = by_expert(gate_grad), by_expert(up_grad)
-
     scores = jnp.where(chosen_own, matmul(normed_own, full_router), NEGATIVE)
     gates_own = jnp.where(chosen_own, jax.nn.softmax(scores, axis=-1), 0.0)
     gates_grad_own = jnp.sum(
@@ -1259,13 +1285,8 @@
     ignored, first_pull = jax.vjp(rms_scale, input_own, gain_attn)
     grad_inputs_norm, ignored = first_pull(message[:own_count])
     message = jnp.concatenate([grad_resid_own + grad_inputs_norm, message[own_count:]], axis=0)
-    message, moe_own, grad_w_down, grad_w_gate, grad_w_up = lax.optimization_barrier(
-        (message.astype(bf16), moe_own, grad_w_down, grad_w_gate, grad_w_up)
-    )
-    message = jnp.concatenate([message, (residual_own + moe_own).astype(bf16)], axis=0)
-    message = gather_tensor(message, 7)
+    message = gather_tensor(message.astype(bf16), 7)
     input_grad = message[:, :own_count].reshape(row_count, width).astype(f32)
-    output = message[:, own_count + 16 :].reshape(row_count, width)
     gain_rows = message[0, own_count : own_count + 2].astype(f32)
     head_gains_grad = jnp.pad(
         gain_rows[1, : 2 * HEAD_SIZE].reshape(2, group_count, -1),
@@ -1276,8 +1297,19 @@
         ((0, 0), (0, 125)),
     )
     grad_qkv = jnp.concatenate([matmul_tn(normed_one, grad_raw), extra], axis=1)
-    grad_qkv = scatter_groups(grad_qkv.astype(bf16), 208, 10)
-    grad_qkv, grad_w_output = lax.optimization_barrier((grad_qkv, grad_w_output))
+    grad_qkv, hidden_gated = lax.optimization_barrier((grad_qkv.astype(bf16), hidden_gated))
+    grad_qkv = lax.psum_scatter(grad_qkv, GROUPS, scatter_dimension=0, tiled=True)
+    moe_own, grad_w_gate, grad_w_up, grad_w_down = run_outputs(
+        normed_all, grad_out_all, hidden_gated, gate_grad, up_grad, down_flat, 10
+    )
+
+    def by_expert(grad):
+        return grad.reshape(width, local_experts, hidden_width).transpose(1, 0, 2)
+
+    grad_w_gate, grad_w_up = by_expert(grad_w_gate), by_expert(grad_w_up)
+    output = gather_tensor((residual_own + moe_own).astype(bf16), 11).reshape(row_count, width)
+    output, grad_qkv, grad_w_output = lax.optimization_barrier((output, grad_qkv, grad_w_output))
+    grad_qkv, grad_w_output = grad_qkv.astype(f32), grad_w_output.astype(f32)
     value_at, extra_at = query_width + HEAD_SIZE, query_width + 2 * HEAD_SIZE
     return (
         output[None],
@@ -1286,14 +1318,14 @@
         grad_qkv[:, :query_width],
         grad_qkv[:, query_width:value_at],
         grad_qkv[:, value_at:extra_at],
-        grad_w_output[:, :query_width].astype(f32),
+        grad_w_output[:, :query_width],
         grad_qkv[: query_gain.shape[0], extra_at + 1],
         grad_qkv[: key_gain.shape[0], extra_at + 2],
-        grad_w_output[:, query_width + experts_total].astype(f32),
-        grad_w_output[:, query_width : query_width + experts_total].astype(f32),
+        grad_w_output[:, query_width + experts_total],
+        grad_w_output[:, query_width : query_width + experts_total],
         grad_w_gate,
         grad_w_up,
-        grad_w_down,
+        grad_w_down.reshape(down_weight.shape),
     )
 
 

time: 854 us -> 776 us (0.909)
  matrix products: 99.8 us -> 19.4 us
  local copies, waits for them, and re-layouts: 50.3 us -> 62.1 us
    dot_general x2 -> x0, matrix products: 37.7 us -> none  [by_expert(): jnp.einsum('td,tju->jdu', normed_all, unit_grad, preferred_element_type=f32)]
    pallas_call x2, Pallas kernels: 233 us -> 260 us  [the longest x1 133 us: run_experts(): pl.pallas_call(expert_kernel, out_shape=[jax.ShapeDtypeStruct((rows, W),...]
    pallas_call x2, Pallas kernels: 58.3 us -> 34.1 us  [scatter_tensor(): pl.pallas_call(tensor_scatter_kernel, out_shape=jax.ShapeDtypeStruct((row...]
    dot_general x4 -> x3, matrix products: 30.3 us -> 7.74 us  [matmul_tn(): lax.dot_general(left_side, right_side, (((0,), (0,)), ((), ())), preferre...]
    dot_general x3 -> x2, matrix products: 21.3 us -> 1.83 us  [matmul(): return jnp.dot(left_side, right_side, preferred_element_type=jnp.float32)]
    unnamed x63 -> x72, local copies, waits for them, and re-layouts: 3.39 us -> 14.7 us
    pallas_call x1, Pallas kernels: 109 us -> 118 us  [gather_everyone(): pl.pallas_call(gather_kernel, out_shape=jax.ShapeDtypeStruct((32 * rows,...]
    pallas_call x1, Pallas kernels: 35.3 us -> 26.4 us  [attend_back(): pl.pallas_call(attend_back_kernel, out_shape=[S((rows, q_width + 2 * HEAD...]
  transfers between devices with their start and end apart: 3 -> 3, of which waited for: 0 -> 0; matrix products, arithmetic and copies ran while one was open for 17% -> 8% of each run, Pallas kernels for 46% -> 48%
where the time goes in v3:
time: 776 us; the launch traced here: 767 us
  Pallas kernels  635 us (82%)
  local copies, waits for them, and re-layouts  62.1 us (8%)
  other arithmetic  36.3 us (5%)
  matrix products  19.4 us (2%)
  between operations  14.8 us (2%)
    pallas_call x1, Pallas kernels, run_experts(): pl.pallas_call(expert_kernel, out_shape=[jax.ShapeDtypeStruct((rows, W),...  133 us
    pallas_call x1, Pallas kernels, run_outputs(): pl.pallas_call(output_kernel, out_shape=[S((rows, width), f32), S((width,...  126 us
    pallas_call x1, Pallas kernels, gather_everyone(): pl.pallas_call(gather_kernel, out_shape=jax.ShapeDtypeStruct((32 * rows,...  118 us
    pallas_call x1, Pallas kernels, gather_groups(): pl.pallas_call(functools.partial(groups_kernel, splits), out_shape=[jax.S...  111 us
    pallas_call x3, Pallas kernels, gather_tensor(): pl.pallas_call(tensor_gather_kernel, out_shape=jax.ShapeDtypeStruct((4, *...  63.5 us
    pallas_call x2, Pallas kernels, scatter_tensor(): pl.pallas_call(tensor_scatter_kernel, out_shape=jax.ShapeDtypeStruct((row...  34.1 us
    pallas_call x1, Pallas kernels, attend_back(): pl.pallas_call(attend_back_kernel, out_shape=[S((rows, q_width + 2 * HEAD...  26.4 us
    pallas_call x1, Pallas kernels, attend(): pl.pallas_call(attend_kernel, out_shape=[S((rows, width), bf16), S((rows,...  22 us
  transfers between devices with their start and end apart: 3, of which 0 were waited for; matrix products, arithmetic and copies ran while one was open for 8% of the time, Pallas kernels for 48%

profile of v3, /device:TPU:0, one launch (start us, length us, event | category | flops | bytes accessed | tf_op | source)
XLA Modules:
  0.0 767.4 jit_solution(15115694091087332439)
XLA Ops:
  10.3 2.8 concatenate.41
  17.4 110.7 %shard_map.263 = (bf16[1664,128]{1,0:T(8,128)(2,1)}, bf16[2048,1280]{1,0:T(8,128)(2,1)}, bf16[2048,1024]{1,0:T(8,128)(2,1)}) custom-call(bf16[208,128]{1,0:T(8,128)(2,1)} %pad_bitcast_fusion.refs_0_, bf16[256,1280]{1,0:T(8,128)(2,1)} %pad_maximum_fusion.2.refs_1_, bf16[256,1024]{1,0:T(8,128)(2,1)} %refs_2_.1), custom_call_target="tpu_custom_call" | custom-call | tf_op jit(solution)/shard_map/pallas_call | solution.py:631
  129.7 4.6 copy.79.gate_ref
  134.3 4.7 copy.80.up_ref
  143.4 22.0 %shard_map.264 = (bf16[512,2048]{1,0:T(8,128)(2,1)S(1)}, f32[512,1152]{1,0:T(8,128)}, bf16[512,1024]{1,0:T(8,128)(2,1)S(1)}, bf16[512,256]{1,0:T(8,128)(2,1)S(1)...) custom-call(bf16[512,2048]{1,0:T(8,128)(2,1)} %bitcast.92, f32[1,2048]{1,0:T(1,128)S(1)} %bitcast.91, ...), custom_call_target="tpu_custom_call" | custom-call | tf_op jit(solution)/shard_map/pallas_call | solution.py:1035
  165.4 4.7 convolution_convert_fusion.2.part_ref
  170.2 16.3 %shard_map.265 = f32[128,2048]{1,0:T(8,128)S(1)} custom-call(bf16[512,2048]{1,0:T(8,128)(2,1)S(1)} %convolution_convert_fusion.2.part_ref), custom_call_target="tpu_custom_call" | custom-call | tf_op jit(solution)/shard_map/pallas_call | solution.py:681
  188.9 118.2 %shard_map.266.normed_ref = bf16[4096,2048]{1,0:T(8,128)(2,1)} custom-call(bf16[128,2048]{1,0:T(8,128)(2,1)} %multiply_convert_fusion.x_ref), custom_call_target="tpu_custom_call" | custom-call | tf_op jit(solution)/shard_map/pallas_call | solution.py:574
  311.7 3.2 pad_maximum_fusion.4.router_ref
  314.8 133.2 %shard_map.267 = (f32[128,2176]{1,0:T(8,128)}, bf16[4096,768]{1,0:T(8,128)(2,1)}, bf16[4096,768]{1,0:T(8,128)(2,1)}, bf16[4096,768]{1,0:T(8,128)(2,1)}) custom-call(bf16[4096,2048]{1,0:T(8,128)(2,1)} %shard_map.266.normed_ref, bf16[4096,2048]{1,0:T(8,128)(2,1)} %all-gather.2.cloned.1.call-done.cot_ref, bf16[1664,128]{1,0:T(8,128)(2,1)} %get-tuple-element.47.code_ref, ...), custom_call_target="tpu_custom_call" | custom-call | tf_op jit(solution)/shard_map/pallas_call | solution.py:898
  458.4 21.7 %shard_map.268 = bf16[4,144,2176]{2,1,0:T(8,128)(2,1)} custom-call(bf16[144,2176]{1,0:T(8,128)(2,1)} %fusion.20.x_ref), custom_call_target="tpu_custom_call" | custom-call | tf_op jit(solution)/shard_map/pallas_call | solution.py:654
  494.3 26.4 %shard_map.269 = (bf16[512,1280]{1,0:T(8,128)(2,1)S(1)}, f32[8,128]{1,0:T(8,128)S(1)}) custom-call(bf16[512,2048]{1,0:T(8,128)(2,1)} %bitcast.97, bf16[2048,1024]{1,0:T(8,128)(2,1)} %get-tuple-element.44.out_w_ref, bf16[512,1024]{1,0:T(8,128)(2,1)S(1)} %get-tuple-element.49.q_ref, bf16[512,256]{1,0:T(8,128)(2,1)S(1)} %get-tuple-element.50.kv_ref, ...), custom_call_target="tpu_custom_call" | custom-call | tf_op jit(solution)/shard_map/pallas_call | solution.py:1114
  520.7 3.2 fusion.2
  524.3 17.8 %shard_map.270 = f32[144,2048]{1,0:T(8,128)S(1)} custom-call(bf16[576,2048]{1,0:T(8,128)(2,1)S(1)} %bitcast.90), custom_call_target="tpu_custom_call" | custom-call | tf_op jit(solution)/shard_map/pallas_call | solution.py:681
  544.0 19.1 %shard_map.271 = bf16[4,144,2048]{2,1,0:T(8,128)(2,1)} custom-call(bf16[144,2048]{1,0:T(8,128)(2,1)} %pad_maximum_fusion.3.x_ref), custom_call_target="tpu_custom_call" | custom-call | tf_op jit(solution)/shard_map/pallas_call | solution.py:654
  564.9 3.2 convolution_convert_fusion
  568.1 3.0 pad_maximum_fusion
  571.1 126.4 %shard_map.272 = (f32[128,2048]{1,0:T(8,128)}, f32[2048,768]{1,0:T(8,128)}, f32[2048,768]{1,0:T(8,128)}, f32[768,2048]{1,0:T(8,128)}) custom-call(bf16[4096,2048]{1,0:T(8,128)(2,1)} %shard_map.266.normed_ref, bf16[4096,2048]{1,0:T(8,128)(2,1)} %all-gather.2.cloned.1.call-done.cot_ref, bf16[4096,768]{1,0:T(8,128)(2,1)} %get-tuple-element.57.hid_ref, ...), custom_call_target="tpu_custom_call" | custom-call | tf_op jit(solution)/shard_map/pallas_call | solution.py:960
  699.7 22.7 %shard_map.273 = bf16[4,128,2048]{2,1,0:T(8,128)(2,1)} custom-call(bf16[128,2048]{1,0:T(8,128)(2,1)} %add_convert_fusion.x_ref), custom_call_target="tpu_custom_call" | custom-call | tf_op jit(solution)/shard_map/pallas_call | solution.py:654
  722.4 6.6 copy.87
  729.0 6.7 copy.88
  735.7 2.5 bitcast_convert_fusion
  749.3 2.5 copy.89
  754.4 6.3 copy.108
  (167 shorter events, 63.9 us)
Async XLA Ops:
  7.2 8.4 %copy-start.17 = (bf16[256,1024]{1,0:T(8,128)(2,1)S(1)}, bf16[256,1024]{1,0:T(8,128)(2,1)}, u32[]{:S(2)}) copy-start(bf16[256,1024]{1,0:T(8,128)(2,1)} %param.18) | copy-start | bytes 1572868
  7.2 307.6 %all-gather.2.cloned.1.call-start = ((), (), s32[]{:S(2)}) async-start(), calls=%async_computation.2 | async-start | bytes 17301504 | tf_op jit(solution)/shard_map/all_gather | solution.py:1174
  13.7 115.8 %copy-start.19 = (s32[1,512]{1,0:T(1,128)S(1)}, s32[1,512]{1,0:T(1,128)}, u32[]{:S(2)}) copy-start(s32[1,512]{1,0:T(1,128)} %param.30) | copy-start | bytes 6148
  128.1 610.2 %reduce-scatter.5.cloned.1.call-start = ((), (), s32[]{:S(2)}) async-start(), calls=%async_computation.4 | async-start | bytes 5308416 | tf_op jit(solution)/shard_map/reduce_scatter | solution.py:1271
  129.5 178.2 %copy-start.18 = (pred[128,32]{1,0:T(32,128)(4,1)}, pred[128,32]{1,0:T(32,128)(4,1)S(1)}, u32[]{:S(2)}) copy-start(pred[128,32]{1,0:T(32,128)(4,1)S(1)} %copy.94) | copy-start | bytes 12292
  143.3 22.1 %copy-start.15 = (bf16[2048,1024]{1,0:T(8,128)(2,1)S(1)}, bf16[2048,1024]{1,0:T(8,128)(2,1)}, u32[]{:S(2)}) copy-start(bf16[2048,1024]{1,0:T(8,128)(2,1)} %get-tuple-element.44.out_w_ref) | copy-start | bytes 12582916
  187.7 119.4 %copy-start.25 = (f32[128]{0:T(128)}, f32[128]{0:T(128)S(1)}, u32[]{:S(2)}) copy-start(f32[128]{0:T(128)S(1)} %get-tuple-element.130) | copy-start | bytes 1540
  187.8 268.7 %copy-start.4 = (f32[128,2048]{1,0:T(8,128)}, f32[128,2048]{1,0:T(8,128)S(1)}, u32[]{:S(2)}) copy-start(f32[128,2048]{1,0:T(8,128)S(1)} %get-tuple-element.131) | copy-start | bytes 3145732
  187.8 119.4 %copy-start.22 = (f32[128]{0:T(128)}, f32[128]{0:T(128)S(1)}, u32[]{:S(2)}) copy-start(f32[128]{0:T(128)S(1)} %fusion.36) | copy-start | bytes 1540
  309.3 138.7 %copy-start.24 = (f32[128]{0:T(128)}, f32[128]{0:T(128)S(1)}, u32[]{:S(2)}) copy-start(f32[128]{0:T(128)S(1)} %get-tuple-element.153) | copy-start | bytes 1540
  491.1 247.2 %reduce-scatter.3.cloned.1.call-start = ((), (), s32[]{:S(2)}) async-start(), calls=%async_computation.3 | async-start | bytes 6488064 | tf_op jit(solution)/shard_map/reduce_scatter | solution.py:1301
  492.0 28.7 %slice-start.1 = ((s8[5242880]{0:T(1024)(128)(4,1)}), s8[4194304]{0:T(1024)(128)(4,1)S(1)}, s32[]{:S(2)}) async-start(s8[5242880]{0:T(1024)(128)(4,1)} %bitcast.102), calls=%async_computation.6 | async-start | bytes 8388608
  494.2 26.5 %copy-start.7 = (bf16[1,512,2048]{2,1,0:T(8,128)(2,1)S(1)}, bf16[1,512,2048]{2,1,0:T(8,128)(2,1)}, u32[]{:S(2)}) copy-start(bf16[1,512,2048]{2,1,0:T(8,128)(2,1)} %param.16) | copy-start | bytes 6291460
  494.2 26.5 %slice-start.2 = ((s8[5242880]{0:T(1024)(128)(4,1)}), s8[1048576]{0:T(1024)(128)(4,1)S(1)}, s32[]{:S(2)}) async-start(s8[5242880]{0:T(1024)(128)(4,1)} %bitcast.102), calls=%async_computation.7 | async-start | bytes 2097152
  524.3 18.2 %copy-start.5 = (f32[128,2048]{1,0:T(8,128)S(1)}, f32[128,2048]{1,0:T(8,128)}, u32[]{:S(2)}) copy-start(f32[128,2048]{1,0:T(8,128)} %copy-done.4) | copy-start | bytes 3145732
  524.3 18.2 %copy-start.9 = (f32[128,2048]{1,0:T(8,128)S(1)}, f32[128,2048]{1,0:T(8,128)}, u32[]{:S(2)}) copy-start(f32[128,2048]{1,0:T(8,128)} %copy-done.8) | copy-start | bytes 3145732
  524.3 18.2 %copy-start.13 = (bf16[128,2048]{1,0:T(8,128)(2,1)S(1)}, bf16[128,2048]{1,0:T(8,128)(2,1)}, u32[]{:S(2)}) copy-start(bf16[128,2048]{1,0:T(8,128)(2,1)} %dynamic-slice_bitcast_fusion) | copy-start | bytes 1572868
  524.3 18.2 %copy-start.23 = (f32[128]{0:T(128)S(1)}, f32[128]{0:T(128)}, u32[]{:S(2)}) copy-start(f32[128]{0:T(128)} %copy-done.22) | copy-start | bytes 1540
  543.1 21.7 %copy-start.1 = (bf16[512,2048]{1,0:T(8,128)(2,1)S(1)}, bf16[512,2048]{1,0:T(8,128)(2,1)}, u32[]{:S(2)}) copy-start(bf16[512,2048]{1,0:T(8,128)(2,1)} %copy-done) | copy-start | bytes 6291460
  543.1 21.7 %copy-start.3 = (bf16[512,1280]{1,0:T(8,128)(2,1)S(1)}, bf16[512,1280]{1,0:T(8,128)(2,1)}, u32[]{:S(2)}) copy-start(bf16[512,1280]{1,0:T(8,128)(2,1)} %copy-done.2) | copy-start | bytes 3932164
  571.1 126.4 %copy-start.6 = (f32[128,2048]{1,0:T(8,128)S(1)}, f32[128,2048]{1,0:T(8,128)}, u32[]{:S(2)}) copy-start(f32[128,2048]{1,0:T(8,128)} %copy-done.4) | copy-start | bytes 3145732
  729.0 6.7 slice-start
  738.3 5.9 copy-start.14
  746.4 6.6 copy-start.11
  (9 other events, 24.6 us)
Sparse Core Ops, SparseCore 0:
  128.2 145.9 all-gather.1
  491.2 95.4 reduce-scatter.4
  591.0 137.0 reduce-scatter.2
